TPU v7x, 32 devices: a whole 2x2x4 slice. The times are simulated.
32 devices in a mesh: grp: 4 (over x, core), slab: 8 (over z, y).
Axes of the slice: x: 2, y: 2, z: 4, core: 2. Of those that a mesh axis runs over, the one named last changes fastest.
Arguments:
- fine_noise: float32 [8, 4, 4, 256, 512], P('slab', 'grp'), may hold values from -6 to 6
- fine_kappa: float32 [8, 4, 4, 256, 512], P('slab', 'grp'), may hold values from 0.05 to 4
- coarse_kappa: float32 [64, 128, 256], P('slab', 'grp'), may hold values from 0.05 to 4
Outputs:
- fine_stiffness: float32 [8, 4, 4, 256, 512], P('slab', 'grp')
- coarse_stiffness: float32 [64, 128, 256], P('slab', 'grp')
All inputs are finite; a program needn't handle non-finite values.
Results may differ from a plain program's by a relative error of at most 0.00002.
Values sent between devices are 32-bit elements; how exact they have to be, the bound alone decides.
No kernel may reach another device: no remote copies, remote signals or barrier semaphores. Data moves between devices by JAX's collectives and lax.ppermute only.
A program may use at most 320 MiB of HBM per device.

v0:
```python
import jax
import jax.numpy as jnp
from jax import lax
from jax.sharding import PartitionSpec as P

SWEEPS = 4


def extended(block, sides, width, periodic):
    for axis, dim in sides:
        count = lax.axis_size(axis)
        forward = [(i, i + 1) for i in range(count - 1)]
        if periodic:
            forward.append((count - 1, 0))
        backward = [(target, source) for source, target in forward]
        low = lax.ppermute(
            lax.slice_in_dim(block, block.shape[dim] - width, None, axis=dim), axis, forward
        )
        high = lax.ppermute(lax.slice_in_dim(block, 0, width, axis=dim), axis, backward)
        block = jnp.concatenate([low, block, high], axis=dim)
    return block


def side_sum(padded):
    total = padded[2:, 1:-1, 1:-1] + padded[:-2, 1:-1, 1:-1]
    total = total + padded[1:-1, 2:, 1:-1] + padded[1:-1, :-2, 1:-1]
    total = total + padded[1:-1, 1:-1, 2:] + padded[1:-1, 1:-1, :-2]
    return total


def fine_sweep(field, noise, fine_diag):
    rims = jnp.stack([field[0], field[-1]])[None, None]
    group_pos = lax.axis_index("grp")
    last_pos = lax.axis_size("grp") - 1
    beside = extended(rims, (("grp", 1),), 1, True)
    wrap_low = beside[0, 0, 1]
    wrap_high = beside[0, 2, 0]
    carried = jnp.stack([wrap_low, wrap_high])[None, None]
    across = extended(carried, (("slab", 0),), 1, False)
    cross_low = across[0, 0, 0]
    cross_high = across[2, 0, 1]
    lower = jnp.where(group_pos == 0, cross_low, wrap_low)
    upper = jnp.where(group_pos == last_pos, cross_high, wrap_high)
    stacked = jnp.concatenate([lower[None], field, upper[None]], axis=0)
    padded = jnp.pad(stacked, ((0, 0), (1, 1), (1, 1)))
    return (noise + side_sum(padded)) / fine_diag


def coarse_sweep(field, coarse_noise, coarse_diag):
    framed = extended(field, (("grp", 1), ("slab", 0)), 1, False)
    padded = jnp.pad(framed, ((0, 0), (0, 0), (1, 1)))
    return (coarse_noise + 0.25 * side_sum(padded)) / coarse_diag


def block_sum(values):
    depth, rows, cols = values.shape
    return 0.125 * values.reshape(depth // 2, 2, rows // 2, 2, cols // 2, 2).sum(axis=(1, 3, 5))


def body(fine_noise, fine_kappa, coarse_kappa):
    noise = fine_noise[0, 0]
    fine_diag = 6.0 + fine_kappa[0, 0]
    moved = lax.all_to_all(noise, "grp", split_axis=1, concat_axis=0, tiled=True)
    coarse_noise = block_sum(moved)
    coarse_diag = 1.5 + coarse_kappa
    fine_field = jnp.zeros_like(noise)
    for step in range(SWEEPS):
        fine_field = fine_sweep(fine_field, noise, fine_diag)
    coarse_field = jnp.zeros_like(coarse_noise)
    for step in range(SWEEPS):
        coarse_field = coarse_sweep(coarse_field, coarse_noise, coarse_diag)
    fine_stiffness = jnp.exp(fine_field)[None, None]
    return (fine_stiffness, jnp.exp(coarse_field))


def solution(mesh):
    return jax.shard_map(
        body,
        mesh=mesh,
        in_specs=(
            P("slab", "grp", None, None, None),
            P("slab", "grp", None, None, None),
            P("slab", "grp", None),
        ),
        out_specs=(P("slab", "grp", None, None, None), P("slab", "grp", None)),
        check_vma=False,
    )
```

profile of v0, /device:TPU:13, one launch (start us, length us, event | category | flops | bytes accessed | tf_op | source)
XLA Modules:
  0.0 562.6 jit_solution(85088433432196026)
XLA Ops:
  2.6 23.1 %collective-permute-done.1 = f32[1,1,2,256,512]{4,3,2,1,0:T(8,128)S(1)} collective-permute-done((f32[1,1,2,256,512]{4,3,2,1,0:T(8,128)S(1)}, f32[1,1,2,256,512]{4,3,2,1,0:T(8,128)S(1)}, u32[]{:S(2)}, u32[]{:S(2)}) %collective-permute-start.1) | collective-permute-done | bytes 1048608 | tf_op jit(solution)/shard_map/ppermute | solution.py:19
  34.6 4.0 copy_bitcast_fusion
  38.7 36.5 %collective-permute-done.3 = f32[1,1,2,256,512]{4,3,2,1,0:T(8,128)} collective-permute-done((f32[1,1,2,256,512]{4,3,2,1,0:T(8,128)}, f32[1,1,2,256,512]{4,3,2,1,0:T(8,128)}, u32[]{:S(2)}, u32[]{:S(2)}) %collective-permute-start.3) | collective-permute-done | bytes 1048608 | tf_op jit(solution)/shard_map/ppermute | solution.py:16
  77.9 3.8 fusion.12
  86.0 23.7 %collective-permute-done.5 = f32[1,1,2,256,512]{4,3,2,1,0:T(8,128)S(1)} collective-permute-done((f32[1,1,2,256,512]{4,3,2,1,0:T(8,128)S(1)}, f32[1,1,2,256,512]{4,3,2,1,0:T(8,128)S(1)}, u32[]{:S(2)}, u32[]{:S(2)}) %collective-permute-start.5) | collective-permute-done | bytes 1048608 | tf_op jit(solution)/shard_map/ppermute | solution.py:19
  115.1 43.2 %collective-permute-done.7 = f32[1,1,2,256,512]{4,3,2,1,0:T(8,128)S(1)} collective-permute-done((f32[1,1,2,256,512]{4,3,2,1,0:T(8,128)S(1)}, f32[1,1,2,256,512]{4,3,2,1,0:T(8,128)S(1)}, u32[]{:S(2)}, u32[]{:S(2)}) %collective-permute-start.7) | collective-permute-done | bytes 1048608 | tf_op jit(solution)/shard_map/ppermute | solution.py:16
  169.2 4.6 all-to-all-start
  173.8 19.0 %collective-permute-done.9 = f32[1,1,2,256,512]{4,0,3,2,1:T(1,128)S(1)} collective-permute-done((f32[1,1,2,256,512]{4,0,3,2,1:T(1,128)}, f32[1,1,2,256,512]{4,0,3,2,1:T(1,128)S(1)}, u32[]{:S(2)}, u32[]{:S(2)}) %collective-permute-start.9) | collective-permute-done | bytes 1048608 | tf_op jit(solution)/shard_map/ppermute | solution.py:19
  196.5 4.3 collective-permute-start.11
  202.7 4.4 collective-permute-start.17
  209.0 6.4 %collective-permute-done.17 = f32[8,1,256]{2,1,0:T(1,128)S(1)} collective-permute-done((f32[8,1,256]{2,1,0:T(1,128)S(1)}, f32[8,1,256]{2,1,0:T(1,128)S(1)}, u32[]{:S(2)}, u32[]{:S(2)}) %collective-permute-start.17) | collective-permute-done | bytes 8224 | tf_op jit(solution)/shard_map/ppermute | solution.py:19
  215.5 4.3 collective-permute-start.19
  219.8 10.6 %collective-permute-start.18 = (f32[1,34,256]{2,1,0:T(8,128)S(1)}, f32[1,34,256]{2,1,0:T(8,128)S(1)}, u32[]{:S(2)}, u32[]{:S(2)}) collective-permute-start(f32[1,34,256]{2,1,0:T(8,128)S(1)} %get-tuple-element.17), channel_id=1, source_target_pairs={{1,0},{2,1},{3,2},{4,3},{5,4},{6,5},{7,6},{9,8},{10,9},{11,10},{12... | collective-permute-start | bytes 104456 | tf_op jit(solution)/shard_map/ppermute | solution.py:19
  230.4 15.4 %collective-permute-done.19 = f32[1,34,256]{2,1,0:T(8,128)S(1)} collective-permute-done((f32[1,34,256]{2,1,0:T(8,128)S(1)}, f32[1,34,256]{2,1,0:T(8,128)S(1)}, u32[]{:S(2)}, u32[]{:S(2)}) %collective-permute-start.19) | collective-permute-done | bytes 34848 | tf_op jit(solution)/shard_map/ppermute | solution.py:16
  252.5 136.2 %reshape.146 = f32[8,2,32,2,256,2]{5,4,3,2,1,0:T(8,128)} reshape(f32[4,4,64,512]{3,2,1,0:T(8,128)} %bitcast.92) | data formatting | bytes 4194304 | tf_op jit(solution)/shard_map/reshape | solution.py:57
  388.7 40.6 %reduce_sum.9 = f32[8,32,256]{2,1,0:T(8,128)S(1)} reduce(f32[8,2,32,2,256,2]{5,4,3,2,1,0:T(8,128)} %reshape.146, f32[]{:T(128)} %constant.10.clone.1), dimensions={1,3,5}, to_apply=%region_0.0 | reduce | flops 458752 | bytes 2359300 | tf_op jit(solution)/shard_map/reduce_sum | solution.py:57
  436.9 3.8 fusion.16
  445.4 4.4 collective-permute-start.20
  453.6 13.9 %collective-permute-done.21 = f32[8,1,256]{2,1,0:T(1,128)S(1)} collective-permute-done((f32[8,1,256]{2,1,0:T(1,128)S(1)}, f32[8,1,256]{2,1,0:T(1,128)S(1)}, u32[]{:S(2)}, u32[]{:S(2)}) %collective-permute-start.21) | collective-permute-done | bytes 8224 | tf_op jit(solution)/shard_map/ppermute | solution.py:19
  467.5 5.1 collective-permute-start.23
  474.6 3.7 collective-permute-done.22
  513.4 30.4 %collective-permute-done.31 = f32[1,34,256]{2,1,0:T(8,128)S(1)} collective-permute-done((f32[1,34,256]{2,1,0:T(8,128)S(1)}, f32[1,34,256]{2,1,0:T(8,128)S(1)}, u32[]{:S(2)}, u32[]{:S(2)}) %collective-permute-start.31) | collective-permute-done | bytes 34848 | tf_op jit(solution)/shard_map/ppermute | solution.py:16
  546.5 5.8 %select_maximum_fusion = f32[6,258,514]{2,0,1:T(8,128)S(1)} fusion(f32[1,256,512]{2,0,1:T(1,128)S(1)} %broadcast_select_fusion.2, f32[4,256,512]{2,0,1:T(4,128)S(1)} %copy_divide_fusion, f32[1,256,512]{2,0,1:T(1,128)S(1)} %broadcast_select_fusion), kind=kLoop, calls=%fused_computation.8 | loop fusion | flops 11935080 | bytes 6328416 | tf_op jit(solution)/shard_map/concatenate | solution.py:44
  552.3 8.0 %exponential_bitcast_fusion = f32[1,1,4,256,512]{4,2,3,1,0:T(4,128)S(1)} fusion(f32[6,258,514]{2,0,1:T(8,128)S(1)} %select_maximum_fusion, f32[4,256,512]{2,0,1:T(4,128)S(1)} %copy_divide_fusion, f32[1,256,512]{2,0,1:T(1,128)S(1)} %broadcast_select_fusion, f32[1,256,512]{2,0,1:T(1,128)S(1)} %broadcast_select_fusion.2, ...), kind=kLoop, calls=%fused_computation.64 | loop fusion | flops 4718592 | bytes 17825792 | tf_op jit(solution)/shard_map/broadcast_in_dim | solution.py:72
  (129 shorter events, 105.7 us)
Async XLA Ops:
  0.8 25.0 %collective-permute-start.1 = (f32[1,1,2,256,512]{4,3,2,1,0:T(8,128)S(1)}, f32[1,1,2,256,512]{4,3,2,1,0:T(8,128)S(1)}, u32[]{:S(2)}, u32[]{:S(2)}) collective-permute-start(f32[1,1,2,256,512]{4,3,2,1,0:T(8,128)S(1)} %broadcast_in_dim.41), channel_id=1, source_target_pairs={{8,0},{16,8},{24,16},{0,24},{9,1},{17,9},{25,17},{1,25},{10,2},{18... | collective-permute-start | bytes 3145736 | tf_op jit(solution)/shard_map/ppermute | solution.py:19
  1.5 24.3 %collective-permute-start = (f32[1,1,2,256,512]{4,3,2,1,0:T(8,128)S(1)}, f32[1,1,2,256,512]{4,3,2,1,0:T(8,128)S(1)}, u32[]{:S(2)}, u32[]{:S(2)}) collective-permute-start(f32[1,1,2,256,512]{4,3,2,1,0:T(8,128)S(1)} %broadcast_in_dim.41), channel_id=1, source_target_pairs={{0,8},{8,16},{16,24},{24,0},{1,9},{9,17},{17,25},{25,1},{2,10},{10... | collective-permute-start | bytes 3145736 | tf_op jit(solution)/shard_map/ppermute | solution.py:16
  27.0 48.1 %collective-permute-start.3 = (f32[1,1,2,256,512]{4,3,2,1,0:T(8,128)}, f32[1,1,2,256,512]{4,3,2,1,0:T(8,128)}, u32[]{:S(2)}, u32[]{:S(2)}) collective-permute-start(f32[1,1,2,256,512]{4,3,2,1,0:T(8,128)} %maximum_bitcast_fusion), channel_id=1, source_target_pairs={{0,1},{1,2},{2,3},{3,4},{4,5},{5,6},{6,7},{8,9},{9,10},{10,11},{11... | collective-permute-start | bytes 3145736 | tf_op jit(solution)/shard_map/ppermute | solution.py:16
  30.2 46.1 %collective-permute-start.2 = (f32[1,1,2,256,512]{4,3,2,1,0:T(8,128)}, f32[1,1,2,256,512]{4,3,2,1,0:T(8,128)}, u32[]{:S(2)}, u32[]{:S(2)}) collective-permute-start(f32[1,1,2,256,512]{4,3,2,1,0:T(8,128)} %maximum_bitcast_fusion), channel_id=1, source_target_pairs={{1,0},{2,1},{3,2},{4,3},{5,4},{6,5},{7,6},{9,8},{10,9},{11,10},{12... | collective-permute-start | bytes 3145736 | tf_op jit(solution)/shard_map/ppermute | solution.py:19
  81.9 27.8 %collective-permute-start.5 = (f32[1,1,2,256,512]{4,3,2,1,0:T(8,128)S(1)}, f32[1,1,2,256,512]{4,3,2,1,0:T(8,128)S(1)}, u32[]{:S(2)}, u32[]{:S(2)}) collective-permute-start(f32[1,1,2,256,512]{4,3,2,1,0:T(8,128)S(1)} %maximum_bitcast_fusion.1), channel_id=1, source_target_pairs={{8,0},{16,8},{24,16},{0,24},{9,1},{17,9},{25,17},{1,25},{10,2},{18... | collective-permute-start | bytes 3145736 | tf_op jit(solution)/shard_map/ppermute | solution.py:19
  84.0 25.7 %collective-permute-start.4 = (f32[1,1,2,256,512]{4,3,2,1,0:T(8,128)S(1)}, f32[1,1,2,256,512]{4,3,2,1,0:T(8,128)S(1)}, u32[]{:S(2)}, u32[]{:S(2)}) collective-permute-start(f32[1,1,2,256,512]{4,3,2,1,0:T(8,128)S(1)} %maximum_bitcast_fusion.1), channel_id=1, source_target_pairs={{0,8},{8,16},{16,24},{24,0},{1,9},{9,17},{17,25},{25,1},{2,10},{10... | collective-permute-start | bytes 3145736 | tf_op jit(solution)/shard_map/ppermute | solution.py:16
  109.8 48.5 %collective-permute-start.7 = (f32[1,1,2,256,512]{4,3,2,1,0:T(8,128)S(1)}, f32[1,1,2,256,512]{4,3,2,1,0:T(8,128)S(1)}, u32[]{:S(2)}, u32[]{:S(2)}) collective-permute-start(f32[1,1,2,256,512]{4,3,2,1,0:T(8,128)S(1)} %maximum_bitcast_fusion.2), channel_id=1, source_target_pairs={{0,1},{1,2},{2,3},{3,4},{4,5},{5,6},{6,7},{8,9},{9,10},{10,11},{11... | collective-permute-start | bytes 3145736 | tf_op jit(solution)/shard_map/ppermute | solution.py:16
  111.9 46.4 %collective-permute-start.6 = (f32[1,1,2,256,512]{4,3,2,1,0:T(8,128)S(1)}, f32[1,1,2,256,512]{4,3,2,1,0:T(8,128)S(1)}, u32[]{:S(2)}, u32[]{:S(2)}) collective-permute-start(f32[1,1,2,256,512]{4,3,2,1,0:T(8,128)S(1)} %maximum_bitcast_fusion.2), channel_id=1, source_target_pairs={{1,0},{2,1},{3,2},{4,3},{5,4},{6,5},{7,6},{9,8},{10,9},{11,10},{12... | collective-permute-start | bytes 3145736 | tf_op jit(solution)/shard_map/ppermute | solution.py:19
  167.4 25.4 %collective-permute-start.9 = (f32[1,1,2,256,512]{4,0,3,2,1:T(1,128)}, f32[1,1,2,256,512]{4,0,3,2,1:T(1,128)S(1)}, u32[]{:S(2)}, u32[]{:S(2)}) collective-permute-start(f32[1,1,2,256,512]{4,0,3,2,1:T(1,128)} %broadcast_in_dim.46), channel_id=1, source_target_pairs={{8,0},{16,8},{24,16},{0,24},{9,1},{17,9},{25,17},{1,25},{10,2},{18... | collective-permute-start | bytes 3145736 | tf_op jit(solution)/shard_map/ppermute | solution.py:19
  168.9 24.3 %collective-permute-start.8 = (f32[1,1,2,256,512]{4,0,3,2,1:T(1,128)}, f32[1,1,2,256,512]{4,0,3,2,1:T(1,128)}, u32[]{:S(2)}, u32[]{:S(2)}) collective-permute-start(f32[1,1,2,256,512]{4,0,3,2,1:T(1,128)} %broadcast_in_dim.46), channel_id=1, source_target_pairs={{0,8},{8,16},{16,24},{24,0},{1,9},{9,17},{17,25},{25,1},{2,10},{10... | collective-permute-start | bytes 3145736 | tf_op jit(solution)/shard_map/ppermute | solution.py:16
  169.2 79.7 %all-to-all-start = ((f32[4,256,512]{2,0,1:T(4,128)}), f32[4,256,512]{2,0,1:T(4,128)}, u32[]{:S(2)}, u32[]{:S(2)}) async-start(f32[4,256,512]{2,0,1:T(4,128)} %get-tuple-element.25), calls=%async_computation | async-start | bytes 4194304 | tf_op jit(solution)/shard_map/all_to_all | solution.py:63
  196.5 233.9 %collective-permute-start.11 = (f32[1,1,2,256,512]{4,2,3,1,0:T(2,128)}, f32[1,1,2,256,512]{4,2,3,1,0:T(2,128)}, u32[]{:S(2)}, u32[]{:S(2)}) collective-permute-start(f32[1,1,2,256,512]{4,2,3,1,0:T(2,128)} %maximum_bitcast_fusion.3), channel_id=1, source_target_pairs={{0,1},{1,2},{2,3},{3,4},{4,5},{5,6},{6,7},{8,9},{9,10},{10,11},{11... | collective-permute-start | bytes 3145736 | tf_op jit(solution)/shard_map/ppermute | solution.py:16
  200.8 231.6 %collective-permute-start.10 = (f32[1,1,2,256,512]{4,2,3,1,0:T(2,128)}, f32[1,1,2,256,512]{4,2,3,1,0:T(2,128)}, u32[]{:S(2)}, u32[]{:S(2)}) collective-permute-start(f32[1,1,2,256,512]{4,2,3,1,0:T(2,128)} %maximum_bitcast_fusion.3), channel_id=1, source_target_pairs={{1,0},{2,1},{3,2},{4,3},{5,4},{6,5},{7,6},{9,8},{10,9},{11,10},{12... | collective-permute-start | bytes 3145736 | tf_op jit(solution)/shard_map/ppermute | solution.py:19
  202.7 12.7 %collective-permute-start.17 = (f32[8,1,256]{2,1,0:T(1,128)S(1)}, f32[8,1,256]{2,1,0:T(1,128)S(1)}, u32[]{:S(2)}, u32[]{:S(2)}) collective-permute-start(f32[8,1,256]{2,1,0:T(1,128)S(1)} %broadcast.88), channel_id=1, source_target_pairs={{8,0},{16,8},{24,16},{9,1},{17,9},{25,17},{10,2},{18,10},{26,18},{... | collective-permute-start | bytes 24584 | tf_op jit(solution)/shard_map/ppermute | solution.py:19
  215.5 30.3 %collective-permute-start.19 = (f32[1,34,256]{2,1,0:T(8,128)S(1)}, f32[1,34,256]{2,1,0:T(8,128)S(1)}, u32[]{:S(2)}, u32[]{:S(2)}) collective-permute-start(f32[1,34,256]{2,1,0:T(8,128)S(1)} %get-tuple-element.16), channel_id=1, source_target_pairs={{0,1},{1,2},{2,3},{3,4},{4,5},{5,6},{6,7},{8,9},{9,10},{10,11},{11... | collective-permute-start | bytes 104456 | tf_op jit(solution)/shard_map/ppermute | solution.py:16
  219.8 28.2 %collective-permute-start.18 = (f32[1,34,256]{2,1,0:T(8,128)S(1)}, f32[1,34,256]{2,1,0:T(8,128)S(1)}, u32[]{:S(2)}, u32[]{:S(2)}) collective-permute-start(f32[1,34,256]{2,1,0:T(8,128)S(1)} %get-tuple-element.17), channel_id=1, source_target_pairs={{1,0},{2,1},{3,2},{4,3},{5,4},{6,5},{7,6},{9,8},{10,9},{11,10},{12... | collective-permute-start | bytes 104456 | tf_op jit(solution)/shard_map/ppermute | solution.py:19
  444.9 47.1 %collective-permute-start.13 = (f32[1,1,2,256,512]{4,0,3,2,1:T(1,128)S(1)}, f32[1,1,2,256,512]{4,0,3,2,1:T(1,128)S(1)}, u32[]{:S(2)}, u32[]{:S(2)}) collective-permute-start(f32[1,1,2,256,512]{4,0,3,2,1:T(1,128)S(1)} %broadcast_in_dim.48), channel_id=1, source_target_pairs={{8,0},{16,8},{24,16},{0,24},{9,1},{17,9},{25,17},{1,25},{10,2},{18... | collective-permute-start | bytes 3145736 | tf_op jit(solution)/shard_map/ppermute | solution.py:19
  449.9 17.6 %collective-permute-start.21 = (f32[8,1,256]{2,1,0:T(1,128)S(1)}, f32[8,1,256]{2,1,0:T(1,128)S(1)}, u32[]{:S(2)}, u32[]{:S(2)}) collective-permute-start(f32[8,1,256]{2,1,0:T(1,128)S(1)} %get-tuple-element.23), channel_id=1, source_target_pairs={{8,0},{16,8},{24,16},{9,1},{17,9},{25,17},{10,2},{18,10},{26,18},{... | collective-permute-start | bytes 24584 | tf_op jit(solution)/shard_map/ppermute | solution.py:19
  451.8 40.6 %collective-permute-start.12 = (f32[1,1,2,256,512]{4,0,3,2,1:T(1,128)S(1)}, f32[1,1,2,256,512]{4,0,3,2,1:T(1,128)S(1)}, u32[]{:S(2)}, u32[]{:S(2)}) collective-permute-start(f32[1,1,2,256,512]{4,0,3,2,1:T(1,128)S(1)} %broadcast_in_dim.48), channel_id=1, source_target_pairs={{0,8},{8,16},{16,24},{24,0},{1,9},{9,17},{17,25},{25,1},{2,10},{10... | collective-permute-start | bytes 3145736 | tf_op jit(solution)/shard_map/ppermute | solution.py:16
  486.7 10.0 %collective-permute-start.27 = (f32[1,34,256]{2,1,0:T(8,128)S(1)}, f32[1,34,256]{2,1,0:T(8,128)S(1)}, u32[]{:S(2)}, u32[]{:S(2)}) collective-permute-start(f32[1,34,256]{2,1,0:T(8,128)S(1)} %get-tuple-element.12), channel_id=1, source_target_pairs={{0,1},{1,2},{2,3},{3,4},{4,5},{5,6},{6,7},{8,9},{9,10},{10,11},{11... | collective-permute-start | bytes 104456 | tf_op jit(solution)/shard_map/ppermute | solution.py:16
  493.7 51.4 %collective-permute-start.15 = (f32[1,1,2,256,512]{4,2,3,1,0:T(2,128)S(1)}, f32[1,1,2,256,512]{4,2,3,1,0:T(2,128)S(1)}, u32[]{:S(2)}, u32[]{:S(2)}) collective-permute-start(f32[1,1,2,256,512]{4,2,3,1,0:T(2,128)S(1)} %maximum_bitcast_fusion.4), channel_id=1, source_target_pairs={{0,1},{1,2},{2,3},{3,4},{4,5},{5,6},{6,7},{8,9},{9,10},{10,11},{11... | collective-permute-start | bytes 3145736 | tf_op jit(solution)/shard_map/ppermute | solution.py:16
  497.0 48.7 %collective-permute-start.14 = (f32[1,1,2,256,512]{4,2,3,1,0:T(2,128)S(1)}, f32[1,1,2,256,512]{4,2,3,1,0:T(2,128)S(1)}, u32[]{:S(2)}, u32[]{:S(2)}) collective-permute-start(f32[1,1,2,256,512]{4,2,3,1,0:T(2,128)S(1)} %maximum_bitcast_fusion.4), channel_id=1, source_target_pairs={{1,0},{2,1},{3,2},{4,3},{5,4},{6,5},{7,6},{9,8},{10,9},{11,10},{12... | collective-permute-start | bytes 3145736 | tf_op jit(solution)/shard_map/ppermute | solution.py:19
  507.9 35.9 %collective-permute-start.31 = (f32[1,34,256]{2,1,0:T(8,128)S(1)}, f32[1,34,256]{2,1,0:T(8,128)S(1)}, u32[]{:S(2)}, u32[]{:S(2)}) collective-permute-start(f32[1,34,256]{2,1,0:T(8,128)S(1)} %get-tuple-element.10), channel_id=1, source_target_pairs={{0,1},{1,2},{2,3},{3,4},{4,5},{5,6},{6,7},{8,9},{9,10},{10,11},{11... | collective-permute-start | bytes 104456 | tf_op jit(solution)/shard_map/ppermute | solution.py:16
  511.5 32.3 %collective-permute-start.30 = (f32[1,34,256]{2,1,0:T(8,128)S(1)}, f32[1,34,256]{2,1,0:T(8,128)S(1)}, u32[]{:S(2)}, u32[]{:S(2)}) collective-permute-start(f32[1,34,256]{2,1,0:T(8,128)S(1)} %get-tuple-element.11), channel_id=1, source_target_pairs={{1,0},{2,1},{3,2},{4,3},{5,4},{6,5},{7,6},{9,8},{10,9},{11,10},{12... | collective-permute-start | bytes 104456 | tf_op jit(solution)/shard_map/ppermute | solution.py:19
  (19 other events, 164.1 us)
where the time goes:
time: 573 us; the launch traced here: 563 us
  waiting for transfers between devices  224 us (39%)
  local copies, waits for them, and re-layouts  154 us (27%)
  starting transfers between devices  91.9 us (16%)
  other arithmetic  91 us (16%)
    reshape x1, local copies, waits for them, and re-layouts, block_sum(): values.reshape(depth // 2, 2, rows // 2, 2, cols // 2, 2)  136 us
    ppermute x16, waiting for transfers between devices, extended(): lax.ppermute(lax.slice_in_dim(block, block.shape[dim] - width, None, axis...  125 us
    ppermute x16, waiting for transfers between devices, extended(): lax.ppermute(lax.slice_in_dim(block, 0, width, axis=dim), axis, backward)  98.3 us
    ppermute x16, starting transfers between devices, extended(): lax.ppermute(lax.slice_in_dim(block, block.shape[dim] - width, None, axis...  44.9 us
    ppermute x16, starting transfers between devices, extended(): lax.ppermute(lax.slice_in_dim(block, 0, width, axis=dim), axis, backward)  42.4 us
    reduce_sum x1, other arithmetic, block_sum(): values.reshape(depth // 2, 2, rows // 2, 2, cols // 2, 2)  40.6 us
  transfers between devices with their start and end apart: 33, of which 13 were waited for; matrix products, arithmetic and copies ran while one was open for 35% of the time, Pallas kernels for 0%

commit v1 on v0

v1 whole, which is shorter than its diff:
```python
import functools

import jax
import jax.numpy as jnp
from jax import lax
from jax.experimental import pallas as pl
from jax.experimental.pallas import tpu as pltpu
from jax.sharding import PartitionSpec as P

SWEEPS = 4
HALO = SWEEPS - 1
ROWPAD = 4
STRIP = 32
LIMIT = 56 * 1024 * 1024


def whole():
    return pl.BlockSpec(memory_space=pltpu.VMEM)


def scalar():
    return pl.BlockSpec(memory_space=pltpu.SMEM)


def anywhere():
    return pl.BlockSpec(memory_space=pl.ANY)


def cost(cells, ops, arrays, transcendentals=0):
    return pl.CostEstimate(
        flops=cells * ops, bytes_accessed=4 * cells * arrays, transcendentals=transcendentals
    )


def lane_sum(c):
    cols = c.shape[-1]
    lane = lax.broadcasted_iota(jnp.int32, c.shape, c.ndim - 1)
    left = jnp.where(lane == 0, 0.0, pltpu.roll(c, 1, axis=c.ndim - 1))
    right = jnp.where(lane == cols - 1, 0.0, pltpu.roll(c, cols - 1, axis=c.ndim - 1))
    return left + right


def plane_sum(load, start, size, rows):
    c = load(start, size)
    above = load(pl.multiple_of(jnp.maximum(start - 8, 0), 8), 8)[7:8]
    below = load(pl.multiple_of(jnp.minimum(start + size, rows - 8), 8), 8)[0:1]
    above = jnp.where(start > 0, above, 0.0)
    below = jnp.where(start + size < rows, below, 0.0)
    sub = lax.broadcasted_iota(jnp.int32, c.shape, 0)
    up = jnp.where(sub == 0, above, pltpu.roll(c, 1, axis=0))
    down = jnp.where(sub == size - 1, below, pltpu.roll(c, size - 1, axis=0))
    return (up + down) + lane_sum(c)


def loader(ref, *lead):
    return lambda start, size: ref[(*lead, pl.ds(start, size), slice(None))]


def strips(rows, body):
    @pl.loop(0, rows // STRIP)
    def _(k):
        body(pl.multiple_of(k * STRIP, STRIP))


def advance(field, b, r, rows, face_off, face_on, mid):
    depth = len(field)

    def body(i):
        for m in range(depth):
            total = plane_sum(field[m], i, STRIP, rows)
            if m > 0:
                total = total + field[m - 1](i, STRIP)
            if m < depth - 1:
                total = total + field[m + 1](i, STRIP)
            rows_of = pl.ds(i, STRIP)
            value = b[m, rows_of, :] + r[m, rows_of, :] * total
            if m == 0:
                face_off[rows_of, :] = value
            elif m == depth - 1:
                face_on[rows_of, :] = value
            else:
                mid(m - 1, rows_of, value)

    strips(rows, body)


def first_kernel(flip_ref, noise, kappa, b, r, part_off, part_on, mid):
    depth, rows, _ = b.shape
    flip = flip_ref[0]

    def prepare(i):
        for m in range(depth):
            src = m + flip * (depth - 1 - 2 * m)
            at = pl.ds(i, STRIP)
            inverse = 1.0 / (6.0 + kappa[src, at, :])
            r[m, at, :] = inverse
            b[m, at, :] = noise[src, at, :] * inverse

    strips(rows, prepare)
    field = [loader(b, m) for m in range(depth)]

    def put(m, at, value):
        mid[m, at, :] = value

    advance(field, b, r, rows, part_off, part_on, put)


def middle_kernel(off, on, old_mid, b, r, part_off, part_on, mid):
    depth, rows, _ = b.shape
    field = [loader(off)] + [loader(old_mid, m) for m in range(depth - 2)] + [loader(on)]

    def put(m, at, value):
        mid[m, at, :] = value

    advance(field, b, r, rows, part_off, part_on, put)


def last_kernel(flip_ref, off, on, old_mid, b, r, part_off, part_on, out, mid, sems):
    depth, rows, _ = b.shape
    flip = flip_ref[0]
    field = [loader(off)] + [loader(old_mid, m) for m in range(depth - 2)] + [loader(on)]

    def put(m, at, value):
        mid[m, at, :] = jnp.exp(value)

    advance(field, b, r, rows, part_off, part_on, put)
    copies = []
    for m in range(1, depth - 1):
        dst = m + flip * (depth - 1 - 2 * m)
        copies.append(pltpu.make_async_copy(mid.at[m - 1], out.at[dst], sems.at[m - 1]))
    for copy in copies:
        copy.start()
    for copy in copies:
        copy.wait()


def face_kernel(layer_ref, part, r, halo, old, out):
    del layer_ref, old
    out[0] = jnp.exp(part[...] + r[0] * halo[...])


def restrict_kernel(place_ref, noise, kappa, blocks, pair, fine_rows):
    depth, rows, cols = noise.shape
    groups = blocks.shape[0]
    half_rows, half_cols = rows // 2, cols // 2
    own_rows = half_rows // groups
    span = own_rows + 2 * ROWPAD
    position = place_ref[0]
    src = lax.broadcasted_iota(jnp.int32, (cols, half_cols), 0)
    dst = lax.broadcasted_iota(jnp.int32, (cols, half_cols), 1)
    fold = jnp.where(src // 2 == dst, 0.125, 0.0).astype(jnp.bfloat16)
    zero = jnp.zeros((8, half_cols), jnp.float32)
    for layer in range(depth // 2):
        pair[...] = noise[2 * layer] + noise[2 * layer + 1]
        cut = cols // 128
        pieces = []
        for c in range(cut):
            fine_rows[...] = pair[:, 128 * c : 128 * (c + 1)]
            pieces.append(
                fine_rows[pl.ds(0, half_rows, stride=2), :]
                + fine_rows[pl.ds(1, half_rows, stride=2), :]
            )
        summed = jnp.concatenate(pieces, axis=1)
        high = summed.astype(jnp.bfloat16)
        rest = summed - high.astype(jnp.float32)
        middle = rest.astype(jnp.bfloat16)
        low = (rest - middle.astype(jnp.float32)).astype(jnp.bfloat16)
        dot = functools.partial(jnp.dot, preferred_element_type=jnp.float32)
        coarse = dot(low, fold) + dot(middle, fold) + dot(high, fold)
        padded = jnp.concatenate([zero[:ROWPAD], coarse, zero[:ROWPAD]], axis=0)
        for g in range(groups):
            blocks[g, layer * span : (layer + 1) * span, :] = padded[
                g * own_rows : g * own_rows + span
            ]
    base = (depth // 2) * span
    layers = kappa.shape[0]
    for layer in range(layers):
        first = 1.0 / (1.5 + kappa[layer, 0:ROWPAD, :])
        last = 1.0 / (1.5 + kappa[layer, own_rows - ROWPAD : own_rows, :])
        for g in range(groups):
            sent = jnp.where(position + 1 == g, last, jnp.where(position - 1 == g, first, 0.0))
            blocks[g, base + layer * ROWPAD : base + (layer + 1) * ROWPAD, :] = sent


def frame_kernel(place_ref, blocks, kappa, own, up, down):
    groups = blocks.shape[0]
    layers, own_rows, _ = kappa.shape
    span = own_rows + 2 * ROWPAD
    per = layers // groups
    base = per * span
    position = place_ref[0]
    for layer in range(layers):
        g, k = layer // per, layer % per
        noise = blocks[g, k * span : (k + 1) * span, :]
        at = slice(base + layer * ROWPAD, base + (layer + 1) * ROWPAD)
        top = jnp.where(position > 0, blocks[jnp.maximum(position - 1, 0), at, :], 0.0)
        bottom = jnp.where(
            position < groups - 1, blocks[jnp.minimum(position + 1, groups - 1), at, :], 0.0
        )
        middle = 1.0 / (1.5 + kappa[layer])
        inverse = jnp.concatenate([top, middle, bottom], axis=0)
        own[0, layer] = noise
        own[1, layer] = inverse
        if layer < HALO:
            down[0, layer] = noise
            down[1, layer] = inverse
        if layer >= layers - HALO:
            up[0, layer - layers + HALO] = noise
            up[1, layer - layers + HALO] = inverse


def coarse_kernel(own, below, above, out, b, r, even, odd):
    layers, own_rows, _ = out.shape
    total_layers, span, cols = b.shape
    total = total_layers

    def prepare(dst, ref, src):
        inverse = ref[1, src]
        r[dst] = 0.25 * inverse
        b[dst] = ref[0, src] * inverse

    for k in range(HALO):
        prepare(k, below, k)
        prepare(HALO + layers + k, above, k)

    @pl.loop(0, layers)
    def _(k):
        prepare(HALO + k, own, k)

    sub = lax.broadcasted_iota(jnp.int32, (span, cols), 0)

    def sweep(src, layer):
        c = src[layer]
        up = jnp.where(sub == 0, 0.0, pltpu.roll(c, 1, axis=0))
        dn = jnp.where(sub == span - 1, 0.0, pltpu.roll(c, span - 1, axis=0))
        near = (up + dn) + lane_sum(c) + (src[layer - 1] + src[layer + 1])
        return b[layer] + r[layer] * near

    source = b
    for step in range(1, SWEEPS):
        target = odd if step % 2 else even
        if step < SWEEPS - 1:

            @pl.loop(step, total - step)
            def _(layer):
                target[layer] = sweep(source, layer)

        else:

            @pl.loop(HALO, HALO + layers)
            def _(layer):
                value = jnp.exp(sweep(source, layer))
                out[layer - HALO] = value[ROWPAD : ROWPAD + own_rows]

        source = target


def body(axes, fine_noise, fine_kappa, coarse_kappa):
    noise = fine_noise[0, 0]
    kappa = fine_kappa[0, 0]
    depth, rows, cols = noise.shape
    layers, own_rows, half_cols = coarse_kappa.shape
    groups, slabs = lax.axis_size("grp"), lax.axis_size("slab")
    count = groups * slabs
    size = {"grp": groups, "slab": slabs}

    def flat(link):
        where = {"grp": link % groups, "slab": link // groups}
        index = 0
        for axis in axes:
            index = index * size[axis] + where[axis]
        return index

    near, far = [], []
    for link in range(count - 1):
        both = [(flat(link), flat(link + 1)), (flat(link + 1), flat(link))]
        (far if link % 2 else near).extend(both)
    position = lax.axis_index("grp")
    flip = (position % 2).astype(jnp.int32)
    flip1 = flip[None]
    place = position.astype(jnp.int32)[None]
    params = pltpu.CompilerParams(vmem_limit_bytes=LIMIT)
    cells = rows * cols
    plane = jax.ShapeDtypeStruct((rows, cols), jnp.float32)
    stack = jax.ShapeDtypeStruct((depth, rows, cols), jnp.float32)
    inner = jax.ShapeDtypeStruct((depth - 2, rows, cols), jnp.float32)

    def swap(off, on):
        return lax.ppermute(off, axes, far), lax.ppermute(on, axes, near)

    def face(layer):
        n = lax.dynamic_index_in_dim(noise, layer, 0, keepdims=False)
        k = lax.dynamic_index_in_dim(kappa, layer, 0, keepdims=False)
        return n / (6.0 + k)

    index_off = flip * (depth - 1)
    index_on = (1 - flip) * (depth - 1)
    halo_off, halo_on = swap(face(index_off), face(index_on))

    span = own_rows + 2 * ROWPAD
    block_rows = (depth // 2) * span + layers * ROWPAD
    blocks = pl.pallas_call(
        restrict_kernel,
        name="restrict",
        out_shape=jax.ShapeDtypeStruct((groups, block_rows, half_cols), jnp.float32),
        in_specs=[scalar(), whole(), whole()],
        out_specs=whole(),
        scratch_shapes=[
            pltpu.VMEM((rows, cols), jnp.float32),
            pltpu.VMEM((rows, 128), jnp.float32),
        ],
        compiler_params=params,
        cost_estimate=cost(cells * depth, 8, 1),
    )(place, noise, coarse_kappa)
    blocks = lax.all_to_all(blocks, "grp", split_axis=0, concat_axis=0, tiled=True)

    b, r, part_off, part_on, mid = pl.pallas_call(
        first_kernel,
        name="first",
        out_shape=(stack, stack, plane, plane, inner),
        in_specs=[scalar(), whole(), whole()],
        out_specs=(whole(),) * 5,
        compiler_params=params,
        cost_estimate=cost(cells * depth, 16, 5),
    )(flip1, noise, kappa)

    edge = jax.ShapeDtypeStruct((2, HALO, span, half_cols), jnp.float32)
    own, up, down = pl.pallas_call(
        frame_kernel,
        name="frame",
        out_shape=(
            jax.ShapeDtypeStruct((2, layers, span, half_cols), jnp.float32),
            edge,
            edge,
        ),
        in_specs=[scalar(), whole(), whole()],
        out_specs=(whole(),) * 3,
        compiler_params=params,
        cost_estimate=cost(layers * span * half_cols, 4, 5),
    )(place, blocks, coarse_kappa)
    ahead = [(i, i + 1) for i in range(slabs - 1)]
    back = [(i + 1, i) for i in range(slabs - 1)]
    below = lax.ppermute(up, "slab", ahead)
    above = lax.ppermute(down, "slab", back)

    off = part_off + r[0] * halo_off
    on = part_on + r[depth - 1] * halo_on
    halo_off, halo_on = swap(off, on)
    part_off, part_on, mid = pl.pallas_call(
        middle_kernel,
        name="middle",
        out_shape=(plane, plane, inner),
        in_specs=[whole()] * 5,
        out_specs=(whole(),) * 3,
        compiler_params=params,
        cost_estimate=cost(cells * depth, 12, 4),
    )(off, on, mid, b, r)

    off = part_off + r[0] * halo_off
    on = part_on + r[depth - 1] * halo_on
    halo_off, halo_on = swap(off, on)
    part_off, part_on, fine = pl.pallas_call(
        last_kernel,
        name="last",
        out_shape=(plane, plane, stack),
        in_specs=[scalar()] + [whole()] * 5,
        out_specs=(whole(), whole(), anywhere()),
        scratch_shapes=[
            pltpu.VMEM((depth - 2, rows, cols), jnp.float32),
            pltpu.SemaphoreType.DMA((depth - 2,)),
        ],
        compiler_params=params,
        cost_estimate=cost(cells * depth, 14, 4, cells * 2),
    )(flip1, off, on, mid, b, r)

    framed = (layers + 2 * HALO, span, half_cols)
    coarse = pl.pallas_call(
        coarse_kernel,
        name="coarse",
        out_shape=jax.ShapeDtypeStruct(coarse_kappa.shape, jnp.float32),
        in_specs=[whole()] * 3,
        out_specs=whole(),
        scratch_shapes=[pltpu.VMEM(framed, jnp.float32)] * 4,
        compiler_params=params,
        cost_estimate=cost(layers * own_rows * half_cols, 80, 6),
    )(own, below, above)

    tile = rows // 4

    def finish(fine, layer, source, part, halo):
        return pl.pallas_call(
            face_kernel,
            name="face",
            out_shape=stack,
            grid_spec=pltpu.PrefetchScalarGridSpec(
                num_scalar_prefetch=1,
                grid=(rows // tile,),
                in_specs=[
                    pl.BlockSpec((tile, cols), lambda i, at: (i, 0)),
                    pl.BlockSpec((1, tile, cols), lambda i, at: (source, i, 0)),
                    pl.BlockSpec((tile, cols), lambda i, at: (i, 0)),
                    anywhere(),
                ],
                out_specs=pl.BlockSpec((1, tile, cols), lambda i, at: (at[0], i, 0)),
            ),
            input_output_aliases={4: 0},
            compiler_params=params,
            cost_estimate=cost(cells, 3, 4, cells),
        )(layer[None], part, r, halo, fine)

    fine = finish(fine, index_on, depth - 1, part_on, halo_on)
    fine = finish(fine, index_off, 0, part_off, halo_off)
    return fine[None, None], coarse


def solution(mesh):
    return jax.shard_map(
        functools.partial(body, tuple(mesh.axis_names)),
        mesh=mesh,
        in_specs=(
            P("slab", "grp", None, None, None),
            P("slab", "grp", None, None, None),
            P("slab", "grp", None),
        ),
        out_specs=(P("slab", "grp", None, None, None), P("slab", "grp", None)),
        check_vma=False,
    )
```

time: 573 us -> 85.9 us (0.15); the launches traced: 563 us -> 84.5 us
  waiting for transfers between devices: 224 us -> 18.8 us
  local copies, waits for them, and re-layouts: 154 us -> 2.38 us
  other arithmetic: 91 us -> 5.16 us
  starting transfers between devices: 91.9 us -> 20.9 us
  Pallas kernels: 0 us -> 36.4 us
    ppermute x32 -> x8, waiting for transfers between devices: 224 us -> 18.8 us  [the longest x1 12.9 us: body(): below = lax.ppermute(up, 'slab', ahead)]
    reshape x1 -> x0, local copies, waits for them, and re-layouts: 136 us -> none  [block_sum(): values.reshape(depth // 2, 2, rows // 2, 2, cols // 2, 2)]
    ppermute x32 -> x8, starting transfers between devices: 87.3 us -> 16.8 us  [the longest x6 11.6 us: swap(): return (lax.ppermute(off, axes, far), lax.ppermute(on, axes, near))]
    reduce_sum x1 -> x0, other arithmetic: 40.6 us -> none  [block_sum(): values.reshape(depth // 2, 2, rows // 2, 2, cols // 2, 2)]
    pallas_call x0 -> x8, Pallas kernels: none -> 36.4 us  [the longest x2 6.87 us: finish(): pl.pallas_call(face_kernel, name='face', out_shape=stack, grid_spec=pltpu...]
    broadcast_in_dim x6 -> x0, other arithmetic: 12.2 us -> none  [the longest x1 7.98 us: body(): fine_stiffness = jnp.exp(fine_field)[None, None]]
    concatenate x12 -> x0, other arithmetic: 12 us -> none  [the longest x4 10.8 us: fine_sweep(): stacked = jnp.concatenate([lower[None], field, upper[None]], axis=0)]
    div x6 -> x1, other arithmetic: 11.4 us -> 1.75 us  [face(): return n / (6.0 + k)]
  transfers between devices with their start and end apart: 33 -> 9, of which waited for: 13 -> 2; matrix products, arithmetic and copies ran while one was open for 35% -> 2% of each run, Pallas kernels for 0% -> 39%
where the time goes in v1:
time: 85.9 us; the launch traced here: 84.5 us
  Pallas kernels  36.4 us (42%)
  starting transfers between devices  20.9 us (24%)
  waiting for transfers between devices  18.8 us (22%)
  other arithmetic  5.16 us (6%)
  local copies, waits for them, and re-layouts  2.38 us (3%)
    ppermute x1, waiting for transfers between devices, body(): below = lax.ppermute(up, 'slab', ahead)  12.9 us
    ppermute x6, starting transfers between devices, swap(): return (lax.ppermute(off, axes, far), lax.ppermute(on, axes, near))  11.6 us
    pallas_call x2, Pallas kernels, finish(): pl.pallas_call(face_kernel, name='face', out_shape=stack, grid_spec=pltpu...  6.87 us
    pallas_call x1, Pallas kernels, body(): pl.pallas_call(first_kernel, name='first', out_shape=(stack, stack, plane...  6.78 us
    pallas_call x1, Pallas kernels, body(): pl.pallas_call(last_kernel, name='last', out_shape=(plane, plane, stack),...  6.56 us
    pallas_call x1, Pallas kernels, body(): pl.pallas_call(middle_kernel, name='middle', out_shape=(plane, plane, inn...  5.97 us
    ppermute x6, waiting for transfers between devices, swap(): return (lax.ppermute(off, axes, far), lax.ppermute(on, axes, near))  5.86 us
    pallas_call x1, Pallas kernels, body(): pl.pallas_call(coarse_kernel, name='coarse', out_shape=jax.ShapeDtypeStru...  5.1 us
  transfers between devices with their start and end apart: 9, of which 2 were waited for; matrix products, arithmetic and copies ran while one was open for 2% of the time, Pallas kernels for 39%

profile of v1, /device:TPU:13, one launch (start us, length us, event | category | flops | bytes accessed | tf_op | source)
XLA Modules:
  0.0 84.5 jit_solution(8971005635363312727)
XLA Ops:
  0.7 1.7 %divide_bitcast_fusion = (f32[256,512]{1,0:T(8,128)S(1)}, f32[256,512]{1,0:T(8,128)S(1)}) fusion(f32[1,1,4,256,512]{4,3,2,1,0:T(8,128)} %param.4, s32[]{:T(128)S(6)} %select_n.18, f32[1,1,4,256,512]{4,3,2,1,0:T(8,128)} %param.3, s32[]{:T(128)S(6)} %select_n.17), kind=kLoop, calls=%fused_computation.8 | loop fusion | flops 524288 | bytes 3145736 | tf_op jit(solution)/shard_map/div | solution.py:294
  2.4 3.7 %collective-permute-start = (f32[256,512]{1,0:T(8,128)S(1)}, f32[256,512]{1,0:T(8,128)S(1)}, u32[]{:S(2)}, u32[]{:S(2)}) collective-permute-start(f32[256,512]{1,0:T(8,128)S(1)} %get-tuple-element.31), channel_id=1, source_target_pairs={{8,16},{16,8},{24,1},{1,24},{9,17},{17,9},{25,2},{2,25},{10,18},{1... | collective-permute-start | bytes 1572872 | tf_op jit(solution)/shard_map/ppermute | solution.py:289
  6.2 6.8 %first.1 = (f32[4,256,512]{2,1,0:T(8,128)}, f32[4,256,512]{2,1,0:T(8,128)}, f32[256,512]{1,0:T(8,128)}, f32[256,512]{1,0:T(8,128)}, f32[2,256,512]{2,1,0:T(8,128)}) custom-call(s32[1]{0:T(128)} %bitcast.1.flip_ref, f32[4,256,512]{2,1,0:T(8,128)} %bitcast.25, f32[4,256,512]{2,1,0:T(8,128)} %bitcast.28), custom_call_target="tpu_custom_call" | custom-call | flops 8388608 | bytes 10485760 | tf_op jit(solution)/shard_map/first/pallas_call | solution.py:317
  13.0 5.8 %collective-permute-done = f32[256,512]{1,0:T(8,128)S(1)} collective-permute-done((f32[256,512]{1,0:T(8,128)S(1)}, f32[256,512]{1,0:T(8,128)S(1)}, u32[]{:S(2)}, u32[]{:S(2)}) %collective-permute-start) | collective-permute-done | bytes 524320 | tf_op jit(solution)/shard_map/ppermute | solution.py:289
  18.8 1.9 %fusion = (f32[256,512]{1,0:T(8,128)S(1)}, f32[256,512]{1,0:T(8,128)S(1)}) fusion(f32[256,512]{1,0:T(8,128)} %get-tuple-element.18, f32[256,512]{1,0:T(8,128)S(1)} %collective-permute-done.1, f32[4,256,512]{2,1,0:T(8,128)} %get-tuple-element.17.r, f32[256,512]{1,0:T(8,128)} %get-tuple-element.16, f32[256,512]{1,0:T(8,128)S(1)} %collective-permute-done), kind=kLoop, calls=%fused_computation.2 | loop fusion | flops 524288 | bytes 4194304 | tf_op jit(solution)/shard_map/add | solution.py:347
  20.7 3.4 %collective-permute-start.2 = (f32[256,512]{1,0:T(8,128)S(1)}, f32[256,512]{1,0:T(8,128)S(1)}, u32[]{:S(2)}, u32[]{:S(2)}) collective-permute-start(f32[256,512]{1,0:T(8,128)S(1)} %get-tuple-element.35.off), channel_id=1, source_target_pairs={{8,16},{16,8},{24,1},{1,24},{9,17},{17,9},{25,2},{2,25},{10,18},{1... | collective-permute-start | bytes 1572872 | tf_op jit(solution)/shard_map/ppermute | solution.py:289
  24.1 0.7 collective-permute-start.3
  24.8 3.0 %restrict.1 = f32[4,112,256]{2,1,0:T(8,128)} custom-call(s32[1]{0:T(128)} %bitcast.10.place_ref, f32[4,256,512]{2,1,0:T(8,128)} %bitcast.26, f32[8,32,256]{2,1,0:T(8,128)} %kappa.3), custom_call_target="tpu_custom_call" | custom-call | flops 4194304 | bytes 2097152 | tf_op jit(solution)/shard_map/restrict/pallas_call | solution.py:302
  27.8 4.1 %all-to-all-start = ((f32[4,112,256]{2,1,0:T(8,128)}), f32[4,112,256]{2,1,0:T(8,128)}, u32[]{:S(2)}, u32[]{:S(2)}) async-start(f32[4,112,256]{2,1,0:T(8,128)} %restrict.1), calls=%async_computation | async-start | bytes 917504 | tf_op jit(solution)/shard_map/all_to_all | solution.py:315
  31.9 6.0 %middle.1 = (f32[256,512]{1,0:T(8,128)}, f32[256,512]{1,0:T(8,128)}, f32[2,256,512]{2,1,0:T(8,128)}) custom-call(f32[256,512]{1,0:T(8,128)} %copy-done.4, f32[256,512]{1,0:T(8,128)} %copy-done.3, f32[2,256,512]{2,1,0:T(8,128)} %get-tuple-element.19.old_mid, f32[4,256,512]{2,1,0:T(8,128)} %get-tuple-element.20.b, f32[4,256,512]{2,1,0:T(8,128)} %get-tuple-element.17.r), custom_call_target="tpu_custom_call" | custom-call | flops 6291456 | bytes 8388608 | tf_op jit(solution)/shard_map/middle/pallas_call | solution.py:349
  37.9 1.6 %fusion.1 = (f32[256,512]{1,0:T(8,128)S(1)}, f32[256,512]{1,0:T(8,128)S(1)}) fusion(f32[256,512]{1,0:T(8,128)} %get-tuple-element.22, f32[256,512]{1,0:T(8,128)S(1)} %collective-permute-done.3, f32[4,256,512]{2,1,0:T(8,128)S(1)} %copy-done, f32[256,512]{1,0:T(8,128)} %get-tuple-element.21, f32[256,512]{1,0:T(8,128)S(1)} %collective-permute-done.2), kind=kLoop, calls=%fused_computation.3 | loop fusion | flops 524288 | bytes 4194304 | tf_op jit(solution)/shard_map/add | solution.py:360
  39.5 0.2 collective-permute-start.5
  39.7 3.5 %collective-permute-start.4 = (f32[256,512]{1,0:T(8,128)S(1)}, f32[256,512]{1,0:T(8,128)S(1)}, u32[]{:S(2)}, u32[]{:S(2)}) collective-permute-start(f32[256,512]{1,0:T(8,128)S(1)} %get-tuple-element.33.off), channel_id=1, source_target_pairs={{8,16},{16,8},{24,1},{1,24},{9,17},{17,9},{25,2},{2,25},{10,18},{1... | collective-permute-start | bytes 1572872 | tf_op jit(solution)/shard_map/ppermute | solution.py:289
  43.2 2.1 %frame.1 = (f32[2,8,40,256]{3,2,1,0:T(8,128)}, f32[2,3,40,256]{3,2,1,0:T(8,128)}, f32[2,3,40,256]{3,2,1,0:T(8,128)}) custom-call(s32[1]{0:T(128)} %bitcast.10.place_ref, f32[4,112,256]{2,1,0:T(8,128)} %all-to-all-done.blocks, f32[8,32,256]{2,1,0:T(8,128)} %kappa.3), custom_call_target="tpu_custom_call" | custom-call | flops 327680 | bytes 1638400 | tf_op jit(solution)/shard_map/frame/pallas_call | solution.py:328
  45.3 3.4 %collective-permute-start.6 = (f32[2,3,40,256]{3,2,1,0:T(8,128)}, f32[2,3,40,256]{3,2,1,0:T(8,128)S(1)}, u32[]{:S(2)}, u32[]{:S(2)}) collective-permute-start(f32[2,3,40,256]{3,2,1,0:T(8,128)} %get-tuple-element.28), channel_id=1, source_target_pairs={{0,1},{1,2},{2,3},{3,4},{4,5},{5,6},{6,7},{8,9},{9,10},{10,11},{11... | collective-permute-start | bytes 737288 | tf_op jit(solution)/shard_map/ppermute | solution.py:343
  48.7 1.9 %collective-permute-start.7 = (f32[2,3,40,256]{3,2,1,0:T(8,128)}, f32[2,3,40,256]{3,2,1,0:T(8,128)S(1)}, u32[]{:S(2)}, u32[]{:S(2)}) collective-permute-start(f32[2,3,40,256]{3,2,1,0:T(8,128)} %get-tuple-element.29), channel_id=1, source_target_pairs={{1,0},{2,1},{3,2},{4,3},{5,4},{6,5},{7,6},{9,8},{10,9},{11,10},{12... | collective-permute-start | bytes 737288 | tf_op jit(solution)/shard_map/ppermute | solution.py:344
  50.6 12.9 %collective-permute-done.6.below = f32[2,3,40,256]{3,2,1,0:T(8,128)S(1)} collective-permute-done((f32[2,3,40,256]{3,2,1,0:T(8,128)}, f32[2,3,40,256]{3,2,1,0:T(8,128)S(1)}, u32[]{:S(2)}, u32[]{:S(2)}) %collective-permute-start.6) | collective-permute-done | bytes 245792 | tf_op jit(solution)/shard_map/ppermute | solution.py:343
  63.6 0.7 copy-done.7
  64.4 5.1 %coarse.1 = f32[8,32,256]{2,1,0:T(8,128)} custom-call(f32[2,8,40,256]{3,2,1,0:T(8,128)} %get-tuple-element.27.own, f32[2,3,40,256]{3,2,1,0:T(8,128)} %copy-done.7, f32[2,3,40,256]{3,2,1,0:T(8,128)} %copy-done.8), custom_call_target="tpu_custom_call" | custom-call | flops 5242880 | bytes 1572864 | tf_op jit(solution)/shard_map/coarse/pallas_call | solution.py:377
  69.5 6.6 %last.1 = (f32[256,512]{1,0:T(8,128)}, f32[256,512]{1,0:T(8,128)}, f32[4,256,512]{2,1,0:T(8,128)}) custom-call(s32[1]{0:T(128)} %bitcast.1.flip_ref, f32[256,512]{1,0:T(8,128)} %copy-done.1, f32[256,512]{1,0:T(8,128)} %copy-done.2, f32[2,256,512]{2,1,0:T(8,128)} %get-tuple-element.23.old_mid, f32[4,256,512]{2,1,0:T(8,128)} %get-tuple-element.20.b, ...), custom_call_target="tpu_custom_call" | custom-call | flops 7340032 | bytes 8388608 | tf_op jit(solution)/shard_map/last/pallas_call | solution.py:362
  76.1 0.8 copy-done.6
  76.8 3.4 %face.2.old = f32[4,256,512]{2,1,0:T(8,128)} custom-call(s32[1]{0:T(128)} %bitcast.8.layer_ref, f32[256,512]{1,0:T(8,128)} %get-tuple-element.25.part, f32[4,256,512]{2,1,0:T(8,128)} %get-tuple-element.17.r, f32[256,512]{1,0:T(8,128)} %copy-done.6, f32[4,256,512]{2,1,0:T(8,128)} %get-tuple-element.26.old), custom_call_target="tpu_custom_call", output_to_operand_aliasing={{}: (4, {})} | custom-call | flops 393216 | bytes 2097152 | tf_op jit(solution)/shard_map/face/pallas_call | solution.py:391
  80.3 0.8 copy-done.5
  81.1 3.4 %face.3 = f32[4,256,512]{2,1,0:T(8,128)} custom-call(s32[1]{0:T(128)} %bitcast.layer_ref, f32[256,512]{1,0:T(8,128)} %get-tuple-element.24.part, f32[4,256,512]{2,1,0:T(8,128)} %get-tuple-element.17.r, f32[256,512]{1,0:T(8,128)} %copy-done.5, f32[4,256,512]{2,1,0:T(8,128)} %face.2.old), custom_call_target="tpu_custom_call", output_to_operand_aliasing={{}: (4, {})} | custom-call | flops 393216 | bytes 2097152 | tf_op jit(solution)/shard_map/face/pallas_call | solution.py:391
  (23 shorter events, 0.2 us)
Async XLA Ops:
  2.4 16.4 %collective-permute-start = (f32[256,512]{1,0:T(8,128)S(1)}, f32[256,512]{1,0:T(8,128)S(1)}, u32[]{:S(2)}, u32[]{:S(2)}) collective-permute-start(f32[256,512]{1,0:T(8,128)S(1)} %get-tuple-element.31), channel_id=1, source_target_pairs={{8,16},{16,8},{24,1},{1,24},{9,17},{17,9},{25,2},{2,25},{10,18},{1... | collective-permute-start | bytes 1572872 | tf_op jit(solution)/shard_map/ppermute | solution.py:289
  6.1 12.7 %collective-permute-start.1 = (f32[256,512]{1,0:T(8,128)S(1)}, f32[256,512]{1,0:T(8,128)S(1)}, u32[]{:S(2)}, u32[]{:S(2)}) collective-permute-start(f32[256,512]{1,0:T(8,128)S(1)} %get-tuple-element.30), channel_id=1, source_target_pairs={{0,8},{8,0},{16,24},{24,16},{1,9},{9,1},{17,25},{25,17},{2,10},{10... | collective-permute-start | bytes 1572872 | tf_op jit(solution)/shard_map/ppermute | solution.py:289
  20.7 11.2 %copy-start.3 = (f32[256,512]{1,0:T(8,128)}, f32[256,512]{1,0:T(8,128)S(1)}, u32[]{:S(2)}) copy-start(f32[256,512]{1,0:T(8,128)S(1)} %get-tuple-element.34.on) | copy-start | bytes 1572868
  20.7 11.2 %copy-start.4 = (f32[256,512]{1,0:T(8,128)}, f32[256,512]{1,0:T(8,128)S(1)}, u32[]{:S(2)}) copy-start(f32[256,512]{1,0:T(8,128)S(1)} %get-tuple-element.35.off) | copy-start | bytes 1572868
  20.7 17.2 %collective-permute-start.2 = (f32[256,512]{1,0:T(8,128)S(1)}, f32[256,512]{1,0:T(8,128)S(1)}, u32[]{:S(2)}, u32[]{:S(2)}) collective-permute-start(f32[256,512]{1,0:T(8,128)S(1)} %get-tuple-element.35.off), channel_id=1, source_target_pairs={{8,16},{16,8},{24,1},{1,24},{9,17},{17,9},{25,2},{2,25},{10,18},{1... | collective-permute-start | bytes 1572872 | tf_op jit(solution)/shard_map/ppermute | solution.py:289
  24.1 13.8 %collective-permute-start.3 = (f32[256,512]{1,0:T(8,128)S(1)}, f32[256,512]{1,0:T(8,128)S(1)}, u32[]{:S(2)}, u32[]{:S(2)}) collective-permute-start(f32[256,512]{1,0:T(8,128)S(1)} %get-tuple-element.34.on), channel_id=1, source_target_pairs={{0,8},{8,0},{16,24},{24,16},{1,9},{9,1},{17,25},{25,17},{2,10},{10... | collective-permute-start | bytes 1572872 | tf_op jit(solution)/shard_map/ppermute | solution.py:289
  27.8 15.4 %all-to-all-start = ((f32[4,112,256]{2,1,0:T(8,128)}), f32[4,112,256]{2,1,0:T(8,128)}, u32[]{:S(2)}, u32[]{:S(2)}) async-start(f32[4,112,256]{2,1,0:T(8,128)} %restrict.1), calls=%async_computation | async-start | bytes 917504 | tf_op jit(solution)/shard_map/all_to_all | solution.py:315
  31.9 6.0 %copy-start = (f32[4,256,512]{2,1,0:T(8,128)S(1)}, f32[4,256,512]{2,1,0:T(8,128)}, u32[]{:S(2)}) copy-start(f32[4,256,512]{2,1,0:T(8,128)} %get-tuple-element.17.r) | copy-start | bytes 6291460
  39.5 30.0 %copy-start.1 = (f32[256,512]{1,0:T(8,128)}, f32[256,512]{1,0:T(8,128)S(1)}, u32[]{:S(2)}) copy-start(f32[256,512]{1,0:T(8,128)S(1)} %get-tuple-element.33.off) | copy-start | bytes 1572868
  39.5 30.0 %copy-start.2 = (f32[256,512]{1,0:T(8,128)}, f32[256,512]{1,0:T(8,128)S(1)}, u32[]{:S(2)}) copy-start(f32[256,512]{1,0:T(8,128)S(1)} %get-tuple-element.32.on) | copy-start | bytes 1572868
  39.5 36.6 %collective-permute-start.5 = (f32[256,512]{1,0:T(8,128)S(1)}, f32[256,512]{1,0:T(8,128)S(1)}, u32[]{:S(2)}, u32[]{:S(2)}) collective-permute-start(f32[256,512]{1,0:T(8,128)S(1)} %get-tuple-element.32.on), channel_id=1, source_target_pairs={{0,8},{8,0},{16,24},{24,16},{1,9},{9,1},{17,25},{25,17},{2,10},{10... | collective-permute-start | bytes 1572872 | tf_op jit(solution)/shard_map/ppermute | solution.py:289
  39.7 40.5 %collective-permute-start.4 = (f32[256,512]{1,0:T(8,128)S(1)}, f32[256,512]{1,0:T(8,128)S(1)}, u32[]{:S(2)}, u32[]{:S(2)}) collective-permute-start(f32[256,512]{1,0:T(8,128)S(1)} %get-tuple-element.33.off), channel_id=1, source_target_pairs={{8,16},{16,8},{24,1},{1,24},{9,17},{17,9},{25,2},{2,25},{10,18},{1... | collective-permute-start | bytes 1572872 | tf_op jit(solution)/shard_map/ppermute | solution.py:289
  45.3 18.2 %collective-permute-start.6 = (f32[2,3,40,256]{3,2,1,0:T(8,128)}, f32[2,3,40,256]{3,2,1,0:T(8,128)S(1)}, u32[]{:S(2)}, u32[]{:S(2)}) collective-permute-start(f32[2,3,40,256]{3,2,1,0:T(8,128)} %get-tuple-element.28), channel_id=1, source_target_pairs={{0,1},{1,2},{2,3},{3,4},{4,5},{5,6},{6,7},{8,9},{9,10},{10,11},{11... | collective-permute-start | bytes 737288 | tf_op jit(solution)/shard_map/ppermute | solution.py:343
  48.7 14.9 %collective-permute-start.7 = (f32[2,3,40,256]{3,2,1,0:T(8,128)}, f32[2,3,40,256]{3,2,1,0:T(8,128)S(1)}, u32[]{:S(2)}, u32[]{:S(2)}) collective-permute-start(f32[2,3,40,256]{3,2,1,0:T(8,128)} %get-tuple-element.29), channel_id=1, source_target_pairs={{1,0},{2,1},{3,2},{4,3},{5,4},{6,5},{7,6},{9,8},{10,9},{11,10},{12... | collective-permute-start | bytes 737288 | tf_op jit(solution)/shard_map/ppermute | solution.py:344
  63.6 0.7 copy-start.7
  63.6 0.8 copy-start.8
  76.0 0.8 copy-start.6
  80.3 0.8 copy-start.5

commit v2 on v1

--- a/solution.py
+++ b/solution.py
@@ -11,7 +11,8 @@
 HALO = SWEEPS - 1
 ROWPAD = 4
 STRIP = 32
-LIMIT = 56 * 1024 * 1024
+FACE_TILES = 4
+LIMIT = 12 * 1024 * 1024
 
 
 def whole():
@@ -134,9 +135,20 @@
         copy.wait()
 
 
-def face_kernel(layer_ref, part, r, halo, old, out):
-    del layer_ref, old
-    out[0] = jnp.exp(part[...] + r[0] * halo[...])
+def face_kernel(source, layer_ref, part, r, halo, old, out, done, sems):
+    del old
+    rows = part.shape[0]
+    tile = rows // FACE_TILES
+    copies = []
+    for k in range(FACE_TILES):
+        at = pl.ds(k * tile, tile)
+        done[at, :] = jnp.exp(part[at, :] + r[source, at, :] * halo[at, :])
+        copies.append(
+            pltpu.make_async_copy(done.at[at], out.at[layer_ref[0], at], sems.at[k])
+        )
+        copies[-1].start()
+    for copy in copies:
+        copy.wait()
 
 
 def restrict_kernel(place_ref, noise, kappa, blocks, pair, fine_rows):
@@ -223,8 +235,7 @@
         prepare(k, below, k)
         prepare(HALO + layers + k, above, k)
 
-    @pl.loop(0, layers)
-    def _(k):
+    for k in range(layers):
         prepare(HALO + k, own, k)
 
     sub = lax.broadcasted_iota(jnp.int32, (span, cols), 0)
@@ -241,14 +252,10 @@
         target = odd if step % 2 else even
         if step < SWEEPS - 1:
 
-            @pl.loop(step, total - step)
-            def _(layer):
+            for layer in range(step, total - step):
                 target[layer] = sweep(source, layer)
-
         else:
-
-            @pl.loop(HALO, HALO + layers)
-            def _(layer):
+            for layer in range(HALO, HALO + layers):
                 value = jnp.exp(sweep(source, layer))
                 out[layer - HALO] = value[ROWPAD : ROWPAD + own_rows]
 
@@ -295,7 +302,8 @@
 
     index_off = flip * (depth - 1)
     index_on = (1 - flip) * (depth - 1)
-    halo_off, halo_on = swap(face(index_off), face(index_on))
+    first_off, index_on_later = lax.optimization_barrier((face(index_off), index_on))
+    halo_off, halo_on = swap(first_off, face(index_on_later))
 
     span = own_rows + 2 * ROWPAD
     block_rows = (depth // 2) * span + layers * ROWPAD
@@ -324,6 +332,10 @@
         cost_estimate=cost(cells * depth, 16, 5),
     )(flip1, noise, kappa)
 
+    off = part_off + r[0] * halo_off
+    on = part_on + r[depth - 1] * halo_on
+    off, on, blocks = lax.optimization_barrier((off, on, blocks))
+    halo_off, halo_on = swap(off, on)
     edge = jax.ShapeDtypeStruct((2, HALO, span, half_cols), jnp.float32)
     own, up, down = pl.pallas_call(
         frame_kernel,
@@ -343,9 +355,6 @@
     below = lax.ppermute(up, "slab", ahead)
     above = lax.ppermute(down, "slab", back)
 
-    off = part_off + r[0] * halo_off
-    on = part_on + r[depth - 1] * halo_on
-    halo_off, halo_on = swap(off, on)
     part_off, part_on, mid = pl.pallas_call(
         middle_kernel,
         name="middle",
@@ -358,6 +367,7 @@
 
     off = part_off + r[0] * halo_off
     on = part_on + r[depth - 1] * halo_on
+    off, on, below, above = lax.optimization_barrier((off, on, below, above))
     halo_off, halo_on = swap(off, on)
     part_off, part_on, fine = pl.pallas_call(
         last_kernel,
@@ -385,24 +395,17 @@
         cost_estimate=cost(layers * own_rows * half_cols, 80, 6),
     )(own, below, above)
 
-    tile = rows // 4
-
     def finish(fine, layer, source, part, halo):
         return pl.pallas_call(
-            face_kernel,
+            functools.partial(face_kernel, source),
             name="face",
             out_shape=stack,
-            grid_spec=pltpu.PrefetchScalarGridSpec(
-                num_scalar_prefetch=1,
-                grid=(rows // tile,),
-                in_specs=[
-                    pl.BlockSpec((tile, cols), lambda i, at: (i, 0)),
-                    pl.BlockSpec((1, tile, cols), lambda i, at: (source, i, 0)),
-                    pl.BlockSpec((tile, cols), lambda i, at: (i, 0)),
-                    anywhere(),
-                ],
-                out_specs=pl.BlockSpec((1, tile, cols), lambda i, at: (at[0], i, 0)),
-            ),
+            in_specs=[scalar(), whole(), whole(), whole(), anywhere()],
+            out_specs=anywhere(),
+            scratch_shapes=[
+                pltpu.VMEM((rows, cols), jnp.float32),
+                pltpu.SemaphoreType.DMA((FACE_TILES,)),
+            ],
             input_output_aliases={4: 0},
             compiler_params=params,
             cost_estimate=cost(cells, 3, 4, cells),

time: 85.9 us -> 67 us (0.78)
  Pallas kernels: 36.4 us -> 12.3 us
  local copies, waits for them, and re-layouts: 2.38 us -> 8.31 us
    ppermute x6, waiting for transfers between devices: 5.86 us -> 12.3 us  [swap(): return (lax.ppermute(off, axes, far), lax.ppermute(on, axes, near))]
    ppermute x1, waiting for transfers between devices: 12.9 us -> 6.95 us  [body(): below = lax.ppermute(up, 'slab', ahead)]
    unnamed x18, local copies, waits for them, and re-layouts: 2.38 us -> 8.31 us
    pallas_call x2, Pallas kernels: 6.87 us -> 1.72 us  [finish(): pl.pallas_call(functools.partial(face_kernel, source), name='face', out_s...]
    pallas_call x1, Pallas kernels: 6.78 us -> 2.1 us  [body(): pl.pallas_call(first_kernel, name='first', out_shape=(stack, stack, plane...]
    pallas_call x1, Pallas kernels: 5.97 us -> 1.69 us  [body(): pl.pallas_call(middle_kernel, name='middle', out_shape=(plane, plane, inn...]
    pallas_call x1, Pallas kernels: 6.56 us -> 2.82 us  [body(): pl.pallas_call(last_kernel, name='last', out_shape=(plane, plane, stack),...]
    pallas_call x1, Pallas kernels: 5.1 us -> 1.59 us  [body(): pl.pallas_call(coarse_kernel, name='coarse', out_shape=jax.ShapeDtypeStru...]
  transfers between devices with their start and end apart: 9 -> 9, of which waited for: 2 -> 4; matrix products, arithmetic and copies ran while one was open for 2% -> 3% of each run, Pallas kernels for 39% -> 17%
where the time goes in v2:
time: 67 us; the launch traced here: 66 us
  starting transfers between devices  20.6 us (31%)
  waiting for transfers between devices  19.3 us (29%)
  Pallas kernels  12.3 us (18%)
  local copies, waits for them, and re-layouts  8.31 us (12%)
  other arithmetic  4.66 us (7%)
  between operations  0.83 us (1%)
    ppermute x6, waiting for transfers between devices, swap(): return (lax.ppermute(off, axes, far), lax.ppermute(on, axes, near))  12.3 us
    ppermute x6, starting transfers between devices, swap(): return (lax.ppermute(off, axes, far), lax.ppermute(on, axes, near))  10.6 us
    unnamed x18, local copies, waits for them, and re-layouts  8.31 us
    ppermute x1, waiting for transfers between devices, body(): below = lax.ppermute(up, 'slab', ahead)  6.95 us
    all_to_all x1, starting transfers between devices, body(): lax.all_to_all(blocks, 'grp', split_axis=0, concat_axis=0, tiled=True)  4.53 us
    ppermute x1, starting transfers between devices, body(): below = lax.ppermute(up, 'slab', ahead)  3.53 us
    pallas_call x1, Pallas kernels, body(): pl.pallas_call(last_kernel, name='last', out_shape=(plane, plane, stack),...  2.82 us
    div x2, other arithmetic, face(): return n / (6.0 + k)  2.74 us
  transfers between devices with their start and end apart: 9, of which 4 were waited for; matrix products, arithmetic and copies ran while one was open for 3% of the time, Pallas kernels for 17%

profile of v2, /device:TPU:13, one launch (start us, length us, event | category | flops | bytes accessed | tf_op | source)
XLA Modules:
  0.0 66.0 jit_solution(15261869934709478921)
XLA Ops:
  0.7 1.4 %divide_bitcast_fusion.1 = f32[256,512]{1,0:T(8,128)S(1)} fusion(f32[1,1,4,256,512]{4,3,2,1,0:T(8,128)} %param.4, s32[]{:T(128)S(6)} %select_n.17, f32[1,1,4,256,512]{4,3,2,1,0:T(8,128)} %param.3), kind=kLoop, calls=%fused_computation.9 | loop fusion | flops 262144 | bytes 1572868 | tf_op jit(solution)/shard_map/div | solution.py:301
  2.1 1.3 %divide_bitcast_fusion = f32[256,512]{1,0:T(8,128)S(1)} fusion(f32[1,1,4,256,512]{4,3,2,1,0:T(8,128)} %param.4, s32[]{:T(128)S(6)} %select_n.18, f32[1,1,4,256,512]{4,3,2,1,0:T(8,128)} %param.3), kind=kLoop, calls=%fused_computation.8 | loop fusion | flops 262144 | bytes 1572868 | tf_op jit(solution)/shard_map/div | solution.py:301
  4.2 3.0 %collective-permute-start = (f32[256,512]{1,0:T(8,128)S(1)}, f32[256,512]{1,0:T(8,128)}, u32[]{:S(2)}, u32[]{:S(2)}) collective-permute-start(f32[256,512]{1,0:T(8,128)S(1)} %divide_bitcast_fusion.1), channel_id=1, source_target_pairs={{8,16},{16,8},{24,1},{1,24},{9,17},{17,9},{25,2},{2,25},{10,18},{1... | collective-permute-start | bytes 1572872 | tf_op jit(solution)/shard_map/ppermute | solution.py:296
  7.2 1.3 %restrict.1 = f32[4,112,256]{2,1,0:T(8,128)} custom-call(s32[1]{0:T(128)} %bitcast.8.place_ref, f32[4,256,512]{2,1,0:T(8,128)S(1)} %bitcast.25, f32[8,32,256]{2,1,0:T(8,128)S(1)} %copy-done.6), custom_call_target="tpu_custom_call" | custom-call | flops 4194304 | bytes 2097152 | tf_op jit(solution)/shard_map/restrict/pallas_call | solution.py:310
  8.6 4.5 %all-to-all-start = ((f32[4,112,256]{2,1,0:T(8,128)}), f32[4,112,256]{2,1,0:T(8,128)}, u32[]{:S(2)}, u32[]{:S(2)}) async-start(f32[4,112,256]{2,1,0:T(8,128)} %restrict.1), calls=%async_computation | async-start | bytes 917504 | tf_op jit(solution)/shard_map/all_to_all | solution.py:323
  13.1 1.6 %copy-done.1 = f32[1,1,4,256,512]{4,3,2,1,0:T(8,128)S(1)} copy-done((f32[1,1,4,256,512]{4,3,2,1,0:T(8,128)S(1)}, f32[1,1,4,256,512]{4,3,2,1,0:T(8,128)}, u32[]{:S(2)}) %copy-start.1) | copy-done | bytes 2097176
  14.7 1.6 %copy-done.5 = f32[1,1,4,256,512]{4,3,2,1,0:T(8,128)S(1)} copy-done((f32[1,1,4,256,512]{4,3,2,1,0:T(8,128)S(1)}, f32[1,1,4,256,512]{4,3,2,1,0:T(8,128)}, u32[]{:S(2)}) %copy-start.5) | copy-done | bytes 2097176
  16.3 2.1 %first.1 = (f32[4,256,512]{2,1,0:T(8,128)S(1)}, f32[4,256,512]{2,1,0:T(8,128)S(1)}, f32[256,512]{1,0:T(8,128)S(1)}, f32[256,512]{1,0:T(8,128)S(1)}, f32[2,256,512]{2,1,0:T(8,128)S(1)}) custom-call(s32[1]{0:T(128)} %bitcast.1.flip_ref, f32[4,256,512]{2,1,0:T(8,128)S(1)} %bitcast.26, f32[4,256,512]{2,1,0:T(8,128)S(1)} %bitcast.27), custom_call_target="tpu_custom_call" | custom-call | flops 8388608 | bytes 10485760 | tf_op jit(solution)/shard_map/first/pallas_call | solution.py:325
  18.4 1.3 %copy-done.2 = f32[4,256,512]{2,1,0:T(8,128)} copy-done((f32[4,256,512]{2,1,0:T(8,128)}, f32[4,256,512]{2,1,0:T(8,128)S(1)}, u32[]{:S(2)}) %copy-start.2) | copy-done | bytes 2097176
  20.7 2.1 %collective-permute-done = f32[256,512]{1,0:T(8,128)} collective-permute-done((f32[256,512]{1,0:T(8,128)S(1)}, f32[256,512]{1,0:T(8,128)}, u32[]{:S(2)}, u32[]{:S(2)}) %collective-permute-start) | collective-permute-done | bytes 524320 | tf_op jit(solution)/shard_map/ppermute | solution.py:296
  22.8 1.5 %fusion = (f32[256,512]{1,0:T(8,128)S(1)}, f32[256,512]{1,0:T(8,128)S(1)}) fusion(f32[256,512]{1,0:T(8,128)S(1)} %get-tuple-element.28, f32[256,512]{1,0:T(8,128)} %collective-permute-done.1, f32[4,256,512]{2,1,0:T(8,128)S(1)} %get-tuple-element.26.r, f32[256,512]{1,0:T(8,128)S(1)} %get-tuple-element.25, f32[256,512]{1,0:T(8,128)} %collective-permute-done), kind=kLoop, calls=%fused_computation.2 | loop fusion | flops 524288 | bytes 4194304 | tf_op jit(solution)/shard_map/add | solution.py:336
  24.4 3.9 %collective-permute-start.2 = (f32[256,512]{1,0:T(8,128)S(1)}, f32[256,512]{1,0:T(8,128)S(1)}, u32[]{:S(2)}, u32[]{:S(2)}) collective-permute-start(f32[256,512]{1,0:T(8,128)S(1)} %get-tuple-element.30.off), channel_id=1, source_target_pairs={{8,16},{16,8},{24,1},{1,24},{9,17},{17,9},{25,2},{2,25},{10,18},{1... | collective-permute-start | bytes 1572872 | tf_op jit(solution)/shard_map/ppermute | solution.py:296
  28.4 1.1 %frame.1 = (f32[2,8,40,256]{3,2,1,0:T(8,128)S(1)}, f32[2,3,40,256]{3,2,1,0:T(8,128)S(1)}, f32[2,3,40,256]{3,2,1,0:T(8,128)S(1)}) custom-call(s32[1]{0:T(128)} %bitcast.8.place_ref, f32[4,112,256]{2,1,0:T(8,128)} %all-to-all-done.blocks, f32[8,32,256]{2,1,0:T(8,128)S(1)} %copy-done.6), custom_call_target="tpu_custom_call" | custom-call | flops 327680 | bytes 1638400 | tf_op jit(solution)/shard_map/frame/pallas_call | solution.py:340
  29.5 3.5 %collective-permute-start.4 = (f32[2,3,40,256]{3,2,1,0:T(8,128)S(1)}, f32[2,3,40,256]{3,2,1,0:T(8,128)S(1)}, u32[]{:S(2)}, u32[]{:S(2)}) collective-permute-start(f32[2,3,40,256]{3,2,1,0:T(8,128)S(1)} %get-tuple-element.37), channel_id=1, source_target_pairs={{0,1},{1,2},{2,3},{3,4},{4,5},{5,6},{6,7},{8,9},{9,10},{10,11},{11... | collective-permute-start | bytes 737288 | tf_op jit(solution)/shard_map/ppermute | solution.py:355
  33.0 1.9 %collective-permute-start.5 = (f32[2,3,40,256]{3,2,1,0:T(8,128)S(1)}, f32[2,3,40,256]{3,2,1,0:T(8,128)S(1)}, u32[]{:S(2)}, u32[]{:S(2)}) collective-permute-start(f32[2,3,40,256]{3,2,1,0:T(8,128)S(1)} %get-tuple-element.38), channel_id=1, source_target_pairs={{1,0},{2,1},{3,2},{4,3},{5,4},{6,5},{7,6},{9,8},{10,9},{11,10},{12... | collective-permute-start | bytes 737288 | tf_op jit(solution)/shard_map/ppermute | solution.py:356
  35.0 1.6 %copy-done.3 = f32[4,256,512]{2,1,0:T(8,128)S(1)} copy-done((f32[4,256,512]{2,1,0:T(8,128)S(1)}, f32[4,256,512]{2,1,0:T(8,128)}, u32[]{:S(2)}) %copy-start.3) | copy-done | bytes 2097176
  36.6 1.2 %copy-done.8 = f32[2,256,512]{2,1,0:T(8,128)S(1)} copy-done((f32[2,256,512]{2,1,0:T(8,128)S(1)}, f32[2,256,512]{2,1,0:T(8,128)}, u32[]{:S(2)}) %copy-start.8) | copy-done | bytes 1048600
  37.8 1.7 %middle.1 = (f32[256,512]{1,0:T(8,128)S(1)}, f32[256,512]{1,0:T(8,128)S(1)}, f32[2,256,512]{2,1,0:T(8,128)S(1)}) custom-call(f32[256,512]{1,0:T(8,128)S(1)} %get-tuple-element.30.off, f32[256,512]{1,0:T(8,128)S(1)} %get-tuple-element.31.on, f32[2,256,512]{2,1,0:T(8,128)S(1)} %copy-done.8, f32[4,256,512]{2,1,0:T(8,128)S(1)} %copy-done.3, ...), custom_call_target="tpu_custom_call" | custom-call | flops 6291456 | bytes 8388608 | tf_op jit(solution)/shard_map/middle/pallas_call | solution.py:358
  39.5 1.6 %collective-permute-done.2 = f32[256,512]{1,0:T(8,128)S(1)} collective-permute-done((f32[256,512]{1,0:T(8,128)S(1)}, f32[256,512]{1,0:T(8,128)S(1)}, u32[]{:S(2)}, u32[]{:S(2)}) %collective-permute-start.2) | collective-permute-done | bytes 524320 | tf_op jit(solution)/shard_map/ppermute | solution.py:296
  41.5 6.9 %collective-permute-done.4.below = f32[2,3,40,256]{3,2,1,0:T(8,128)S(1)} collective-permute-done((f32[2,3,40,256]{3,2,1,0:T(8,128)S(1)}, f32[2,3,40,256]{3,2,1,0:T(8,128)S(1)}, u32[]{:S(2)}, u32[]{:S(2)}) %collective-permute-start.4) | collective-permute-done | bytes 245792 | tf_op jit(solution)/shard_map/ppermute | solution.py:355
  49.3 2.0 %collective-permute-start.6 = (f32[256,512]{1,0:T(8,128)S(1)}, f32[256,512]{1,0:T(8,128)S(1)}, u32[]{:S(2)}, u32[]{:S(2)}) collective-permute-start(f32[256,512]{1,0:T(8,128)S(1)} %get-tuple-element.39.off), channel_id=1, source_target_pairs={{8,16},{16,8},{24,1},{1,24},{9,17},{17,9},{25,2},{2,25},{10,18},{1... | collective-permute-start | bytes 1572872 | tf_op jit(solution)/shard_map/ppermute | solution.py:296
  51.3 1.6 %coarse.1 = f32[8,32,256]{2,1,0:T(8,128)} custom-call(f32[2,8,40,256]{3,2,1,0:T(8,128)S(1)} %get-tuple-element.45.own, f32[2,3,40,256]{3,2,1,0:T(8,128)S(1)} %collective-permute-done.4.below, f32[2,3,40,256]{3,2,1,0:T(8,128)S(1)} %collective-permute-done.5.above), custom_call_target="tpu_custom_call" | custom-call | flops 5242880 | bytes 1572864 | tf_op jit(solution)/shard_map/coarse/pallas_call | solution.py:387
  52.9 2.8 %last.1 = (f32[256,512]{1,0:T(8,128)S(1)}, f32[256,512]{1,0:T(8,128)S(1)}, f32[4,256,512]{2,1,0:T(8,128)}) custom-call(s32[1]{0:T(128)} %bitcast.1.flip_ref, f32[256,512]{1,0:T(8,128)S(1)} %get-tuple-element.39.off, f32[256,512]{1,0:T(8,128)S(1)} %get-tuple-element.40.on, f32[2,256,512]{2,1,0:T(8,128)S(1)} %get-tuple-element.41.old_mid, ...), custom_call_target="tpu_custom_call" | custom-call | flops 7340032 | bytes 8388608 | tf_op jit(solution)/shard_map/last/pallas_call | solution.py:372
  56.6 8.6 %collective-permute-done.6.halo = f32[256,512]{1,0:T(8,128)S(1)} collective-permute-done((f32[256,512]{1,0:T(8,128)S(1)}, f32[256,512]{1,0:T(8,128)S(1)}, u32[]{:S(2)}, u32[]{:S(2)}) %collective-permute-start.6) | collective-permute-done | bytes 524320 | tf_op jit(solution)/shard_map/ppermute | solution.py:296
  (24 shorter events, 4.8 us)
Async XLA Ops:
  0.6 6.6 %copy-start = (f32[1,1,4,256,512]{4,3,2,1,0:T(8,128)S(1)}, f32[1,1,4,256,512]{4,3,2,1,0:T(8,128)}, u32[]{:S(2)}) copy-start(f32[1,1,4,256,512]{4,3,2,1,0:T(8,128)} %param.3) | copy-start | bytes 6291460
  0.6 6.6 %copy-start.6 = (f32[8,32,256]{2,1,0:T(8,128)S(1)}, f32[8,32,256]{2,1,0:T(8,128)}, u32[]{:S(2)}) copy-start(f32[8,32,256]{2,1,0:T(8,128)} %kappa.3) | copy-start | bytes 786436
  3.4 17.3 %collective-permute-start.1 = (f32[256,512]{1,0:T(8,128)S(1)}, f32[256,512]{1,0:T(8,128)}, u32[]{:S(2)}, u32[]{:S(2)}) collective-permute-start(f32[256,512]{1,0:T(8,128)S(1)} %divide_bitcast_fusion), channel_id=1, source_target_pairs={{0,8},{8,0},{16,24},{24,16},{1,9},{9,1},{17,25},{25,17},{2,10},{10... | collective-permute-start | bytes 1572872 | tf_op jit(solution)/shard_map/ppermute | solution.py:296
  4.2 18.7 %collective-permute-start = (f32[256,512]{1,0:T(8,128)S(1)}, f32[256,512]{1,0:T(8,128)}, u32[]{:S(2)}, u32[]{:S(2)}) collective-permute-start(f32[256,512]{1,0:T(8,128)S(1)} %divide_bitcast_fusion.1), channel_id=1, source_target_pairs={{8,16},{16,8},{24,1},{1,24},{9,17},{17,9},{25,2},{2,25},{10,18},{1... | collective-permute-start | bytes 1572872 | tf_op jit(solution)/shard_map/ppermute | solution.py:296
  8.6 15.8 %all-to-all-start = ((f32[4,112,256]{2,1,0:T(8,128)}), f32[4,112,256]{2,1,0:T(8,128)}, u32[]{:S(2)}, u32[]{:S(2)}) async-start(f32[4,112,256]{2,1,0:T(8,128)} %restrict.1), calls=%async_computation | async-start | bytes 917504 | tf_op jit(solution)/shard_map/all_to_all | solution.py:323
  13.1 1.6 %copy-start.1 = (f32[1,1,4,256,512]{4,3,2,1,0:T(8,128)S(1)}, f32[1,1,4,256,512]{4,3,2,1,0:T(8,128)}, u32[]{:S(2)}) copy-start(f32[1,1,4,256,512]{4,3,2,1,0:T(8,128)} %param.3) | copy-start | bytes 6291460
  14.7 1.6 %copy-start.5 = (f32[1,1,4,256,512]{4,3,2,1,0:T(8,128)S(1)}, f32[1,1,4,256,512]{4,3,2,1,0:T(8,128)}, u32[]{:S(2)}) copy-start(f32[1,1,4,256,512]{4,3,2,1,0:T(8,128)} %param.4) | copy-start | bytes 6291460
  18.4 1.3 %copy-start.2 = (f32[4,256,512]{2,1,0:T(8,128)}, f32[4,256,512]{2,1,0:T(8,128)S(1)}, u32[]{:S(2)}) copy-start(f32[4,256,512]{2,1,0:T(8,128)S(1)} %get-tuple-element.33.b) | copy-start | bytes 6291460
  19.7 1.0 %copy-start.7 = (f32[2,256,512]{2,1,0:T(8,128)}, f32[2,256,512]{2,1,0:T(8,128)S(1)}, u32[]{:S(2)}) copy-start(f32[2,256,512]{2,1,0:T(8,128)S(1)} %get-tuple-element.32.old_mid) | copy-start | bytes 3145732
  24.4 16.7 %collective-permute-start.2 = (f32[256,512]{1,0:T(8,128)S(1)}, f32[256,512]{1,0:T(8,128)S(1)}, u32[]{:S(2)}, u32[]{:S(2)}) collective-permute-start(f32[256,512]{1,0:T(8,128)S(1)} %get-tuple-element.30.off), channel_id=1, source_target_pairs={{8,16},{16,8},{24,1},{1,24},{9,17},{17,9},{25,2},{2,25},{10,18},{1... | collective-permute-start | bytes 1572872 | tf_op jit(solution)/shard_map/ppermute | solution.py:296
  28.3 12.8 %collective-permute-start.3 = (f32[256,512]{1,0:T(8,128)S(1)}, f32[256,512]{1,0:T(8,128)S(1)}, u32[]{:S(2)}, u32[]{:S(2)}) collective-permute-start(f32[256,512]{1,0:T(8,128)S(1)} %get-tuple-element.31.on), channel_id=1, source_target_pairs={{0,8},{8,0},{16,24},{24,16},{1,9},{9,1},{17,25},{25,17},{2,10},{10... | collective-permute-start | bytes 1572872 | tf_op jit(solution)/shard_map/ppermute | solution.py:296
  29.5 18.9 %collective-permute-start.4 = (f32[2,3,40,256]{3,2,1,0:T(8,128)S(1)}, f32[2,3,40,256]{3,2,1,0:T(8,128)S(1)}, u32[]{:S(2)}, u32[]{:S(2)}) collective-permute-start(f32[2,3,40,256]{3,2,1,0:T(8,128)S(1)} %get-tuple-element.37), channel_id=1, source_target_pairs={{0,1},{1,2},{2,3},{3,4},{4,5},{5,6},{6,7},{8,9},{9,10},{10,11},{11... | collective-permute-start | bytes 737288 | tf_op jit(solution)/shard_map/ppermute | solution.py:355
  33.0 15.4 %collective-permute-start.5 = (f32[2,3,40,256]{3,2,1,0:T(8,128)S(1)}, f32[2,3,40,256]{3,2,1,0:T(8,128)S(1)}, u32[]{:S(2)}, u32[]{:S(2)}) collective-permute-start(f32[2,3,40,256]{3,2,1,0:T(8,128)S(1)} %get-tuple-element.38), channel_id=1, source_target_pairs={{1,0},{2,1},{3,2},{4,3},{5,4},{6,5},{7,6},{9,8},{10,9},{11,10},{12... | collective-permute-start | bytes 737288 | tf_op jit(solution)/shard_map/ppermute | solution.py:356
  35.0 1.6 %copy-start.3 = (f32[4,256,512]{2,1,0:T(8,128)S(1)}, f32[4,256,512]{2,1,0:T(8,128)}, u32[]{:S(2)}) copy-start(f32[4,256,512]{2,1,0:T(8,128)} %copy-done.2) | copy-start | bytes 6291460
  36.6 1.2 %copy-start.8 = (f32[2,256,512]{2,1,0:T(8,128)S(1)}, f32[2,256,512]{2,1,0:T(8,128)}, u32[]{:S(2)}) copy-start(f32[2,256,512]{2,1,0:T(8,128)} %copy-done.7) | copy-start | bytes 3145732
  41.1 11.8 %copy-start.4 = (f32[4,256,512]{2,1,0:T(8,128)S(1)}, f32[4,256,512]{2,1,0:T(8,128)}, u32[]{:S(2)}) copy-start(f32[4,256,512]{2,1,0:T(8,128)} %copy-done.2) | copy-start | bytes 6291460
  48.4 7.3 %collective-permute-start.7 = (f32[256,512]{1,0:T(8,128)S(1)}, f32[256,512]{1,0:T(8,128)S(1)}, u32[]{:S(2)}, u32[]{:S(2)}) collective-permute-start(f32[256,512]{1,0:T(8,128)S(1)} %get-tuple-element.40.on), channel_id=1, source_target_pairs={{0,8},{8,0},{16,24},{24,16},{1,9},{9,1},{17,25},{25,17},{2,10},{10... | collective-permute-start | bytes 1572872 | tf_op jit(solution)/shard_map/ppermute | solution.py:296
  49.3 15.9 %collective-permute-start.6 = (f32[256,512]{1,0:T(8,128)S(1)}, f32[256,512]{1,0:T(8,128)S(1)}, u32[]{:S(2)}, u32[]{:S(2)}) collective-permute-start(f32[256,512]{1,0:T(8,128)S(1)} %get-tuple-element.39.off), channel_id=1, source_target_pairs={{8,16},{16,8},{24,1},{1,24},{9,17},{17,9},{25,2},{2,25},{10,18},{1... | collective-permute-start | bytes 1572872 | tf_op jit(solution)/shard_map/ppermute | solution.py:296

commit v3 on v2

--- a/solution.py
+++ b/solution.py
@@ -11,7 +11,8 @@
 HALO = SWEEPS - 1
 ROWPAD = 4
 STRIP = 32
-FACE_TILES = 4
+FACE_TILES = 2
+PIECES = 2
 LIMIT = 12 * 1024 * 1024
 
 
@@ -28,6 +29,7 @@
 
 
 def cost(cells, ops, arrays, transcendentals=0):
+    return pl.CostEstimate(flops=5000000000, bytes_accessed=1000000, transcendentals=0)
     return pl.CostEstimate(
         flops=cells * ops, bytes_accessed=4 * cells * arrays, transcendentals=transcendentals
     )
@@ -106,8 +108,26 @@
     advance(field, b, r, rows, part_off, part_on, put)
 
 
-def middle_kernel(off, on, old_mid, b, r, part_off, part_on, mid):
+def meet_kernel(layer, start, part, halo, r, out):
+    rows = out.shape[0]
+    size = min(2 * STRIP, rows)
+    for k in range(rows // size):
+        at = pl.ds(k * size, size)
+        of = pl.ds(start + k * size, size)
+        out[at, :] = part[of, :] + r[layer, of, :] * halo[at, :]
+
+
+def joined(pieces, whole_ref):
+    rows = pieces[0].shape[0]
+    for k, piece in enumerate(pieces):
+        whole_ref[k * rows : (k + 1) * rows, :] = piece[...]
+
+
+def middle_kernel(*refs):
+    pieces = refs[:PIECES]
+    on, old_mid, b, r, part_off, part_on, mid, off = refs[PIECES:]
     depth, rows, _ = b.shape
+    joined(pieces, off)
     field = [loader(off)] + [loader(old_mid, m) for m in range(depth - 2)] + [loader(on)]
 
     def put(m, at, value):
@@ -116,8 +136,11 @@
     advance(field, b, r, rows, part_off, part_on, put)
 
 
-def last_kernel(flip_ref, off, on, old_mid, b, r, part_off, part_on, out, mid, sems):
+def last_kernel(flip_ref, *refs):
+    pieces = refs[:PIECES]
+    on, old_mid, b, r, part_off, part_on, out, mid, sems, off = refs[PIECES:]
     depth, rows, _ = b.shape
+    joined(pieces, off)
     flip = flip_ref[0]
     field = [loader(off)] + [loader(old_mid, m) for m in range(depth - 2)] + [loader(on)]
 
@@ -135,38 +158,41 @@
         copy.wait()
 
 
-def face_kernel(source, layer_ref, part, r, halo, old, out, done, sems):
+def face_kernel(source, start, layer_ref, part, r, halo, old, out, done, sems):
     del old
-    rows = part.shape[0]
-    tile = rows // FACE_TILES
+    tile = halo.shape[0] // FACE_TILES
     copies = []
     for k in range(FACE_TILES):
         at = pl.ds(k * tile, tile)
-        done[at, :] = jnp.exp(part[at, :] + r[source, at, :] * halo[at, :])
+        of = pl.ds(start + k * tile, tile)
+        done[at, :] = jnp.exp(part[of, :] + r[source, of, :] * halo[at, :])
         copies.append(
-            pltpu.make_async_copy(done.at[at], out.at[layer_ref[0], at], sems.at[k])
+            pltpu.make_async_copy(done.at[at], out.at[layer_ref[0], of], sems.at[k])
         )
         copies[-1].start()
     for copy in copies:
         copy.wait()
 
 
-def restrict_kernel(place_ref, noise, kappa, blocks, pair, fine_rows):
+def restrict_kernel(place_ref, noise, kappa, far, near, own, pair, fine_rows, padded):
     depth, rows, cols = noise.shape
-    groups = blocks.shape[0]
     half_rows, half_cols = rows // 2, cols // 2
-    own_rows = half_rows // groups
+    own_rows = kappa.shape[1]
     span = own_rows + 2 * ROWPAD
+    part = (depth // 2) * span
     position = place_ref[0]
     src = lax.broadcasted_iota(jnp.int32, (cols, half_cols), 0)
     dst = lax.broadcasted_iota(jnp.int32, (cols, half_cols), 1)
     fold = jnp.where(src // 2 == dst, 0.125, 0.0).astype(jnp.bfloat16)
-    zero = jnp.zeros((8, half_cols), jnp.float32)
+    padded[...] = jnp.zeros_like(padded)
+    flip1 = 1 - 2 * (position % 2)
+    other = position + flip1
+    across = jnp.where(position < 2, position + 2, position - 2)
+    beyond = across + flip1
     for layer in range(depth // 2):
         pair[...] = noise[2 * layer] + noise[2 * layer + 1]
-        cut = cols // 128
         pieces = []
-        for c in range(cut):
+        for c in range(cols // 128):
             fine_rows[...] = pair[:, 128 * c : 128 * (c + 1)]
             pieces.append(
                 fine_rows[pl.ds(0, half_rows, stride=2), :]
@@ -179,46 +205,62 @@
         low = (rest - middle.astype(jnp.float32)).astype(jnp.bfloat16)
         dot = functools.partial(jnp.dot, preferred_element_type=jnp.float32)
         coarse = dot(low, fold) + dot(middle, fold) + dot(high, fold)
-        padded = jnp.concatenate([zero[:ROWPAD], coarse, zero[:ROWPAD]], axis=0)
-        for g in range(groups):
-            blocks[g, layer * span : (layer + 1) * span, :] = padded[
-                g * own_rows : g * own_rows + span
-            ]
-    base = (depth // 2) * span
-    layers = kappa.shape[0]
-    for layer in range(layers):
+        padded[ROWPAD : ROWPAD + half_rows, :] = coarse
+        at = slice(layer * span, (layer + 1) * span)
+
+        def rows_of(g):
+            return padded[pl.ds(pl.multiple_of(g * own_rows, 8), span), :]
+
+        own[at, :] = rows_of(position)
+        near[at, :] = rows_of(other)
+        far[at, :] = rows_of(across)
+        far[part + layer * span : part + (layer + 1) * span, :] = rows_of(beyond)
+    for layer in range(kappa.shape[0]):
         first = 1.0 / (1.5 + kappa[layer, 0:ROWPAD, :])
         last = 1.0 / (1.5 + kappa[layer, own_rows - ROWPAD : own_rows, :])
-        for g in range(groups):
-            sent = jnp.where(position + 1 == g, last, jnp.where(position - 1 == g, first, 0.0))
-            blocks[g, base + layer * ROWPAD : base + (layer + 1) * ROWPAD, :] = sent
-
-
-def frame_kernel(place_ref, blocks, kappa, own, up, down):
-    groups = blocks.shape[0]
+        at = layer * ROWPAD
+        far[2 * part + at : 2 * part + at + ROWPAD, :] = jnp.where(position < 2, last, first)
+        near[part + at : part + at + ROWPAD, :] = jnp.where(position % 2 == 0, last, first)
+
+
+def relay_kernel(near, arrived, out):
+    mine = near.shape[0]
+    carried = out.shape[0] - mine
+    out[0:mine, :] = near[...]
+    out[mine:, :] = arrived[arrived.shape[0] - carried :, :]
+
+
+def frame_kernel(place_ref, kept, across, near, kappa, own, up, down):
     layers, own_rows, _ = kappa.shape
     span = own_rows + 2 * ROWPAD
-    per = layers // groups
-    base = per * span
+    per = kept.shape[0] // span
+    part = per * span
+    edge = layers * ROWPAD
     position = place_ref[0]
+    flip1 = 1 - 2 * (position % 2)
+    beyond_chip = jnp.where(position < 2, position + 2, position - 2)
+    for k in range(per):
+        at = slice(k * span, (k + 1) * span)
+        own[0, per * position + k] = kept[at, :]
+        own[0, per * (position + flip1) + k] = near[at, :]
+        own[0, per * beyond_chip + k] = across[at, :]
+        relayed = slice(part + edge + k * span, part + edge + (k + 1) * span)
+        own[0, per * (beyond_chip + flip1) + k] = near[relayed, :]
     for layer in range(layers):
-        g, k = layer // per, layer % per
-        noise = blocks[g, k * span : (k + 1) * span, :]
-        at = slice(base + layer * ROWPAD, base + (layer + 1) * ROWPAD)
-        top = jnp.where(position > 0, blocks[jnp.maximum(position - 1, 0), at, :], 0.0)
-        bottom = jnp.where(
-            position < groups - 1, blocks[jnp.minimum(position + 1, groups - 1), at, :], 0.0
-        )
+        at = layer * ROWPAD
+        direct = near[part + at : part + at + ROWPAD, :]
+        passed = near[2 * part + edge + at : 2 * part + edge + at + ROWPAD, :]
+        inner = jnp.logical_or(position == 1, position == 2)
+        passed = jnp.where(inner, passed, 0.0)
+        even = position % 2 == 0
+        top = jnp.where(even, passed, direct)
+        bottom = jnp.where(even, direct, passed)
         middle = 1.0 / (1.5 + kappa[layer])
-        inverse = jnp.concatenate([top, middle, bottom], axis=0)
-        own[0, layer] = noise
-        own[1, layer] = inverse
-        if layer < HALO:
-            down[0, layer] = noise
-            down[1, layer] = inverse
-        if layer >= layers - HALO:
-            up[0, layer - layers + HALO] = noise
-            up[1, layer - layers + HALO] = inverse
+        own[1, layer] = jnp.concatenate([top, middle, bottom], axis=0)
+    for k in range(HALO):
+        for half in range(2):
+            down[half, k] = own[half, k]
+            up[half, k] = own[half, layers - HALO + k]
 
 
 def coarse_kernel(own, below, above, out, b, r, even, odd):
@@ -292,8 +334,13 @@
     stack = jax.ShapeDtypeStruct((depth, rows, cols), jnp.float32)
     inner = jax.ShapeDtypeStruct((depth - 2, rows, cols), jnp.float32)
 
-    def swap(off, on):
-        return lax.ppermute(off, axes, far), lax.ppermute(on, axes, near)
+    piece_rows = rows // PIECES
+
+    def send_far(piece):
+        return lax.ppermute(piece, axes, far)
+
+    def send_near(layer):
+        return lax.ppermute(layer, axes, near)
 
     def face(layer):
         n = lax.dynamic_index_in_dim(noise, layer, 0, keepdims=False)
@@ -302,25 +349,29 @@
 
     index_off = flip * (depth - 1)
     index_on = (1 - flip) * (depth - 1)
-    first_off, index_on_later = lax.optimization_barrier((face(index_off), index_on))
-    halo_off, halo_on = swap(first_off, face(index_on_later))
+    off, restrict_place = lax.optimization_barrier((face(index_off), place))
+    halo_off = [send_far(off[k * piece_rows : (k + 1) * piece_rows]) for k in range(PIECES)]
+    halo_on = send_near(face(index_on))
 
     span = own_rows + 2 * ROWPAD
-    block_rows = (depth // 2) * span + layers * ROWPAD
-    blocks = pl.pallas_call(
+    part = (depth // 2) * span
+    edge = layers * ROWPAD
+    flats = [jax.ShapeDtypeStruct((n, half_cols), jnp.float32) for n in (2 * part + edge, part + edge, part)]
+    far_send, near_send, kept = pl.pallas_call(
         restrict_kernel,
         name="restrict",
-        out_shape=jax.ShapeDtypeStruct((groups, block_rows, half_cols), jnp.float32),
+        out_shape=tuple(flats),
         in_specs=[scalar(), whole(), whole()],
-        out_specs=whole(),
+        out_specs=(whole(),) * 3,
         scratch_shapes=[
             pltpu.VMEM((rows, cols), jnp.float32),
             pltpu.VMEM((rows, 128), jnp.float32),
+            pltpu.VMEM((rows // 2 + 2 * ROWPAD, half_cols), jnp.float32),
         ],
         compiler_params=params,
         cost_estimate=cost(cells * depth, 8, 1),
-    )(place, noise, coarse_kappa)
-    blocks = lax.all_to_all(blocks, "grp", split_axis=0, concat_axis=0, tiled=True)
+    )(restrict_place, noise, coarse_kappa)
+    across = lax.ppermute(far_send, "grp", [(g, g ^ 2) for g in range(groups)])
 
     b, r, part_off, part_on, mid = pl.pallas_call(
         first_kernel,
@@ -332,24 +383,50 @@
         cost_estimate=cost(cells * depth, 16, 5),
     )(flip1, noise, kappa)
 
-    off = part_off + r[0] * halo_off
-    on = part_on + r[depth - 1] * halo_on
-    off, on, blocks = lax.optimization_barrier((off, on, blocks))
-    halo_off, halo_on = swap(off, on)
-    edge = jax.ShapeDtypeStruct((2, HALO, span, half_cols), jnp.float32)
+    def meet(layer, start, part, halo):
+        return pl.pallas_call(
+            functools.partial(meet_kernel, layer, start),
+            name="meet",
+            out_shape=jax.ShapeDtypeStruct(halo.shape, jnp.float32),
+            in_specs=[whole()] * 3,
+            out_specs=whole(),
+            compiler_params=params,
+            cost_estimate=cost(halo.size, 2, 4),
+        )(part, halo, r)
+
+    def meet_off(part, halos):
+        return [meet(0, k * piece_rows, part, halo) for k, halo in enumerate(halos)]
+
+    off = meet_off(part_off, halo_off)
+    on = meet(depth - 1, 0, part_on, halo_on)
+    halo_off = [send_far(piece) for piece in off]
+    halo_on = send_near(on)
+    across, off[-1] = lax.optimization_barrier((across, off[-1]))
+
+    relayed = pl.pallas_call(
+        relay_kernel,
+        name="relay",
+        out_shape=jax.ShapeDtypeStruct((2 * part + 2 * edge, half_cols), jnp.float32),
+        in_specs=[whole()] * 2,
+        out_specs=whole(),
+        compiler_params=params,
+        cost_estimate=cost(part * half_cols, 1, 4),
+    )(near_send, across)
+    near_got = lax.ppermute(relayed, "grp", [(g, g ^ 1) for g in range(groups)])
+    rim = jax.ShapeDtypeStruct((2, HALO, span, half_cols), jnp.float32)
     own, up, down = pl.pallas_call(
         frame_kernel,
         name="frame",
         out_shape=(
             jax.ShapeDtypeStruct((2, layers, span, half_cols), jnp.float32),
-            edge,
-            edge,
+            rim,
+            rim,
         ),
-        in_specs=[scalar(), whole(), whole()],
+        in_specs=[scalar()] + [whole()] * 4,
         out_specs=(whole(),) * 3,
         compiler_params=params,
         cost_estimate=cost(layers * span * half_cols, 4, 5),
-    )(place, blocks, coarse_kappa)
+    )(place, kept, across, near_got, coarse_kappa)
     ahead = [(i, i + 1) for i in range(slabs - 1)]
     back = [(i + 1, i) for i in range(slabs - 1)]
     below = lax.ppermute(up, "slab", ahead)
@@ -359,29 +436,31 @@
         middle_kernel,
         name="middle",
         out_shape=(plane, plane, inner),
-        in_specs=[whole()] * 5,
+        in_specs=[whole()] * (PIECES + 4),
         out_specs=(whole(),) * 3,
+        scratch_shapes=[pltpu.VMEM((rows, cols), jnp.float32)],
         compiler_params=params,
         cost_estimate=cost(cells * depth, 12, 4),
-    )(off, on, mid, b, r)
-
-    off = part_off + r[0] * halo_off
-    on = part_on + r[depth - 1] * halo_on
-    off, on, below, above = lax.optimization_barrier((off, on, below, above))
-    halo_off, halo_on = swap(off, on)
+    )(*off, on, mid, b, r)
+
+    off = meet_off(part_off, halo_off)
+    on = meet(depth - 1, 0, part_on, halo_on)
+    halo_off = [send_far(piece) for piece in off]
+    halo_on = send_near(on)
     part_off, part_on, fine = pl.pallas_call(
         last_kernel,
         name="last",
         out_shape=(plane, plane, stack),
-        in_specs=[scalar()] + [whole()] * 5,
+        in_specs=[scalar()] + [whole()] * (PIECES + 4),
         out_specs=(whole(), whole(), anywhere()),
         scratch_shapes=[
             pltpu.VMEM((depth - 2, rows, cols), jnp.float32),
             pltpu.SemaphoreType.DMA((depth - 2,)),
+            pltpu.VMEM((rows, cols), jnp.float32),
         ],
         compiler_params=params,
         cost_estimate=cost(cells * depth, 14, 4, cells * 2),
-    )(flip1, off, on, mid, b, r)
+    )(flip1, *off, on, mid, b, r)
 
     framed = (layers + 2 * HALO, span, half_cols)
     coarse = pl.pallas_call(
@@ -395,24 +474,25 @@
         cost_estimate=cost(layers * own_rows * half_cols, 80, 6),
     )(own, below, above)
 
-    def finish(fine, layer, source, part, halo):
+    def finish(fine, layer, source, start, part, halo):
         return pl.pallas_call(
-            functools.partial(face_kernel, source),
+            functools.partial(face_kernel, source, start),
             name="face",
             out_shape=stack,
             in_specs=[scalar(), whole(), whole(), whole(), anywhere()],
             out_specs=anywhere(),
             scratch_shapes=[
-                pltpu.VMEM((rows, cols), jnp.float32),
+                pltpu.VMEM(halo.shape, jnp.float32),
                 pltpu.SemaphoreType.DMA((FACE_TILES,)),
             ],
             input_output_aliases={4: 0},
             compiler_params=params,
-            cost_estimate=cost(cells, 3, 4, cells),
+            cost_estimate=cost(halo.size, 3, 4, halo.size),
         )(layer[None], part, r, halo, fine)
 
-    fine = finish(fine, index_on, depth - 1, part_on, halo_on)
-    fine = finish(fine, index_off, 0, part_off, halo_off)
+    fine = finish(fine, index_on, depth - 1, 0, part_on, halo_on)
+    for k, halo in enumerate(halo_off):
+        fine = finish(fine, index_off, 0, k * piece_rows, part_off, halo)
     return fine[None, None], coarse
 
 

time: 67 us -> 58.3 us (0.87)
  the two profiles are of different devices: /device:TPU:13 before, /device:TPU:17 now
where the time goes in v3:
time: 58.3 us; the launch traced here: 57.9 us
  starting transfers between devices  32.8 us (56%)
  Pallas kernels  12 us (21%)
  waiting for transfers between devices  10.3 us (18%)
  other arithmetic  1.9 us (3%)
  between operations  0.93 us (2%)
    ppermute x6, starting transfers between devices, send_far(): return lax.ppermute(piece, axes, far)  21.6 us
    ppermute x1, waiting for transfers between devices, body(): across = lax.ppermute(far_send, 'grp', [(g, g ^ 2) for g in range(groups)])  5.13 us
    ppermute x1, waiting for transfers between devices, body(): above = lax.ppermute(down, 'slab', back)  4.42 us
    ppermute x1, starting transfers between devices, body(): above = lax.ppermute(down, 'slab', back)  3.89 us
    pallas_call x1, Pallas kernels, body(): pl.pallas_call(last_kernel, name='last', out_shape=(plane, plane, stack),...  2.88 us
    ppermute x3, starting transfers between devices, send_near(): return lax.ppermute(layer, axes, near)  2.87 us
    pallas_call x3, Pallas kernels, finish(): pl.pallas_call(functools.partial(face_kernel, source, start), name='face'...  2.35 us
    ppermute x1, starting transfers between devices, body(): below = lax.ppermute(up, 'slab', ahead)  2.3 us
  transfers between devices with their start and end apart: 13, of which 3 were waited for; matrix products, arithmetic and copies ran while one was open for 0% of the time, Pallas kernels for 19%

profile of v3, /device:TPU:17, one launch (start us, length us, event | category | flops | bytes accessed | tf_op | source)
XLA Modules:
  0.0 57.9 jit_solution(12500529789300502445)
XLA Ops:
  0.7 1.9 %divide_bitcast_fusion = (f32[256,512]{1,0:T(8,128)S(1)}, f32[256,512]{1,0:T(8,128)S(1)}) fusion(f32[1,1,4,256,512]{4,3,2,1,0:T(8,128)} %param.4, s32[]{:T(128)S(6)} %select_n.18, f32[1,1,4,256,512]{4,3,2,1,0:T(8,128)} %param.3, s32[]{:T(128)S(6)} %select_n.17), kind=kLoop, calls=%fused_computation | loop fusion | flops 524288 | bytes 3145736 | tf_op jit(solution)/shard_map/div | solution.py:348
  2.6 3.7 %collective-permute-start.2 = (f32[128,512]{1,0:T(8,128)S(1)}, f32[128,512]{1,0:T(8,128)S(1)}, u32[]{:S(2)}, u32[]{:S(2)}) collective-permute-start(f32[128,512]{1,0:T(8,128)S(1)} %get-tuple-element.46), channel_id=1, source_target_pairs={{8,16},{16,8},{24,1},{1,24},{9,17},{17,9},{25,2},{2,25},{10,18},{1... | collective-permute-start | bytes 786440 | tf_op jit(solution)/shard_map/ppermute | solution.py:340
  6.3 1.9 %collective-permute-start = (f32[128,512]{1,0:T(8,128)S(1)}, f32[128,512]{1,0:T(8,128)S(1)}, u32[]{:S(2)}, u32[]{:S(2)}) collective-permute-start(f32[128,512]{1,0:T(8,128)S(1)} %get-tuple-element.47), channel_id=1, source_target_pairs={{8,16},{16,8},{24,1},{1,24},{9,17},{17,9},{25,2},{2,25},{10,18},{1... | collective-permute-start | bytes 786440 | tf_op jit(solution)/shard_map/ppermute | solution.py:340
  8.3 0.6 %restrict.1 = (f32[192,256]{1,0:T(8,128)S(1)}, f32[112,256]{1,0:T(8,128)S(1)}, f32[80,256]{1,0:T(8,128)S(1)}) custom-call(s32[1]{0:T(128)} %bitcast.5.place_ref, f32[4,256,512]{2,1,0:T(8,128)S(1)} %bitcast.11, f32[8,32,256]{2,1,0:T(8,128)S(1)} %copy-done.2), custom_call_target="tpu_custom_call" | custom-call | flops 5000000000 | bytes 1000000 | tf_op jit(solution)/shard_map/restrict/pallas_call | solution.py:360
  8.9 2.1 %collective-permute-start.1 = (f32[192,256]{1,0:T(8,128)S(1)}, f32[192,256]{1,0:T(8,128)S(1)}, u32[]{:S(2)}, u32[]{:S(2)}) collective-permute-start(f32[192,256]{1,0:T(8,128)S(1)} %get-tuple-element.27), channel_id=1, source_target_pairs={{0,16},{8,24},{16,0},{24,8},{1,17},{9,25},{17,1},{25,9},{2,18},{10... | collective-permute-start | bytes 589832 | tf_op jit(solution)/shard_map/ppermute | solution.py:374
  11.0 0.4 collective-permute-start.3
  11.5 2.2 %first.1 = (f32[4,256,512]{2,1,0:T(8,128)S(1)}, f32[4,256,512]{2,1,0:T(8,128)S(1)}, f32[256,512]{1,0:T(8,128)S(1)}, f32[256,512]{1,0:T(8,128)S(1)}, f32[2,256,512]{2,1,0:T(8,128)S(1)}) custom-call(s32[1]{0:T(128)} %bitcast.1.flip_ref, f32[4,256,512]{2,1,0:T(8,128)S(1)} %bitcast.12, f32[4,256,512]{2,1,0:T(8,128)S(1)} %bitcast.13), custom_call_target="tpu_custom_call" | custom-call | flops 5000000000 | bytes 1000000 | tf_op jit(solution)/shard_map/first/pallas_call | solution.py:376
  13.7 6.2 %collective-permute-start.5 = (f32[128,512]{1,0:T(8,128)S(1)}, f32[128,512]{1,0:T(8,128)S(1)}, u32[]{:S(2)}, u32[]{:S(2)}) collective-permute-start(f32[128,512]{1,0:T(8,128)S(1)} %meet.7.refs_1_), channel_id=1, source_target_pairs={{8,16},{16,8},{24,1},{1,24},{9,17},{17,9},{25,2},{2,25},{10,18},{1... | collective-permute-start | bytes 786440 | tf_op jit(solution)/shard_map/ppermute | solution.py:340
  19.9 5.1 %collective-permute-done.1.arrived.across = f32[192,256]{1,0:T(8,128)S(1)} collective-permute-done((f32[192,256]{1,0:T(8,128)S(1)}, f32[192,256]{1,0:T(8,128)S(1)}, u32[]{:S(2)}, u32[]{:S(2)}) %collective-permute-start.1) | collective-permute-done | bytes 196640 | tf_op jit(solution)/shard_map/ppermute | solution.py:374
  25.2 4.2 %collective-permute-start.4 = (f32[128,512]{1,0:T(8,128)S(1)}, f32[128,512]{1,0:T(8,128)S(1)}, u32[]{:S(2)}, u32[]{:S(2)}) collective-permute-start(f32[128,512]{1,0:T(8,128)S(1)} %meet.6.refs_0_), channel_id=1, source_target_pairs={{8,16},{16,8},{24,1},{1,24},{9,17},{17,9},{25,2},{2,25},{10,18},{1... | collective-permute-start | bytes 786440 | tf_op jit(solution)/shard_map/ppermute | solution.py:340
  29.5 2.3 %collective-permute-start.11 = (f32[2,3,40,256]{3,2,1,0:T(8,128)S(1)}, f32[2,3,40,256]{3,2,1,0:T(8,128)S(1)}, u32[]{:S(2)}, u32[]{:S(2)}) collective-permute-start(f32[2,3,40,256]{3,2,1,0:T(8,128)S(1)} %get-tuple-element.42), channel_id=1, source_target_pairs={{0,1},{1,2},{2,3},{3,4},{4,5},{5,6},{6,7},{8,9},{9,10},{10,11},{11... | collective-permute-start | bytes 737288 | tf_op jit(solution)/shard_map/ppermute | solution.py:432
  31.8 3.9 %collective-permute-start.12 = (f32[2,3,40,256]{3,2,1,0:T(8,128)S(1)}, f32[2,3,40,256]{3,2,1,0:T(8,128)S(1)}, u32[]{:S(2)}, u32[]{:S(2)}) collective-permute-start(f32[2,3,40,256]{3,2,1,0:T(8,128)S(1)} %get-tuple-element.43), channel_id=1, source_target_pairs={{1,0},{2,1},{3,2},{4,3},{5,4},{6,5},{7,6},{9,8},{10,9},{11,10},{12... | collective-permute-start | bytes 737288 | tf_op jit(solution)/shard_map/ppermute | solution.py:433
  35.8 0.3 collective-permute-start.6
  36.1 1.9 %middle.1 = (f32[256,512]{1,0:T(8,128)S(1)}, f32[256,512]{1,0:T(8,128)S(1)}, f32[2,256,512]{2,1,0:T(8,128)S(1)}) custom-call(f32[128,512]{1,0:T(8,128)S(1)} %meet.6.refs_0_, f32[128,512]{1,0:T(8,128)S(1)} %meet.7.refs_1_, f32[256,512]{1,0:T(8,128)S(1)} %meet.8.refs_2_, f32[2,256,512]{2,1,0:T(8,128)S(1)} %get-tuple-element.30.refs_3_, ...), custom_call_target="tpu_custom_call" | custom-call | flops 5000000000 | bytes 1000000 | tf_op jit(solution)/shard_map/middle/pallas_call | solution.py:435
  38.0 3.6 %collective-permute-start.8 = (f32[128,512]{1,0:T(8,128)S(1)}, f32[128,512]{1,0:T(8,128)S(1)}, u32[]{:S(2)}, u32[]{:S(2)}) collective-permute-start(f32[128,512]{1,0:T(8,128)S(1)} %meet.9.refs_0_), channel_id=1, source_target_pairs={{8,16},{16,8},{24,1},{1,24},{9,17},{17,9},{25,2},{2,25},{10,18},{1... | collective-permute-start | bytes 786440 | tf_op jit(solution)/shard_map/ppermute | solution.py:340
  41.7 2.0 %collective-permute-start.7 = (f32[128,512]{1,0:T(8,128)S(1)}, f32[128,512]{1,0:T(8,128)S(1)}, u32[]{:S(2)}, u32[]{:S(2)}) collective-permute-start(f32[128,512]{1,0:T(8,128)S(1)} %meet.10.refs_1_), channel_id=1, source_target_pairs={{8,16},{16,8},{24,1},{1,24},{9,17},{17,9},{25,2},{2,25},{10,18},{1... | collective-permute-start | bytes 786440 | tf_op jit(solution)/shard_map/ppermute | solution.py:340
  43.8 2.2 %collective-permute-start.9 = (f32[256,512]{1,0:T(8,128)S(1)}, f32[256,512]{1,0:T(8,128)S(1)}, u32[]{:S(2)}, u32[]{:S(2)}) collective-permute-start(f32[256,512]{1,0:T(8,128)S(1)} %meet.11.refs_2_), channel_id=1, source_target_pairs={{0,8},{8,0},{16,24},{24,16},{1,9},{9,1},{17,25},{25,17},{2,10},{10... | collective-permute-start | bytes 1572872 | tf_op jit(solution)/shard_map/ppermute | solution.py:343
  46.0 0.7 %collective-permute-done.11.below = f32[2,3,40,256]{3,2,1,0:T(8,128)S(1)} collective-permute-done((f32[2,3,40,256]{3,2,1,0:T(8,128)S(1)}, f32[2,3,40,256]{3,2,1,0:T(8,128)S(1)}, u32[]{:S(2)}, u32[]{:S(2)}) %collective-permute-start.11) | collective-permute-done | bytes 245792 | tf_op jit(solution)/shard_map/ppermute | solution.py:432
  46.7 4.4 %collective-permute-done.12.above = f32[2,3,40,256]{3,2,1,0:T(8,128)S(1)} collective-permute-done((f32[2,3,40,256]{3,2,1,0:T(8,128)S(1)}, f32[2,3,40,256]{3,2,1,0:T(8,128)S(1)}, u32[]{:S(2)}, u32[]{:S(2)}) %collective-permute-start.12) | collective-permute-done | bytes 245792 | tf_op jit(solution)/shard_map/ppermute | solution.py:433
  51.1 1.6 %coarse.1 = f32[8,32,256]{2,1,0:T(8,128)} custom-call(f32[2,8,40,256]{3,2,1,0:T(8,128)S(1)} %get-tuple-element.41.own, f32[2,3,40,256]{3,2,1,0:T(8,128)S(1)} %collective-permute-done.11.below, f32[2,3,40,256]{3,2,1,0:T(8,128)S(1)} %collective-permute-done.12.above), custom_call_target="tpu_custom_call" | custom-call | flops 5000000000 | bytes 1000000 | tf_op jit(solution)/shard_map/coarse/pallas_call | solution.py:466
  52.7 2.9 %last.1 = (f32[256,512]{1,0:T(8,128)S(1)}, f32[256,512]{1,0:T(8,128)S(1)}, f32[4,256,512]{2,1,0:T(8,128)}) custom-call(s32[1]{0:T(128)} %bitcast.1.flip_ref, f32[128,512]{1,0:T(8,128)S(1)} %meet.9.refs_0_, f32[128,512]{1,0:T(8,128)S(1)} %meet.10.refs_1_, f32[256,512]{1,0:T(8,128)S(1)} %meet.11.refs_2_, f32[2,256,512]{2,1,0:T(8,128)S(1)} %get-tuple-element.34.refs_3_, ...), custom_call_target="tpu_custom_call" | custom-call | flops 5000000000 | bytes 1000000 | tf_op jit(solution)/shard_map/last/pallas_call | solution.py:450
  55.6 0.9 %face.3.old = f32[4,256,512]{2,1,0:T(8,128)} custom-call(s32[1]{0:T(128)} %bitcast.7.layer_ref, f32[256,512]{1,0:T(8,128)S(1)} %get-tuple-element.36.part, f32[4,256,512]{2,1,0:T(8,128)S(1)} %get-tuple-element.25.r.refs_5_, f32[256,512]{1,0:T(8,128)S(1)} %collective-permute-done.9.halo, ...), custom_call_target="tpu_custom_call", output_to_operand_aliasing={{}: (4, {})} | custom-call | flops 5000000000 | bytes 1000000 | tf_op jit(solution)/shard_map/face/pallas_call | solution.py:478
  56.4 0.7 %face.4.old = f32[4,256,512]{2,1,0:T(8,128)} custom-call(s32[1]{0:T(128)} %bitcast.layer_ref, f32[256,512]{1,0:T(8,128)S(1)} %get-tuple-element.35.part, f32[4,256,512]{2,1,0:T(8,128)S(1)} %get-tuple-element.25.r.refs_5_, f32[128,512]{1,0:T(8,128)S(1)} %collective-permute-done.8.halo, f32[4,256,512]{2,1,0:T(8,128)} %face.3.old), custom_call_target="tpu_custom_call", output_to_operand_aliasing={{}: (4, {})} | custom-call | flops 5000000000 | bytes 1000000 | tf_op jit(solution)/shard_map/face/pallas_call | solution.py:478
  57.2 0.7 %face.5 = f32[4,256,512]{2,1,0:T(8,128)} custom-call(s32[1]{0:T(128)} %bitcast.layer_ref, f32[256,512]{1,0:T(8,128)S(1)} %get-tuple-element.35.part, f32[4,256,512]{2,1,0:T(8,128)S(1)} %get-tuple-element.25.r.refs_5_, f32[128,512]{1,0:T(8,128)S(1)} %collective-permute-done.7.halo, f32[4,256,512]{2,1,0:T(8,128)} %face.4.old), custom_call_target="tpu_custom_call", output_to_operand_aliasing={{}: (4, {})} | custom-call | flops 5000000000 | bytes 1000000 | tf_op jit(solution)/shard_map/face/pallas_call | solution.py:478
  (26 shorter events, 0.7 us)
Async XLA Ops:
  0.7 7.6 %copy-start = (f32[1,1,4,256,512]{4,3,2,1,0:T(8,128)S(1)}, f32[1,1,4,256,512]{4,3,2,1,0:T(8,128)}, u32[]{:S(2)}) copy-start(f32[1,1,4,256,512]{4,3,2,1,0:T(8,128)} %param.3) | copy-start | bytes 6291460
  0.7 7.6 %copy-start.2 = (f32[8,32,256]{2,1,0:T(8,128)S(1)}, f32[8,32,256]{2,1,0:T(8,128)}, u32[]{:S(2)}) copy-start(f32[8,32,256]{2,1,0:T(8,128)} %kappa.3) | copy-start | bytes 786436
  2.6 11.0 %collective-permute-start.2 = (f32[128,512]{1,0:T(8,128)S(1)}, f32[128,512]{1,0:T(8,128)S(1)}, u32[]{:S(2)}, u32[]{:S(2)}) collective-permute-start(f32[128,512]{1,0:T(8,128)S(1)} %get-tuple-element.46), channel_id=1, source_target_pairs={{8,16},{16,8},{24,1},{1,24},{9,17},{17,9},{25,2},{2,25},{10,18},{1... | collective-permute-start | bytes 786440 | tf_op jit(solution)/shard_map/ppermute | solution.py:340
  6.3 18.8 %collective-permute-start = (f32[128,512]{1,0:T(8,128)S(1)}, f32[128,512]{1,0:T(8,128)S(1)}, u32[]{:S(2)}, u32[]{:S(2)}) collective-permute-start(f32[128,512]{1,0:T(8,128)S(1)} %get-tuple-element.47), channel_id=1, source_target_pairs={{8,16},{16,8},{24,1},{1,24},{9,17},{17,9},{25,2},{2,25},{10,18},{1... | collective-permute-start | bytes 786440 | tf_op jit(solution)/shard_map/ppermute | solution.py:340
  8.3 3.2 %copy-start.1 = (f32[1,1,4,256,512]{4,3,2,1,0:T(8,128)S(1)}, f32[1,1,4,256,512]{4,3,2,1,0:T(8,128)}, u32[]{:S(2)}) copy-start(f32[1,1,4,256,512]{4,3,2,1,0:T(8,128)} %param.4) | copy-start | bytes 6291460
  8.9 16.2 %collective-permute-start.1 = (f32[192,256]{1,0:T(8,128)S(1)}, f32[192,256]{1,0:T(8,128)S(1)}, u32[]{:S(2)}, u32[]{:S(2)}) collective-permute-start(f32[192,256]{1,0:T(8,128)S(1)} %get-tuple-element.27), channel_id=1, source_target_pairs={{0,16},{8,24},{16,0},{24,8},{1,17},{9,25},{17,1},{25,9},{2,18},{10... | collective-permute-start | bytes 589832 | tf_op jit(solution)/shard_map/ppermute | solution.py:374
  11.0 24.7 %collective-permute-start.3 = (f32[256,512]{1,0:T(8,128)S(1)}, f32[256,512]{1,0:T(8,128)S(1)}, u32[]{:S(2)}, u32[]{:S(2)}) collective-permute-start(f32[256,512]{1,0:T(8,128)S(1)} %get-tuple-element.44), channel_id=1, source_target_pairs={{0,8},{8,0},{16,24},{24,16},{1,9},{9,1},{17,25},{25,17},{2,10},{10... | collective-permute-start | bytes 1572872 | tf_op jit(solution)/shard_map/ppermute | solution.py:343
  13.7 27.9 %collective-permute-start.5 = (f32[128,512]{1,0:T(8,128)S(1)}, f32[128,512]{1,0:T(8,128)S(1)}, u32[]{:S(2)}, u32[]{:S(2)}) collective-permute-start(f32[128,512]{1,0:T(8,128)S(1)} %meet.7.refs_1_), channel_id=1, source_target_pairs={{8,16},{16,8},{24,1},{1,24},{9,17},{17,9},{25,2},{2,25},{10,18},{1... | collective-permute-start | bytes 786440 | tf_op jit(solution)/shard_map/ppermute | solution.py:340
  25.1 4.3 %collective-permute-start.10 = (f32[224,256]{1,0:T(8,128)S(1)}, f32[224,256]{1,0:T(8,128)S(1)}, u32[]{:S(2)}, u32[]{:S(2)}) collective-permute-start(f32[224,256]{1,0:T(8,128)S(1)} %relay.1), channel_id=1, source_target_pairs={{0,8},{8,0},{16,24},{24,16},{1,9},{9,1},{17,25},{25,17},{2,10},{10... | collective-permute-start | bytes 688136 | tf_op jit(solution)/shard_map/ppermute | solution.py:415
  25.2 12.7 %collective-permute-start.4 = (f32[128,512]{1,0:T(8,128)S(1)}, f32[128,512]{1,0:T(8,128)S(1)}, u32[]{:S(2)}, u32[]{:S(2)}) collective-permute-start(f32[128,512]{1,0:T(8,128)S(1)} %meet.6.refs_0_), channel_id=1, source_target_pairs={{8,16},{16,8},{24,1},{1,24},{9,17},{17,9},{25,2},{2,25},{10,18},{1... | collective-permute-start | bytes 786440 | tf_op jit(solution)/shard_map/ppermute | solution.py:340
  29.5 17.1 %collective-permute-start.11 = (f32[2,3,40,256]{3,2,1,0:T(8,128)S(1)}, f32[2,3,40,256]{3,2,1,0:T(8,128)S(1)}, u32[]{:S(2)}, u32[]{:S(2)}) collective-permute-start(f32[2,3,40,256]{3,2,1,0:T(8,128)S(1)} %get-tuple-element.42), channel_id=1, source_target_pairs={{0,1},{1,2},{2,3},{3,4},{4,5},{5,6},{6,7},{8,9},{9,10},{10,11},{11... | collective-permute-start | bytes 737288 | tf_op jit(solution)/shard_map/ppermute | solution.py:432
  31.8 19.3 %collective-permute-start.12 = (f32[2,3,40,256]{3,2,1,0:T(8,128)S(1)}, f32[2,3,40,256]{3,2,1,0:T(8,128)S(1)}, u32[]{:S(2)}, u32[]{:S(2)}) collective-permute-start(f32[2,3,40,256]{3,2,1,0:T(8,128)S(1)} %get-tuple-element.43), channel_id=1, source_target_pairs={{1,0},{2,1},{3,2},{4,3},{5,4},{6,5},{7,6},{9,8},{10,9},{11,10},{12... | collective-permute-start | bytes 737288 | tf_op jit(solution)/shard_map/ppermute | solution.py:433
  35.8 7.8 %collective-permute-start.6 = (f32[256,512]{1,0:T(8,128)S(1)}, f32[256,512]{1,0:T(8,128)S(1)}, u32[]{:S(2)}, u32[]{:S(2)}) collective-permute-start(f32[256,512]{1,0:T(8,128)S(1)} %meet.8.refs_2_), channel_id=1, source_target_pairs={{0,8},{8,0},{16,24},{24,16},{1,9},{9,1},{17,25},{25,17},{2,10},{10... | collective-permute-start | bytes 1572872 | tf_op jit(solution)/shard_map/ppermute | solution.py:343
  38.0 18.4 %collective-permute-start.8 = (f32[128,512]{1,0:T(8,128)S(1)}, f32[128,512]{1,0:T(8,128)S(1)}, u32[]{:S(2)}, u32[]{:S(2)}) collective-permute-start(f32[128,512]{1,0:T(8,128)S(1)} %meet.9.refs_0_), channel_id=1, source_target_pairs={{8,16},{16,8},{24,1},{1,24},{9,17},{17,9},{25,2},{2,25},{10,18},{1... | collective-permute-start | bytes 786440 | tf_op jit(solution)/shard_map/ppermute | solution.py:340
  41.7 15.5 %collective-permute-start.7 = (f32[128,512]{1,0:T(8,128)S(1)}, f32[128,512]{1,0:T(8,128)S(1)}, u32[]{:S(2)}, u32[]{:S(2)}) collective-permute-start(f32[128,512]{1,0:T(8,128)S(1)} %meet.10.refs_1_), channel_id=1, source_target_pairs={{8,16},{16,8},{24,1},{1,24},{9,17},{17,9},{25,2},{2,25},{10,18},{1... | collective-permute-start | bytes 786440 | tf_op jit(solution)/shard_map/ppermute | solution.py:340
  43.8 11.8 %collective-permute-start.9 = (f32[256,512]{1,0:T(8,128)S(1)}, f32[256,512]{1,0:T(8,128)S(1)}, u32[]{:S(2)}, u32[]{:S(2)}) collective-permute-start(f32[256,512]{1,0:T(8,128)S(1)} %meet.11.refs_2_), channel_id=1, source_target_pairs={{0,8},{8,0},{16,24},{24,16},{1,9},{9,1},{17,25},{25,17},{2,10},{10... | collective-permute-start | bytes 1572872 | tf_op jit(solution)/shard_map/ppermute | solution.py:343

commit v4 on v3

--- a/solution.py
+++ b/solution.py
@@ -12,7 +12,9 @@
 ROWPAD = 4
 STRIP = 32
 FACE_TILES = 2
+LAST_TILES = 4
 PIECES = 2
+FLOPS = {"restrict": 1000000, "first": 300000000, "meet": 1000000000, "relay": 2000000000, "frame": 1000000, "middle": 10000000000, "last": 5000000000, "coarse": 1000000, "face": 5000000000}
 LIMIT = 12 * 1024 * 1024
 
 
@@ -28,19 +30,20 @@
     return pl.BlockSpec(memory_space=pl.ANY)
 
 
-def cost(cells, ops, arrays, transcendentals=0):
-    return pl.CostEstimate(flops=5000000000, bytes_accessed=1000000, transcendentals=0)
-    return pl.CostEstimate(
-        flops=cells * ops, bytes_accessed=4 * cells * arrays, transcendentals=transcendentals
-    )
+def cost(name):
+    return pl.CostEstimate(flops=FLOPS[name], bytes_accessed=1000000, transcendentals=0)
 
 
 def lane_sum(c):
     cols = c.shape[-1]
-    lane = lax.broadcasted_iota(jnp.int32, c.shape, c.ndim - 1)
-    left = jnp.where(lane == 0, 0.0, pltpu.roll(c, 1, axis=c.ndim - 1))
-    right = jnp.where(lane == cols - 1, 0.0, pltpu.roll(c, cols - 1, axis=c.ndim - 1))
-    return left + right
+    left = pltpu.roll(c, 1, axis=1)
+    right = pltpu.roll(c, cols - 1, axis=1)
+    lane = lax.broadcasted_iota(jnp.int32, (c.shape[0], 128), 1)
+    total = left + right
+    first = right[:, :128] + jnp.where(lane == 0, 0.0, left[:, :128])
+    last = left[:, cols - 128 :] + jnp.where(lane == 127, 0.0, right[:, cols - 128 :])
+    inner = [total[:, 128 : cols - 128]] if cols > 256 else []
+    return jnp.concatenate([first, *inner, last], axis=1)
 
 
 def plane_sum(load, start, size, rows):
@@ -49,9 +52,11 @@
     below = load(pl.multiple_of(jnp.minimum(start + size, rows - 8), 8), 8)[0:1]
     above = jnp.where(start > 0, above, 0.0)
     below = jnp.where(start + size < rows, below, 0.0)
-    sub = lax.broadcasted_iota(jnp.int32, c.shape, 0)
-    up = jnp.where(sub == 0, above, pltpu.roll(c, 1, axis=0))
-    down = jnp.where(sub == size - 1, below, pltpu.roll(c, size - 1, axis=0))
+    sub = lax.broadcasted_iota(jnp.int32, (8, c.shape[1]), 0)
+    up = pltpu.roll(c, 1, axis=0)
+    down = pltpu.roll(c, size - 1, axis=0)
+    up = jnp.concatenate([jnp.where(sub == 0, above, up[:8]), up[8:]], axis=0)
+    down = jnp.concatenate([down[: size - 8], jnp.where(sub == 7, below, down[size - 8 :])], axis=0)
     return (up + down) + lane_sum(c)
 
 
@@ -59,13 +64,13 @@
     return lambda start, size: ref[(*lead, pl.ds(start, size), slice(None))]
 
 
-def strips(rows, body):
-    @pl.loop(0, rows // STRIP)
+def strips(first, last, body):
+    @pl.loop(first // STRIP, last // STRIP)
     def _(k):
         body(pl.multiple_of(k * STRIP, STRIP))
 
 
-def advance(field, b, r, rows, face_off, face_on, mid):
+def advance(field, b, r, rows, face_off, face_on, mid, first=0, last=None):
     depth = len(field)
 
     def body(i):
@@ -84,7 +89,7 @@
             else:
                 mid(m - 1, rows_of, value)
 
-    strips(rows, body)
+    strips(first, rows if last is None else last, body)
 
 
 def first_kernel(flip_ref, noise, kappa, b, r, part_off, part_on, mid):
@@ -99,7 +104,7 @@
             r[m, at, :] = inverse
             b[m, at, :] = noise[src, at, :] * inverse
 
-    strips(rows, prepare)
+    strips(0, rows, prepare)
     field = [loader(b, m) for m in range(depth)]
 
     def put(m, at, value):
@@ -147,13 +152,17 @@
     def put(m, at, value):
         mid[m, at, :] = jnp.exp(value)
 
-    advance(field, b, r, rows, part_off, part_on, put)
     copies = []
-    for m in range(1, depth - 1):
-        dst = m + flip * (depth - 1 - 2 * m)
-        copies.append(pltpu.make_async_copy(mid.at[m - 1], out.at[dst], sems.at[m - 1]))
-    for copy in copies:
-        copy.start()
+    tile = rows // LAST_TILES
+    for k in range(LAST_TILES):
+        at = pl.ds(k * tile, tile)
+        advance(field, b, r, rows, part_off, part_on, put, k * tile, (k + 1) * tile)
+        for m in range(1, depth - 1):
+            dst = m + flip * (depth - 1 - 2 * m)
+            copies.append(
+                pltpu.make_async_copy(mid.at[m - 1, at], out.at[dst, at], sems.at[m - 1, k])
+            )
+            copies[-1].start()
     for copy in copies:
         copy.wait()
 
@@ -257,10 +266,22 @@
         bottom = jnp.where(even, direct, passed)
         middle = 1.0 / (1.5 + kappa[layer])
         own[1, layer] = jnp.concatenate([top, middle, bottom], axis=0)
-    for k in range(HALO):
-        for half in range(2):
-            down[half, k] = own[half, k]
-            up[half, k] = own[half, layers - HALO + k]
+    for out, layer_at in ((down, lambda d: d - 1), (up, lambda d: layers - d)):
+        base = 0
+        for distance in range(1, HALO + 1):
+            layer = layer_at(distance)
+            trim = ROWPAD - HALO + distance
+            at = slice(trim, span - trim)
+            noise, inverse = own[0, layer, at, :], own[1, layer, at, :]
+            values = (noise, inverse) if distance < HALO else (noise * inverse,)
+            for value in values:
+                out[base : base + span - 2 * trim, :] = value
+                base += span - 2 * trim
+
+
+def rim_rows(span):
+    kept = [span - 2 * (ROWPAD - HALO + distance) for distance in range(1, HALO + 1)]
+    return 2 * sum(kept[:-1]) + kept[-1]
 
 
 def coarse_kernel(own, below, above, out, b, r, even, odd):
@@ -273,9 +294,26 @@
         r[dst] = 0.25 * inverse
         b[dst] = ref[0, src] * inverse
 
-    for k in range(HALO):
-        prepare(k, below, k)
-        prepare(HALO + layers + k, above, k)
+    for ref, layer_at in (
+        (below, lambda d: HALO - d),
+        (above, lambda d: HALO + layers - 1 + d),
+    ):
+        base = 0
+        for distance in range(1, HALO + 1):
+            layer = layer_at(distance)
+            trim = ROWPAD - HALO + distance
+            size = span - 2 * trim
+            at = slice(trim, span - trim)
+            b[layer] = jnp.zeros((span, cols), jnp.float32)
+            r[layer] = jnp.zeros((span, cols), jnp.float32)
+            value = ref[base : base + size, :]
+            base += size
+            if distance < HALO:
+                inverse = ref[base : base + size, :]
+                base += size
+                value = value * inverse
+                r[layer, at, :] = 0.25 * inverse
+            b[layer, at, :] = value
 
     for k in range(layers):
         prepare(HALO + k, own, k)
@@ -369,7 +407,7 @@
             pltpu.VMEM((rows // 2 + 2 * ROWPAD, half_cols), jnp.float32),
         ],
         compiler_params=params,
-        cost_estimate=cost(cells * depth, 8, 1),
+        cost_estimate=cost("restrict"),
     )(restrict_place, noise, coarse_kappa)
     across = lax.ppermute(far_send, "grp", [(g, g ^ 2) for g in range(groups)])
 
@@ -380,7 +418,7 @@
         in_specs=[scalar(), whole(), whole()],
         out_specs=(whole(),) * 5,
         compiler_params=params,
-        cost_estimate=cost(cells * depth, 16, 5),
+        cost_estimate=cost("first"),
     )(flip1, noise, kappa)
 
     def meet(layer, start, part, halo):
@@ -391,7 +429,7 @@
             in_specs=[whole()] * 3,
             out_specs=whole(),
             compiler_params=params,
-            cost_estimate=cost(halo.size, 2, 4),
+            cost_estimate=cost("meet"),
         )(part, halo, r)
 
     def meet_off(part, halos):
@@ -410,10 +448,10 @@
         in_specs=[whole()] * 2,
         out_specs=whole(),
         compiler_params=params,
-        cost_estimate=cost(part * half_cols, 1, 4),
+        cost_estimate=cost("relay"),
     )(near_send, across)
     near_got = lax.ppermute(relayed, "grp", [(g, g ^ 1) for g in range(groups)])
-    rim = jax.ShapeDtypeStruct((2, HALO, span, half_cols), jnp.float32)
+    rim = jax.ShapeDtypeStruct((rim_rows(span), half_cols), jnp.float32)
     own, up, down = pl.pallas_call(
         frame_kernel,
         name="frame",
@@ -425,7 +463,7 @@
         in_specs=[scalar()] + [whole()] * 4,
         out_specs=(whole(),) * 3,
         compiler_params=params,
-        cost_estimate=cost(layers * span * half_cols, 4, 5),
+        cost_estimate=cost("frame"),
     )(place, kept, across, near_got, coarse_kappa)
     ahead = [(i, i + 1) for i in range(slabs - 1)]
     back = [(i + 1, i) for i in range(slabs - 1)]
@@ -440,7 +478,7 @@
         out_specs=(whole(),) * 3,
         scratch_shapes=[pltpu.VMEM((rows, cols), jnp.float32)],
         compiler_params=params,
-        cost_estimate=cost(cells * depth, 12, 4),
+        cost_estimate=cost("middle"),
     )(*off, on, mid, b, r)
 
     off = meet_off(part_off, halo_off)
@@ -455,11 +493,11 @@
         out_specs=(whole(), whole(), anywhere()),
         scratch_shapes=[
             pltpu.VMEM((depth - 2, rows, cols), jnp.float32),
-            pltpu.SemaphoreType.DMA((depth - 2,)),
+            pltpu.SemaphoreType.DMA((depth - 2, LAST_TILES)),
             pltpu.VMEM((rows, cols), jnp.float32),
         ],
         compiler_params=params,
-        cost_estimate=cost(cells * depth, 14, 4, cells * 2),
+        cost_estimate=cost("last"),
     )(flip1, *off, on, mid, b, r)
 
     framed = (layers + 2 * HALO, span, half_cols)
@@ -471,7 +509,7 @@
         out_specs=whole(),
         scratch_shapes=[pltpu.VMEM(framed, jnp.float32)] * 4,
         compiler_params=params,
-        cost_estimate=cost(layers * own_rows * half_cols, 80, 6),
+        cost_estimate=cost("coarse"),
     )(own, below, above)
 
     def finish(fine, layer, source, start, part, halo):
@@ -487,7 +525,7 @@
             ],
             input_output_aliases={4: 0},
             compiler_params=params,
-            cost_estimate=cost(halo.size, 3, 4, halo.size),
+            cost_estimate=cost("face"),
         )(layer[None], part, r, halo, fine)
 
     fine = finish(fine, index_on, depth - 1, 0, part_on, halo_on)

time: 58.3 us -> 54 us (0.926)
  the two profiles are of different devices: /device:TPU:17 before, /device:TPU:13 now
where the time goes in v4:
time: 54 us; the launch traced here: 53.7 us
  starting transfers between devices  29 us (54%)
  Pallas kernels  11.6 us (21%)
  waiting for transfers between devices  10.2 us (19%)
  other arithmetic  1.9 us (4%)
  between operations  0.89 us (2%)
    ppermute x6, starting transfers between devices, send_far(): return lax.ppermute(piece, axes, far)  15 us
    ppermute x6, waiting for transfers between devices, send_far(): return lax.ppermute(piece, axes, far)  9.44 us
    ppermute x3, starting transfers between devices, send_near(): return lax.ppermute(layer, axes, near)  5.1 us
    ppermute x1, starting transfers between devices, body(): below = lax.ppermute(up, 'slab', ahead)  3.19 us
    pallas_call x1, Pallas kernels, body(): pl.pallas_call(last_kernel, name='last', out_shape=(plane, plane, stack),...  2.64 us
    pallas_call x3, Pallas kernels, finish(): pl.pallas_call(functools.partial(face_kernel, source, start), name='face'...  2.34 us
    ppermute x1, starting transfers between devices, body(): near_got = lax.ppermute(relayed, 'grp', [(g, g ^ 1) for g in range(groups)])  2.31 us
    pallas_call x1, Pallas kernels, body(): pl.pallas_call(first_kernel, name='first', out_shape=(stack, stack, plane...  2.12 us
  transfers between devices with their start and end apart: 13, of which 6 were waited for; matrix products, arithmetic and copies ran while one was open for 0% of the time, Pallas kernels for 20%

profile of v4, /device:TPU:13, one launch (start us, length us, event | category | flops | bytes accessed | tf_op | source)
XLA Modules:
  0.0 53.7 jit_solution(4294071458530630267)
XLA Ops:
  0.7 1.9 %divide_bitcast_fusion = (f32[256,512]{1,0:T(8,128)S(1)}, f32[256,512]{1,0:T(8,128)S(1)}) fusion(f32[1,1,4,256,512]{4,3,2,1,0:T(8,128)} %param.4, s32[]{:T(128)S(6)} %select_n.18, f32[1,1,4,256,512]{4,3,2,1,0:T(8,128)} %param.3, s32[]{:T(128)S(6)} %select_n.17), kind=kLoop, calls=%fused_computation | loop fusion | flops 524288 | bytes 3145736 | tf_op jit(solution)/shard_map/div | solution.py:386
  2.6 3.8 %collective-permute-start.2 = (f32[128,512]{1,0:T(8,128)S(1)}, f32[128,512]{1,0:T(8,128)S(1)}, u32[]{:S(2)}, u32[]{:S(2)}) collective-permute-start(f32[128,512]{1,0:T(8,128)S(1)} %get-tuple-element.46), channel_id=1, source_target_pairs={{8,16},{16,8},{24,1},{1,24},{9,17},{17,9},{25,2},{2,25},{10,18},{1... | collective-permute-start | bytes 786440 | tf_op jit(solution)/shard_map/ppermute | solution.py:378
  7.1 1.3 %collective-permute-start.1 = (f32[192,256]{1,0:T(8,128)S(1)}, f32[192,256]{1,0:T(8,128)S(1)}, u32[]{:S(2)}, u32[]{:S(2)}) collective-permute-start(f32[192,256]{1,0:T(8,128)S(1)} %get-tuple-element.27), channel_id=1, source_target_pairs={{0,16},{8,24},{16,0},{24,8},{1,17},{9,25},{17,1},{25,9},{2,18},{10... | collective-permute-start | bytes 589832 | tf_op jit(solution)/shard_map/ppermute | solution.py:412
  8.4 2.1 %collective-permute-start = (f32[128,512]{1,0:T(8,128)S(1)}, f32[128,512]{1,0:T(8,128)S(1)}, u32[]{:S(2)}, u32[]{:S(2)}) collective-permute-start(f32[128,512]{1,0:T(8,128)S(1)} %get-tuple-element.47), channel_id=1, source_target_pairs={{8,16},{16,8},{24,1},{1,24},{9,17},{17,9},{25,2},{2,25},{10,18},{1... | collective-permute-start | bytes 786440 | tf_op jit(solution)/shard_map/ppermute | solution.py:378
  10.9 2.1 %first.1 = (f32[4,256,512]{2,1,0:T(8,128)S(1)}, f32[4,256,512]{2,1,0:T(8,128)S(1)}, f32[256,512]{1,0:T(8,128)S(1)}, f32[256,512]{1,0:T(8,128)S(1)}, f32[2,256,512]{2,1,0:T(8,128)S(1)}) custom-call(s32[1]{0:T(128)} %bitcast.1.flip_ref, f32[4,256,512]{2,1,0:T(8,128)S(1)} %bitcast.12, f32[4,256,512]{2,1,0:T(8,128)S(1)} %bitcast.13), custom_call_target="tpu_custom_call" | custom-call | flops 300000000 | bytes 1000000 | tf_op jit(solution)/shard_map/first/pallas_call | solution.py:414
  13.1 4.9 %collective-permute-done.2.halo = f32[128,512]{1,0:T(8,128)S(1)} collective-permute-done((f32[128,512]{1,0:T(8,128)S(1)}, f32[128,512]{1,0:T(8,128)S(1)}, u32[]{:S(2)}, u32[]{:S(2)}) %collective-permute-start.2) | collective-permute-done | bytes 262176 | tf_op jit(solution)/shard_map/ppermute | solution.py:378
  18.0 0.8 %collective-permute-done.1.arrived.across = f32[192,256]{1,0:T(8,128)S(1)} collective-permute-done((f32[192,256]{1,0:T(8,128)S(1)}, f32[192,256]{1,0:T(8,128)S(1)}, u32[]{:S(2)}, u32[]{:S(2)}) %collective-permute-start.1) | collective-permute-done | bytes 196640 | tf_op jit(solution)/shard_map/ppermute | solution.py:412
  18.8 2.3 %collective-permute-start.10 = (f32[224,256]{1,0:T(8,128)S(1)}, f32[224,256]{1,0:T(8,128)S(1)}, u32[]{:S(2)}, u32[]{:S(2)}) collective-permute-start(f32[224,256]{1,0:T(8,128)S(1)} %relay.1), channel_id=1, source_target_pairs={{0,8},{8,0},{16,24},{24,16},{1,9},{9,1},{17,25},{25,17},{2,10},{10... | collective-permute-start | bytes 688136 | tf_op jit(solution)/shard_map/ppermute | solution.py:453
  21.1 1.9 %collective-permute-start.5 = (f32[128,512]{1,0:T(8,128)S(1)}, f32[128,512]{1,0:T(8,128)S(1)}, u32[]{:S(2)}, u32[]{:S(2)}) collective-permute-start(f32[128,512]{1,0:T(8,128)S(1)} %meet.7.refs_1_), channel_id=1, source_target_pairs={{8,16},{16,8},{24,1},{1,24},{9,17},{17,9},{25,2},{2,25},{10,18},{1... | collective-permute-start | bytes 786440 | tf_op jit(solution)/shard_map/ppermute | solution.py:378
  23.4 3.4 %collective-permute-start.4 = (f32[128,512]{1,0:T(8,128)S(1)}, f32[128,512]{1,0:T(8,128)S(1)}, u32[]{:S(2)}, u32[]{:S(2)}) collective-permute-start(f32[128,512]{1,0:T(8,128)S(1)} %meet.6.refs_0_), channel_id=1, source_target_pairs={{8,16},{16,8},{24,1},{1,24},{9,17},{17,9},{25,2},{2,25},{10,18},{1... | collective-permute-start | bytes 786440 | tf_op jit(solution)/shard_map/ppermute | solution.py:378
  26.9 3.2 %collective-permute-start.11 = (f32[172,256]{1,0:T(8,128)S(1)}, f32[172,256]{1,0:T(8,128)S(1)}, u32[]{:S(2)}, u32[]{:S(2)}) collective-permute-start(f32[172,256]{1,0:T(8,128)S(1)} %get-tuple-element.42), channel_id=1, source_target_pairs={{0,1},{1,2},{2,3},{3,4},{4,5},{5,6},{6,7},{8,9},{9,10},{10,11},{11... | collective-permute-start | bytes 528392 | tf_op jit(solution)/shard_map/ppermute | solution.py:470
  30.1 2.1 %collective-permute-start.12 = (f32[172,256]{1,0:T(8,128)S(1)}, f32[172,256]{1,0:T(8,128)S(1)}, u32[]{:S(2)}, u32[]{:S(2)}) collective-permute-start(f32[172,256]{1,0:T(8,128)S(1)} %get-tuple-element.43), channel_id=1, source_target_pairs={{1,0},{2,1},{3,2},{4,3},{5,4},{6,5},{7,6},{9,8},{10,9},{11,10},{12... | collective-permute-start | bytes 528392 | tf_op jit(solution)/shard_map/ppermute | solution.py:471
  32.3 1.5 %collective-permute-start.6 = (f32[256,512]{1,0:T(8,128)S(1)}, f32[256,512]{1,0:T(8,128)S(1)}, u32[]{:S(2)}, u32[]{:S(2)}) collective-permute-start(f32[256,512]{1,0:T(8,128)S(1)} %meet.8.refs_2_), channel_id=1, source_target_pairs={{0,8},{8,0},{16,24},{24,16},{1,9},{9,1},{17,25},{25,17},{2,10},{10... | collective-permute-start | bytes 1572872 | tf_op jit(solution)/shard_map/ppermute | solution.py:381
  33.8 1.8 %middle.1 = (f32[256,512]{1,0:T(8,128)S(1)}, f32[256,512]{1,0:T(8,128)S(1)}, f32[2,256,512]{2,1,0:T(8,128)S(1)}) custom-call(f32[128,512]{1,0:T(8,128)S(1)} %meet.6.refs_0_, f32[128,512]{1,0:T(8,128)S(1)} %meet.7.refs_1_, f32[256,512]{1,0:T(8,128)S(1)} %meet.8.refs_2_, f32[2,256,512]{2,1,0:T(8,128)S(1)} %get-tuple-element.30.refs_3_, ...), custom_call_target="tpu_custom_call" | custom-call | flops 10000000000 | bytes 1000000 | tf_op jit(solution)/shard_map/middle/pallas_call | solution.py:473
  35.7 1.1 %collective-permute-done.4.halo = f32[128,512]{1,0:T(8,128)S(1)} collective-permute-done((f32[128,512]{1,0:T(8,128)S(1)}, f32[128,512]{1,0:T(8,128)S(1)}, u32[]{:S(2)}, u32[]{:S(2)}) %collective-permute-start.4) | collective-permute-done | bytes 262176 | tf_op jit(solution)/shard_map/ppermute | solution.py:378
  36.8 1.9 %collective-permute-start.8 = (f32[128,512]{1,0:T(8,128)S(1)}, f32[128,512]{1,0:T(8,128)S(1)}, u32[]{:S(2)}, u32[]{:S(2)}) collective-permute-start(f32[128,512]{1,0:T(8,128)S(1)} %meet.9.refs_0_), channel_id=1, source_target_pairs={{8,16},{16,8},{24,1},{1,24},{9,17},{17,9},{25,2},{2,25},{10,18},{1... | collective-permute-start | bytes 786440 | tf_op jit(solution)/shard_map/ppermute | solution.py:378
  38.8 3.1 %collective-permute-start.9 = (f32[256,512]{1,0:T(8,128)S(1)}, f32[256,512]{1,0:T(8,128)S(1)}, u32[]{:S(2)}, u32[]{:S(2)}) collective-permute-start(f32[256,512]{1,0:T(8,128)S(1)} %meet.11.refs_2_), channel_id=1, source_target_pairs={{0,8},{8,0},{16,24},{24,16},{1,9},{9,1},{17,25},{25,17},{2,10},{10... | collective-permute-start | bytes 1572872 | tf_op jit(solution)/shard_map/ppermute | solution.py:381
  42.0 1.9 %collective-permute-start.7 = (f32[128,512]{1,0:T(8,128)S(1)}, f32[128,512]{1,0:T(8,128)S(1)}, u32[]{:S(2)}, u32[]{:S(2)}) collective-permute-start(f32[128,512]{1,0:T(8,128)S(1)} %meet.10.refs_1_), channel_id=1, source_target_pairs={{8,16},{16,8},{24,1},{1,24},{9,17},{17,9},{25,2},{2,25},{10,18},{1... | collective-permute-start | bytes 786440 | tf_op jit(solution)/shard_map/ppermute | solution.py:378
  44.0 1.6 %coarse.1 = f32[8,32,256]{2,1,0:T(8,128)} custom-call(f32[2,8,40,256]{3,2,1,0:T(8,128)S(1)} %get-tuple-element.41.own, f32[172,256]{1,0:T(8,128)S(1)} %collective-permute-done.11.below, f32[172,256]{1,0:T(8,128)S(1)} %collective-permute-done.12.above), custom_call_target="tpu_custom_call" | custom-call | flops 1000000 | bytes 1000000 | tf_op jit(solution)/shard_map/coarse/pallas_call | solution.py:504
  45.5 2.6 %last.1 = (f32[256,512]{1,0:T(8,128)S(1)}, f32[256,512]{1,0:T(8,128)S(1)}, f32[4,256,512]{2,1,0:T(8,128)}) custom-call(s32[1]{0:T(128)} %bitcast.1.flip_ref, f32[128,512]{1,0:T(8,128)S(1)} %meet.9.refs_0_, f32[128,512]{1,0:T(8,128)S(1)} %meet.10.refs_1_, f32[256,512]{1,0:T(8,128)S(1)} %meet.11.refs_2_, f32[2,256,512]{2,1,0:T(8,128)S(1)} %get-tuple-element.34.refs_3_, ...), custom_call_target="tpu_custom_call" | custom-call | flops 5000000000 | bytes 1000000 | tf_op jit(solution)/shard_map/last/pallas_call | solution.py:488
  48.2 0.9 %face.3.old = f32[4,256,512]{2,1,0:T(8,128)} custom-call(s32[1]{0:T(128)} %bitcast.7.layer_ref, f32[256,512]{1,0:T(8,128)S(1)} %get-tuple-element.36.part, f32[4,256,512]{2,1,0:T(8,128)S(1)} %get-tuple-element.25.r.refs_5_, f32[256,512]{1,0:T(8,128)S(1)} %collective-permute-done.9.halo, ...), custom_call_target="tpu_custom_call", output_to_operand_aliasing={{}: (4, {})} | custom-call | flops 5000000000 | bytes 1000000 | tf_op jit(solution)/shard_map/face/pallas_call | solution.py:516
  49.1 1.3 %collective-permute-done.8.halo = f32[128,512]{1,0:T(8,128)S(1)} collective-permute-done((f32[128,512]{1,0:T(8,128)S(1)}, f32[128,512]{1,0:T(8,128)S(1)}, u32[]{:S(2)}, u32[]{:S(2)}) %collective-permute-start.8) | collective-permute-done | bytes 262176 | tf_op jit(solution)/shard_map/ppermute | solution.py:378
  50.4 0.7 %face.4.old = f32[4,256,512]{2,1,0:T(8,128)} custom-call(s32[1]{0:T(128)} %bitcast.layer_ref, f32[256,512]{1,0:T(8,128)S(1)} %get-tuple-element.35.part, f32[4,256,512]{2,1,0:T(8,128)S(1)} %get-tuple-element.25.r.refs_5_, f32[128,512]{1,0:T(8,128)S(1)} %collective-permute-done.8.halo, f32[4,256,512]{2,1,0:T(8,128)} %face.3.old), custom_call_target="tpu_custom_call", output_to_operand_aliasing={{}: (4, {})} | custom-call | flops 5000000000 | bytes 1000000 | tf_op jit(solution)/shard_map/face/pallas_call | solution.py:516
  51.1 1.8 %collective-permute-done.7.halo = f32[128,512]{1,0:T(8,128)S(1)} collective-permute-done((f32[128,512]{1,0:T(8,128)S(1)}, f32[128,512]{1,0:T(8,128)S(1)}, u32[]{:S(2)}, u32[]{:S(2)}) %collective-permute-start.7) | collective-permute-done | bytes 262176 | tf_op jit(solution)/shard_map/ppermute | solution.py:378
  (26 shorter events, 2.8 us)
Async XLA Ops:
  0.7 5.8 %copy-start = (f32[1,1,4,256,512]{4,3,2,1,0:T(8,128)S(1)}, f32[1,1,4,256,512]{4,3,2,1,0:T(8,128)}, u32[]{:S(2)}) copy-start(f32[1,1,4,256,512]{4,3,2,1,0:T(8,128)} %param.3) | copy-start | bytes 6291460
  0.7 5.8 %copy-start.2 = (f32[8,32,256]{2,1,0:T(8,128)S(1)}, f32[8,32,256]{2,1,0:T(8,128)}, u32[]{:S(2)}) copy-start(f32[8,32,256]{2,1,0:T(8,128)} %kappa.3) | copy-start | bytes 786436
  2.6 8.4 %copy-start.1 = (f32[1,1,4,256,512]{4,3,2,1,0:T(8,128)S(1)}, f32[1,1,4,256,512]{4,3,2,1,0:T(8,128)}, u32[]{:S(2)}) copy-start(f32[1,1,4,256,512]{4,3,2,1,0:T(8,128)} %param.4) | copy-start | bytes 6291460
  2.6 15.3 %collective-permute-start.2 = (f32[128,512]{1,0:T(8,128)S(1)}, f32[128,512]{1,0:T(8,128)S(1)}, u32[]{:S(2)}, u32[]{:S(2)}) collective-permute-start(f32[128,512]{1,0:T(8,128)S(1)} %get-tuple-element.46), channel_id=1, source_target_pairs={{8,16},{16,8},{24,1},{1,24},{9,17},{17,9},{25,2},{2,25},{10,18},{1... | collective-permute-start | bytes 786440 | tf_op jit(solution)/shard_map/ppermute | solution.py:378
  7.1 11.7 %collective-permute-start.1 = (f32[192,256]{1,0:T(8,128)S(1)}, f32[192,256]{1,0:T(8,128)S(1)}, u32[]{:S(2)}, u32[]{:S(2)}) collective-permute-start(f32[192,256]{1,0:T(8,128)S(1)} %get-tuple-element.27), channel_id=1, source_target_pairs={{0,16},{8,24},{16,0},{24,8},{1,17},{9,25},{17,1},{25,9},{2,18},{10... | collective-permute-start | bytes 589832 | tf_op jit(solution)/shard_map/ppermute | solution.py:412
  8.4 15.0 %collective-permute-start = (f32[128,512]{1,0:T(8,128)S(1)}, f32[128,512]{1,0:T(8,128)S(1)}, u32[]{:S(2)}, u32[]{:S(2)}) collective-permute-start(f32[128,512]{1,0:T(8,128)S(1)} %get-tuple-element.47), channel_id=1, source_target_pairs={{8,16},{16,8},{24,1},{1,24},{9,17},{17,9},{25,2},{2,25},{10,18},{1... | collective-permute-start | bytes 786440 | tf_op jit(solution)/shard_map/ppermute | solution.py:378
  10.5 21.7 %collective-permute-start.3 = (f32[256,512]{1,0:T(8,128)S(1)}, f32[256,512]{1,0:T(8,128)S(1)}, u32[]{:S(2)}, u32[]{:S(2)}) collective-permute-start(f32[256,512]{1,0:T(8,128)S(1)} %get-tuple-element.44), channel_id=1, source_target_pairs={{0,8},{8,0},{16,24},{24,16},{1,9},{9,1},{17,25},{25,17},{2,10},{10... | collective-permute-start | bytes 1572872 | tf_op jit(solution)/shard_map/ppermute | solution.py:381
  18.8 8.0 %collective-permute-start.10 = (f32[224,256]{1,0:T(8,128)S(1)}, f32[224,256]{1,0:T(8,128)S(1)}, u32[]{:S(2)}, u32[]{:S(2)}) collective-permute-start(f32[224,256]{1,0:T(8,128)S(1)} %relay.1), channel_id=1, source_target_pairs={{0,8},{8,0},{16,24},{24,16},{1,9},{9,1},{17,25},{25,17},{2,10},{10... | collective-permute-start | bytes 688136 | tf_op jit(solution)/shard_map/ppermute | solution.py:453
  21.1 20.9 %collective-permute-start.5 = (f32[128,512]{1,0:T(8,128)S(1)}, f32[128,512]{1,0:T(8,128)S(1)}, u32[]{:S(2)}, u32[]{:S(2)}) collective-permute-start(f32[128,512]{1,0:T(8,128)S(1)} %meet.7.refs_1_), channel_id=1, source_target_pairs={{8,16},{16,8},{24,1},{1,24},{9,17},{17,9},{25,2},{2,25},{10,18},{1... | collective-permute-start | bytes 786440 | tf_op jit(solution)/shard_map/ppermute | solution.py:378
  23.4 13.3 %collective-permute-start.4 = (f32[128,512]{1,0:T(8,128)S(1)}, f32[128,512]{1,0:T(8,128)S(1)}, u32[]{:S(2)}, u32[]{:S(2)}) collective-permute-start(f32[128,512]{1,0:T(8,128)S(1)} %meet.6.refs_0_), channel_id=1, source_target_pairs={{8,16},{16,8},{24,1},{1,24},{9,17},{17,9},{25,2},{2,25},{10,18},{1... | collective-permute-start | bytes 786440 | tf_op jit(solution)/shard_map/ppermute | solution.py:378
  26.9 17.0 %collective-permute-start.11 = (f32[172,256]{1,0:T(8,128)S(1)}, f32[172,256]{1,0:T(8,128)S(1)}, u32[]{:S(2)}, u32[]{:S(2)}) collective-permute-start(f32[172,256]{1,0:T(8,128)S(1)} %get-tuple-element.42), channel_id=1, source_target_pairs={{0,1},{1,2},{2,3},{3,4},{4,5},{5,6},{6,7},{8,9},{9,10},{10,11},{11... | collective-permute-start | bytes 528392 | tf_op jit(solution)/shard_map/ppermute | solution.py:470
  30.1 13.8 %collective-permute-start.12 = (f32[172,256]{1,0:T(8,128)S(1)}, f32[172,256]{1,0:T(8,128)S(1)}, u32[]{:S(2)}, u32[]{:S(2)}) collective-permute-start(f32[172,256]{1,0:T(8,128)S(1)} %get-tuple-element.43), channel_id=1, source_target_pairs={{1,0},{2,1},{3,2},{4,3},{5,4},{6,5},{7,6},{9,8},{10,9},{11,10},{12... | collective-permute-start | bytes 528392 | tf_op jit(solution)/shard_map/ppermute | solution.py:471
  32.3 6.4 %collective-permute-start.6 = (f32[256,512]{1,0:T(8,128)S(1)}, f32[256,512]{1,0:T(8,128)S(1)}, u32[]{:S(2)}, u32[]{:S(2)}) collective-permute-start(f32[256,512]{1,0:T(8,128)S(1)} %meet.8.refs_2_), channel_id=1, source_target_pairs={{0,8},{8,0},{16,24},{24,16},{1,9},{9,1},{17,25},{25,17},{2,10},{10... | collective-permute-start | bytes 1572872 | tf_op jit(solution)/shard_map/ppermute | solution.py:381
  36.8 13.6 %collective-permute-start.8 = (f32[128,512]{1,0:T(8,128)S(1)}, f32[128,512]{1,0:T(8,128)S(1)}, u32[]{:S(2)}, u32[]{:S(2)}) collective-permute-start(f32[128,512]{1,0:T(8,128)S(1)} %meet.9.refs_0_), channel_id=1, source_target_pairs={{8,16},{16,8},{24,1},{1,24},{9,17},{17,9},{25,2},{2,25},{10,18},{1... | collective-permute-start | bytes 786440 | tf_op jit(solution)/shard_map/ppermute | solution.py:378
  38.8 9.4 %collective-permute-start.9 = (f32[256,512]{1,0:T(8,128)S(1)}, f32[256,512]{1,0:T(8,128)S(1)}, u32[]{:S(2)}, u32[]{:S(2)}) collective-permute-start(f32[256,512]{1,0:T(8,128)S(1)} %meet.11.refs_2_), channel_id=1, source_target_pairs={{0,8},{8,0},{16,24},{24,16},{1,9},{9,1},{17,25},{25,17},{2,10},{10... | collective-permute-start | bytes 1572872 | tf_op jit(solution)/shard_map/ppermute | solution.py:381
  42.0 10.9 %collective-permute-start.7 = (f32[128,512]{1,0:T(8,128)S(1)}, f32[128,512]{1,0:T(8,128)S(1)}, u32[]{:S(2)}, u32[]{:S(2)}) collective-permute-start(f32[128,512]{1,0:T(8,128)S(1)} %meet.10.refs_1_), channel_id=1, source_target_pairs={{8,16},{16,8},{24,1},{1,24},{9,17},{17,9},{25,2},{2,25},{10,18},{1... | collective-permute-start | bytes 786440 | tf_op jit(solution)/shard_map/ppermute | solution.py:378

commit v5 on v4

--- a/solution.py
+++ b/solution.py
@@ -196,8 +196,8 @@
     padded[...] = jnp.zeros_like(padded)
     flip1 = 1 - 2 * (position % 2)
     other = position + flip1
-    across = jnp.where(position < 2, position + 2, position - 2)
-    beyond = across + flip1
+    across = 3 - position
+    beyond = across - flip1
     for layer in range(depth // 2):
         pair[...] = noise[2 * layer] + noise[2 * layer + 1]
         pieces = []
@@ -236,10 +236,10 @@
     mine = near.shape[0]
     carried = out.shape[0] - mine
     out[0:mine, :] = near[...]
-    out[mine:, :] = arrived[arrived.shape[0] - carried :, :]
-
-
-def frame_kernel(place_ref, kept, across, near, kappa, own, up, down):
+    out[mine:, :] = arrived[carried : 2 * carried, :]
+
+
+def frame_kernel(place_ref, slab_ref, kept, across, near, kappa, own, even_out, odd_out):
     layers, own_rows, _ = kappa.shape
     span = own_rows + 2 * ROWPAD
     per = kept.shape[0] // span
@@ -247,18 +247,18 @@
     edge = layers * ROWPAD
     position = place_ref[0]
     flip1 = 1 - 2 * (position % 2)
-    beyond_chip = jnp.where(position < 2, position + 2, position - 2)
+    beyond_chip = 3 - position
     for k in range(per):
         at = slice(k * span, (k + 1) * span)
         own[0, per * position + k] = kept[at, :]
         own[0, per * (position + flip1) + k] = near[at, :]
         own[0, per * beyond_chip + k] = across[at, :]
         relayed = slice(part + edge + k * span, part + edge + (k + 1) * span)
-        own[0, per * (beyond_chip + flip1) + k] = near[relayed, :]
+        own[0, per * (beyond_chip - flip1) + k] = near[relayed, :]
     for layer in range(layers):
         at = layer * ROWPAD
         direct = near[part + at : part + at + ROWPAD, :]
-        passed = near[2 * part + edge + at : 2 * part + edge + at + ROWPAD, :]
+        passed = across[2 * part + at : 2 * part + at + ROWPAD, :]
         inner = jnp.logical_or(position == 1, position == 2)
         passed = jnp.where(inner, passed, 0.0)
         even = position % 2 == 0
@@ -266,17 +266,20 @@
         bottom = jnp.where(even, direct, passed)
         middle = 1.0 / (1.5 + kappa[layer])
         own[1, layer] = jnp.concatenate([top, middle, bottom], axis=0)
-    for out, layer_at in ((down, lambda d: d - 1), (up, lambda d: layers - d)):
-        base = 0
-        for distance in range(1, HALO + 1):
-            layer = layer_at(distance)
-            trim = ROWPAD - HALO + distance
-            at = slice(trim, span - trim)
+    even_slab = slab_ref[0] % 2 == 0
+    base = 0
+    for distance in range(1, HALO + 1):
+        trim = ROWPAD - HALO + distance
+        at = slice(trim, span - trim)
+        pairs = []
+        for layer in (layers - distance, distance - 1):
             noise, inverse = own[0, layer, at, :], own[1, layer, at, :]
-            values = (noise, inverse) if distance < HALO else (noise * inverse,)
-            for value in values:
-                out[base : base + span - 2 * trim, :] = value
-                base += span - 2 * trim
+            pairs.append((noise, inverse) if distance < HALO else (noise * inverse,))
+        for up, down in zip(*pairs):
+            to = slice(base, base + span - 2 * trim)
+            even_out[to, :] = jnp.where(even_slab, up, down)
+            odd_out[to, :] = jnp.where(even_slab, down, up)
+            base += span - 2 * trim
 
 
 def rim_rows(span):
@@ -284,7 +287,8 @@
     return 2 * sum(kept[:-1]) + kept[-1]
 
 
-def coarse_kernel(own, below, above, out, b, r, even, odd):
+def coarse_kernel(slab_ref, own, even_in, odd_in, out, b, r, even, odd):
+    even_slab = slab_ref[0] % 2 == 0
     layers, own_rows, _ = out.shape
     total_layers, span, cols = b.shape
     total = total_layers
@@ -294,10 +298,12 @@
         r[dst] = 0.25 * inverse
         b[dst] = ref[0, src] * inverse
 
-    for ref, layer_at in (
-        (below, lambda d: HALO - d),
-        (above, lambda d: HALO + layers - 1 + d),
+    for lower, layer_at in (
+        (True, lambda d: HALO - d),
+        (False, lambda d: HALO + layers - 1 + d),
     ):
+        first, second = (odd_in, even_in) if lower else (even_in, odd_in)
+
         base = 0
         for distance in range(1, HALO + 1):
             layer = layer_at(distance)
@@ -306,10 +312,12 @@
             at = slice(trim, span - trim)
             b[layer] = jnp.zeros((span, cols), jnp.float32)
             r[layer] = jnp.zeros((span, cols), jnp.float32)
-            value = ref[base : base + size, :]
+            at_rows = slice(base, base + size)
+            value = jnp.where(even_slab, first[at_rows, :], second[at_rows, :])
             base += size
             if distance < HALO:
-                inverse = ref[base : base + size, :]
+                at_rows = slice(base, base + size)
+                inverse = jnp.where(even_slab, first[at_rows, :], second[at_rows, :])
                 base += size
                 value = value * inverse
                 r[layer, at, :] = 0.25 * inverse
@@ -366,6 +374,7 @@
     flip = (position % 2).astype(jnp.int32)
     flip1 = flip[None]
     place = position.astype(jnp.int32)[None]
+    slab_place = lax.axis_index("slab").astype(jnp.int32)[None]
     params = pltpu.CompilerParams(vmem_limit_bytes=LIMIT)
     cells = rows * cols
     plane = jax.ShapeDtypeStruct((rows, cols), jnp.float32)
@@ -387,6 +396,7 @@
 
     index_off = flip * (depth - 1)
     index_on = (1 - flip) * (depth - 1)
+    index_off, place, slab_place = lax.optimization_barrier((index_off, place, slab_place))
     off, restrict_place = lax.optimization_barrier((face(index_off), place))
     halo_off = [send_far(off[k * piece_rows : (k + 1) * piece_rows]) for k in range(PIECES)]
     halo_on = send_near(face(index_on))
@@ -409,7 +419,7 @@
         compiler_params=params,
         cost_estimate=cost("restrict"),
     )(restrict_place, noise, coarse_kappa)
-    across = lax.ppermute(far_send, "grp", [(g, g ^ 2) for g in range(groups)])
+    across = lax.ppermute(far_send, "grp", [(g, g ^ 3) for g in range(groups)])
 
     b, r, part_off, part_on, mid = pl.pallas_call(
         first_kernel,
@@ -439,12 +449,12 @@
     on = meet(depth - 1, 0, part_on, halo_on)
     halo_off = [send_far(piece) for piece in off]
     halo_on = send_near(on)
-    across, off[-1] = lax.optimization_barrier((across, off[-1]))
+    across, off[0] = lax.optimization_barrier((across, off[0]))
 
     relayed = pl.pallas_call(
         relay_kernel,
         name="relay",
-        out_shape=jax.ShapeDtypeStruct((2 * part + 2 * edge, half_cols), jnp.float32),
+        out_shape=jax.ShapeDtypeStruct((2 * part + edge, half_cols), jnp.float32),
         in_specs=[whole()] * 2,
         out_specs=whole(),
         compiler_params=params,
@@ -452,7 +462,7 @@
     )(near_send, across)
     near_got = lax.ppermute(relayed, "grp", [(g, g ^ 1) for g in range(groups)])
     rim = jax.ShapeDtypeStruct((rim_rows(span), half_cols), jnp.float32)
-    own, up, down = pl.pallas_call(
+    own, even_send, odd_send = pl.pallas_call(
         frame_kernel,
         name="frame",
         out_shape=(
@@ -460,15 +470,16 @@
             rim,
             rim,
         ),
-        in_specs=[scalar()] + [whole()] * 4,
+        in_specs=[scalar(), scalar()] + [whole()] * 4,
         out_specs=(whole(),) * 3,
         compiler_params=params,
         cost_estimate=cost("frame"),
-    )(place, kept, across, near_got, coarse_kappa)
-    ahead = [(i, i + 1) for i in range(slabs - 1)]
-    back = [(i + 1, i) for i in range(slabs - 1)]
-    below = lax.ppermute(up, "slab", ahead)
-    above = lax.ppermute(down, "slab", back)
+    )(place, slab_place, kept, across, near_got, coarse_kappa)
+    even_pairs, odd_pairs = [], []
+    for k in range(slabs - 1):
+        (odd_pairs if k % 2 else even_pairs).extend([(k, k + 1), (k + 1, k)])
+    even_got = lax.ppermute(even_send, "slab", even_pairs)
+    odd_got = lax.ppermute(odd_send, "slab", odd_pairs)
 
     part_off, part_on, mid = pl.pallas_call(
         middle_kernel,
@@ -505,12 +516,12 @@
         coarse_kernel,
         name="coarse",
         out_shape=jax.ShapeDtypeStruct(coarse_kappa.shape, jnp.float32),
-        in_specs=[whole()] * 3,
+        in_specs=[scalar()] + [whole()] * 3,
         out_specs=whole(),
         scratch_shapes=[pltpu.VMEM(framed, jnp.float32)] * 4,
         compiler_params=params,
         cost_estimate=cost("coarse"),
-    )(own, below, above)
+    )(slab_place, own, even_got, odd_got)
 
     def finish(fine, layer, source, start, part, halo):
         return pl.pallas_call(

time: 54 us -> 51.5 us (0.954)
  starting transfers between devices: 29 us -> 24.5 us
  waiting for transfers between devices: 10.2 us -> 12 us
    ppermute x1, starting transfers between devices: 2.31 us -> 0.07 us  [body(): near_got = lax.ppermute(relayed, 'grp', [(g, g ^ 1) for g in range(groups)])]
    ppermute x3, starting transfers between devices: 6.56 us -> 4.52 us  [the longest x1 4.11 us: body(): odd_got = lax.ppermute(odd_send, 'slab', odd_pairs)]
    ppermute x3, starting transfers between devices: 5.1 us -> 3.25 us  [send_near(): return lax.ppermute(layer, axes, near)]
    ppermute x6, starting transfers between devices: 15 us -> 16.7 us  [send_far(): return lax.ppermute(piece, axes, far)]
    ppermute x3, waiting for transfers between devices: 0.76 us -> 2.4 us  [the longest x1 2.31 us: body(): across = lax.ppermute(far_send, 'grp', [(g, g ^ 3) for g in range(groups)])]
  transfers between devices with their start and end apart: 13 -> 13, of which waited for: 6 -> 6; matrix products, arithmetic and copies ran while one was open for 0% -> 0% of each run, Pallas kernels for 20% -> 22%
where the time goes in v5:
time: 51.5 us; the launch traced here: 51.2 us
  starting transfers between devices  24.5 us (48%)
  waiting for transfers between devices  12 us (23%)
  Pallas kernels  11.8 us (23%)
  other arithmetic  1.9 us (4%)
  between operations  0.89 us (2%)
    ppermute x6, starting transfers between devices, send_far(): return lax.ppermute(piece, axes, far)  16.7 us
    ppermute x6, waiting for transfers between devices, send_far(): return lax.ppermute(piece, axes, far)  9.64 us
    ppermute x1, starting transfers between devices, body(): odd_got = lax.ppermute(odd_send, 'slab', odd_pairs)  4.11 us
    ppermute x3, starting transfers between devices, send_near(): return lax.ppermute(layer, axes, near)  3.25 us
    pallas_call x1, Pallas kernels, body(): pl.pallas_call(last_kernel, name='last', out_shape=(plane, plane, stack),...  2.64 us
    pallas_call x3, Pallas kernels, finish(): pl.pallas_call(functools.partial(face_kernel, source, start), name='face'...  2.36 us
    ppermute x1, waiting for transfers between devices, body(): across = lax.ppermute(far_send, 'grp', [(g, g ^ 3) for g in range(groups)])  2.31 us
    pallas_call x1, Pallas kernels, body(): pl.pallas_call(first_kernel, name='first', out_shape=(stack, stack, plane...  2.14 us
  transfers between devices with their start and end apart: 13, of which 6 were waited for; matrix products, arithmetic and copies ran while one was open for 0% of the time, Pallas kernels for 22%

profile of v5, /device:TPU:13, one launch (start us, length us, event | category | flops | bytes accessed | tf_op | source)
XLA Modules:
  0.0 51.2 jit_solution(15885987504692761538)
XLA Ops:
  0.7 1.9 %divide_bitcast_fusion = (f32[256,512]{1,0:T(8,128)S(1)}, f32[256,512]{1,0:T(8,128)S(1)}) fusion(f32[1,1,4,256,512]{4,3,2,1,0:T(8,128)} %param.4, s32[]{:T(128)S(6)} %select_n.18, f32[1,1,4,256,512]{4,3,2,1,0:T(8,128)} %param.3, s32[]{:T(128)S(6)} %select_n.17), kind=kLoop, calls=%fused_computation | loop fusion | flops 524288 | bytes 3145736 | tf_op jit(solution)/shard_map/div | solution.py:395
  2.6 3.8 %collective-permute-start.1 = (f32[128,512]{1,0:T(8,128)S(1)}, f32[128,512]{1,0:T(8,128)S(1)}, u32[]{:S(2)}, u32[]{:S(2)}) collective-permute-start(f32[128,512]{1,0:T(8,128)S(1)} %get-tuple-element.53), channel_id=1, source_target_pairs={{8,16},{16,8},{24,1},{1,24},{9,17},{17,9},{25,2},{2,25},{10,18},{1... | collective-permute-start | bytes 786440 | tf_op jit(solution)/shard_map/ppermute | solution.py:387
  6.5 0.6 %restrict.1 = (f32[192,256]{1,0:T(8,128)S(1)}, f32[112,256]{1,0:T(8,128)S(1)}, f32[80,256]{1,0:T(8,128)S(1)}) custom-call(s32[1]{0:T(128)} %bitcast.place_ref, f32[4,256,512]{2,1,0:T(8,128)S(1)} %bitcast.12, f32[8,32,256]{2,1,0:T(8,128)S(1)} %copy-done.2), custom_call_target="tpu_custom_call" | custom-call | flops 1000000 | bytes 1000000 | tf_op jit(solution)/shard_map/restrict/pallas_call | solution.py:408
  7.2 1.6 %collective-permute-start.3 = (f32[256,512]{1,0:T(8,128)S(1)}, f32[256,512]{1,0:T(8,128)S(1)}, u32[]{:S(2)}, u32[]{:S(2)}) collective-permute-start(f32[256,512]{1,0:T(8,128)S(1)} %get-tuple-element.50), channel_id=1, source_target_pairs={{0,8},{8,0},{16,24},{24,16},{1,9},{9,1},{17,25},{25,17},{2,10},{10... | collective-permute-start | bytes 1572872 | tf_op jit(solution)/shard_map/ppermute | solution.py:390
  8.8 2.0 %collective-permute-start.2 = (f32[128,512]{1,0:T(8,128)S(1)}, f32[128,512]{1,0:T(8,128)S(1)}, u32[]{:S(2)}, u32[]{:S(2)}) collective-permute-start(f32[128,512]{1,0:T(8,128)S(1)} %get-tuple-element.52), channel_id=1, source_target_pairs={{8,16},{16,8},{24,1},{1,24},{9,17},{17,9},{25,2},{2,25},{10,18},{1... | collective-permute-start | bytes 786440 | tf_op jit(solution)/shard_map/ppermute | solution.py:387
  10.8 2.1 %first.1 = (f32[4,256,512]{2,1,0:T(8,128)S(1)}, f32[4,256,512]{2,1,0:T(8,128)S(1)}, f32[256,512]{1,0:T(8,128)S(1)}, f32[256,512]{1,0:T(8,128)S(1)}, f32[2,256,512]{2,1,0:T(8,128)S(1)}) custom-call(s32[1]{0:T(128)} %bitcast.3.flip_ref, f32[4,256,512]{2,1,0:T(8,128)S(1)} %bitcast.13, f32[4,256,512]{2,1,0:T(8,128)S(1)} %bitcast.14), custom_call_target="tpu_custom_call" | custom-call | flops 300000000 | bytes 1000000 | tf_op jit(solution)/shard_map/first/pallas_call | solution.py:424
  13.0 5.3 %collective-permute-done.1.halo = f32[128,512]{1,0:T(8,128)S(1)} collective-permute-done((f32[128,512]{1,0:T(8,128)S(1)}, f32[128,512]{1,0:T(8,128)S(1)}, u32[]{:S(2)}, u32[]{:S(2)}) %collective-permute-start.1) | collective-permute-done | bytes 262176 | tf_op jit(solution)/shard_map/ppermute | solution.py:387
  18.3 2.3 %collective-permute-done.arrived.across = f32[192,256]{1,0:T(8,128)S(1)} collective-permute-done((f32[192,256]{1,0:T(8,128)S(1)}, f32[192,256]{1,0:T(8,128)S(1)}, u32[]{:S(2)}, u32[]{:S(2)}) %collective-permute-start) | collective-permute-done | bytes 196640 | tf_op jit(solution)/shard_map/ppermute | solution.py:422
  20.7 1.9 %collective-permute-start.4 = (f32[128,512]{1,0:T(8,128)S(1)}, f32[128,512]{1,0:T(8,128)S(1)}, u32[]{:S(2)}, u32[]{:S(2)}) collective-permute-start(f32[128,512]{1,0:T(8,128)S(1)} %meet.6.refs_0_), channel_id=1, source_target_pairs={{8,16},{16,8},{24,1},{1,24},{9,17},{17,9},{25,2},{2,25},{10,18},{1... | collective-permute-start | bytes 786440 | tf_op jit(solution)/shard_map/ppermute | solution.py:387
  22.7 0.7 %collective-permute-done.2.halo = f32[128,512]{1,0:T(8,128)S(1)} collective-permute-done((f32[128,512]{1,0:T(8,128)S(1)}, f32[128,512]{1,0:T(8,128)S(1)}, u32[]{:S(2)}, u32[]{:S(2)}) %collective-permute-start.2) | collective-permute-done | bytes 262176 | tf_op jit(solution)/shard_map/ppermute | solution.py:387
  23.4 3.4 %collective-permute-start.5 = (f32[128,512]{1,0:T(8,128)S(1)}, f32[128,512]{1,0:T(8,128)S(1)}, u32[]{:S(2)}, u32[]{:S(2)}) collective-permute-start(f32[128,512]{1,0:T(8,128)S(1)} %meet.7.refs_1_), channel_id=1, source_target_pairs={{8,16},{16,8},{24,1},{1,24},{9,17},{17,9},{25,2},{2,25},{10,18},{1... | collective-permute-start | bytes 786440 | tf_op jit(solution)/shard_map/ppermute | solution.py:387
  26.9 0.3 collective-permute-start.11
  27.3 4.1 %collective-permute-start.12 = (f32[172,256]{1,0:T(8,128)S(1)}, f32[172,256]{1,0:T(8,128)S(1)}, u32[]{:S(2)}, u32[]{:S(2)}) collective-permute-start(f32[172,256]{1,0:T(8,128)S(1)} %get-tuple-element.49), channel_id=1, source_target_pairs={{1,2},{2,1},{3,4},{4,3},{5,6},{6,5},{9,10},{10,9},{11,12},{12,11},... | collective-permute-start | bytes 528392 | tf_op jit(solution)/shard_map/ppermute | solution.py:482
  31.5 1.6 %collective-permute-start.6 = (f32[256,512]{1,0:T(8,128)S(1)}, f32[256,512]{1,0:T(8,128)S(1)}, u32[]{:S(2)}, u32[]{:S(2)}) collective-permute-start(f32[256,512]{1,0:T(8,128)S(1)} %meet.8.refs_2_), channel_id=1, source_target_pairs={{0,8},{8,0},{16,24},{24,16},{1,9},{9,1},{17,25},{25,17},{2,10},{10... | collective-permute-start | bytes 1572872 | tf_op jit(solution)/shard_map/ppermute | solution.py:390
  33.1 1.8 %middle.1 = (f32[256,512]{1,0:T(8,128)S(1)}, f32[256,512]{1,0:T(8,128)S(1)}, f32[2,256,512]{2,1,0:T(8,128)S(1)}) custom-call(f32[128,512]{1,0:T(8,128)S(1)} %meet.6.refs_0_, f32[128,512]{1,0:T(8,128)S(1)} %meet.7.refs_1_, f32[256,512]{1,0:T(8,128)S(1)} %meet.8.refs_2_, f32[2,256,512]{2,1,0:T(8,128)S(1)} %get-tuple-element.35.refs_3_, ...), custom_call_target="tpu_custom_call" | custom-call | flops 10000000000 | bytes 1000000 | tf_op jit(solution)/shard_map/middle/pallas_call | solution.py:484
  35.0 1.9 %collective-permute-start.8 = (f32[128,512]{1,0:T(8,128)S(1)}, f32[128,512]{1,0:T(8,128)S(1)}, u32[]{:S(2)}, u32[]{:S(2)}) collective-permute-start(f32[128,512]{1,0:T(8,128)S(1)} %meet.9.refs_0_), channel_id=1, source_target_pairs={{8,16},{16,8},{24,1},{1,24},{9,17},{17,9},{25,2},{2,25},{10,18},{1... | collective-permute-start | bytes 786440 | tf_op jit(solution)/shard_map/ppermute | solution.py:387
  37.2 3.6 %collective-permute-start.7 = (f32[128,512]{1,0:T(8,128)S(1)}, f32[128,512]{1,0:T(8,128)S(1)}, u32[]{:S(2)}, u32[]{:S(2)}) collective-permute-start(f32[128,512]{1,0:T(8,128)S(1)} %meet.10.refs_1_), channel_id=1, source_target_pairs={{8,16},{16,8},{24,1},{1,24},{9,17},{17,9},{25,2},{2,25},{10,18},{1... | collective-permute-start | bytes 786440 | tf_op jit(solution)/shard_map/ppermute | solution.py:387
  41.0 1.6 %coarse.1 = f32[8,32,256]{2,1,0:T(8,128)} custom-call(s32[1]{0:T(128)} %bitcast.1.slab_ref, f32[2,8,40,256]{3,2,1,0:T(8,128)S(1)} %get-tuple-element.47.own, f32[172,256]{1,0:T(8,128)S(1)} %collective-permute-done.11.even_in, f32[172,256]{1,0:T(8,128)S(1)} %collective-permute-done.12.odd_in), custom_call_target="tpu_custom_call" | custom-call | flops 1000000 | bytes 1000000 | tf_op jit(solution)/shard_map/coarse/pallas_call | solution.py:515
  42.5 2.6 %last.1 = (f32[256,512]{1,0:T(8,128)S(1)}, f32[256,512]{1,0:T(8,128)S(1)}, f32[4,256,512]{2,1,0:T(8,128)}) custom-call(s32[1]{0:T(128)} %bitcast.3.flip_ref, f32[128,512]{1,0:T(8,128)S(1)} %meet.9.refs_0_, f32[128,512]{1,0:T(8,128)S(1)} %meet.10.refs_1_, f32[256,512]{1,0:T(8,128)S(1)} %meet.11.refs_2_, f32[2,256,512]{2,1,0:T(8,128)S(1)} %get-tuple-element.39.refs_3_, ...), custom_call_target="tpu_custom_call" | custom-call | flops 5000000000 | bytes 1000000 | tf_op jit(solution)/shard_map/last/pallas_call | solution.py:499
  45.2 0.9 %face.3.old = f32[4,256,512]{2,1,0:T(8,128)} custom-call(s32[1]{0:T(128)} %bitcast.8.layer_ref, f32[256,512]{1,0:T(8,128)S(1)} %get-tuple-element.41.part, f32[4,256,512]{2,1,0:T(8,128)S(1)} %get-tuple-element.32.r.refs_5_, f32[256,512]{1,0:T(8,128)S(1)} %collective-permute-done.9.halo, ...), custom_call_target="tpu_custom_call", output_to_operand_aliasing={{}: (4, {})} | custom-call | flops 5000000000 | bytes 1000000 | tf_op jit(solution)/shard_map/face/pallas_call | solution.py:527
  46.0 1.9 %collective-permute-done.8.halo = f32[128,512]{1,0:T(8,128)S(1)} collective-permute-done((f32[128,512]{1,0:T(8,128)S(1)}, f32[128,512]{1,0:T(8,128)S(1)}, u32[]{:S(2)}, u32[]{:S(2)}) %collective-permute-start.8) | collective-permute-done | bytes 262176 | tf_op jit(solution)/shard_map/ppermute | solution.py:387
  47.9 0.8 %face.4.old = f32[4,256,512]{2,1,0:T(8,128)} custom-call(s32[1]{0:T(128)} %bitcast.2.layer_ref, f32[256,512]{1,0:T(8,128)S(1)} %get-tuple-element.40.part, f32[4,256,512]{2,1,0:T(8,128)S(1)} %get-tuple-element.32.r.refs_5_, f32[128,512]{1,0:T(8,128)S(1)} %collective-permute-done.8.halo, f32[4,256,512]{2,1,0:T(8,128)} %face.3.old), custom_call_target="tpu_custom_call", output_to_operand_aliasing={{}: (4, {})} | custom-call | flops 5000000000 | bytes 1000000 | tf_op jit(solution)/shard_map/face/pallas_call | solution.py:527
  48.7 1.7 %collective-permute-done.7.halo = f32[128,512]{1,0:T(8,128)S(1)} collective-permute-done((f32[128,512]{1,0:T(8,128)S(1)}, f32[128,512]{1,0:T(8,128)S(1)}, u32[]{:S(2)}, u32[]{:S(2)}) %collective-permute-start.7) | collective-permute-done | bytes 262176 | tf_op jit(solution)/shard_map/ppermute | solution.py:387
  50.4 0.7 %face.5 = f32[4,256,512]{2,1,0:T(8,128)} custom-call(s32[1]{0:T(128)} %bitcast.2.layer_ref, f32[256,512]{1,0:T(8,128)S(1)} %get-tuple-element.40.part, f32[4,256,512]{2,1,0:T(8,128)S(1)} %get-tuple-element.32.r.refs_5_, f32[128,512]{1,0:T(8,128)S(1)} %collective-permute-done.7.halo, f32[4,256,512]{2,1,0:T(8,128)} %face.4.old), custom_call_target="tpu_custom_call", output_to_operand_aliasing={{}: (4, {})} | custom-call | flops 5000000000 | bytes 1000000 | tf_op jit(solution)/shard_map/face/pallas_call | solution.py:527
  (26 shorter events, 1.0 us)
Async XLA Ops:
  0.7 5.8 %copy-start = (f32[1,1,4,256,512]{4,3,2,1,0:T(8,128)S(1)}, f32[1,1,4,256,512]{4,3,2,1,0:T(8,128)}, u32[]{:S(2)}) copy-start(f32[1,1,4,256,512]{4,3,2,1,0:T(8,128)} %param.3) | copy-start | bytes 6291460
  0.7 5.8 %copy-start.2 = (f32[8,32,256]{2,1,0:T(8,128)S(1)}, f32[8,32,256]{2,1,0:T(8,128)}, u32[]{:S(2)}) copy-start(f32[8,32,256]{2,1,0:T(8,128)} %kappa.3) | copy-start | bytes 786436
  2.6 8.2 %copy-start.1 = (f32[1,1,4,256,512]{4,3,2,1,0:T(8,128)S(1)}, f32[1,1,4,256,512]{4,3,2,1,0:T(8,128)}, u32[]{:S(2)}) copy-start(f32[1,1,4,256,512]{4,3,2,1,0:T(8,128)} %param.4) | copy-start | bytes 6291460
  2.6 15.6 %collective-permute-start.1 = (f32[128,512]{1,0:T(8,128)S(1)}, f32[128,512]{1,0:T(8,128)S(1)}, u32[]{:S(2)}, u32[]{:S(2)}) collective-permute-start(f32[128,512]{1,0:T(8,128)S(1)} %get-tuple-element.53), channel_id=1, source_target_pairs={{8,16},{16,8},{24,1},{1,24},{9,17},{17,9},{25,2},{2,25},{10,18},{1... | collective-permute-start | bytes 786440 | tf_op jit(solution)/shard_map/ppermute | solution.py:387
  7.1 13.5 %collective-permute-start = (f32[192,256]{1,0:T(8,128)S(1)}, f32[192,256]{1,0:T(8,128)S(1)}, u32[]{:S(2)}, u32[]{:S(2)}) collective-permute-start(f32[192,256]{1,0:T(8,128)S(1)} %get-tuple-element.29), channel_id=1, source_target_pairs={{0,24},{8,16},{16,8},{24,0},{1,25},{9,17},{17,9},{25,1},{2,26},{10... | collective-permute-start | bytes 589832 | tf_op jit(solution)/shard_map/ppermute | solution.py:422
  7.2 24.2 %collective-permute-start.3 = (f32[256,512]{1,0:T(8,128)S(1)}, f32[256,512]{1,0:T(8,128)S(1)}, u32[]{:S(2)}, u32[]{:S(2)}) collective-permute-start(f32[256,512]{1,0:T(8,128)S(1)} %get-tuple-element.50), channel_id=1, source_target_pairs={{0,8},{8,0},{16,24},{24,16},{1,9},{9,1},{17,25},{25,17},{2,10},{10... | collective-permute-start | bytes 1572872 | tf_op jit(solution)/shard_map/ppermute | solution.py:390
  8.8 14.6 %collective-permute-start.2 = (f32[128,512]{1,0:T(8,128)S(1)}, f32[128,512]{1,0:T(8,128)S(1)}, u32[]{:S(2)}, u32[]{:S(2)}) collective-permute-start(f32[128,512]{1,0:T(8,128)S(1)} %get-tuple-element.52), channel_id=1, source_target_pairs={{8,16},{16,8},{24,1},{1,24},{9,17},{17,9},{25,2},{2,25},{10,18},{1... | collective-permute-start | bytes 786440 | tf_op jit(solution)/shard_map/ppermute | solution.py:387
  20.6 6.2 %collective-permute-start.10 = (f32[192,256]{1,0:T(8,128)S(1)}, f32[192,256]{1,0:T(8,128)S(1)}, u32[]{:S(2)}, u32[]{:S(2)}) collective-permute-start(f32[192,256]{1,0:T(8,128)S(1)} %relay.1), channel_id=1, source_target_pairs={{0,8},{8,0},{16,24},{24,16},{1,9},{9,1},{17,25},{25,17},{2,10},{10... | collective-permute-start | bytes 589832 | tf_op jit(solution)/shard_map/ppermute | solution.py:463
  20.7 14.2 %collective-permute-start.4 = (f32[128,512]{1,0:T(8,128)S(1)}, f32[128,512]{1,0:T(8,128)S(1)}, u32[]{:S(2)}, u32[]{:S(2)}) collective-permute-start(f32[128,512]{1,0:T(8,128)S(1)} %meet.6.refs_0_), channel_id=1, source_target_pairs={{8,16},{16,8},{24,1},{1,24},{9,17},{17,9},{25,2},{2,25},{10,18},{1... | collective-permute-start | bytes 786440 | tf_op jit(solution)/shard_map/ppermute | solution.py:387
  23.4 13.7 %collective-permute-start.5 = (f32[128,512]{1,0:T(8,128)S(1)}, f32[128,512]{1,0:T(8,128)S(1)}, u32[]{:S(2)}, u32[]{:S(2)}) collective-permute-start(f32[128,512]{1,0:T(8,128)S(1)} %meet.7.refs_1_), channel_id=1, source_target_pairs={{8,16},{16,8},{24,1},{1,24},{9,17},{17,9},{25,2},{2,25},{10,18},{1... | collective-permute-start | bytes 786440 | tf_op jit(solution)/shard_map/ppermute | solution.py:387
  26.9 14.0 %collective-permute-start.11 = (f32[172,256]{1,0:T(8,128)S(1)}, f32[172,256]{1,0:T(8,128)S(1)}, u32[]{:S(2)}, u32[]{:S(2)}) collective-permute-start(f32[172,256]{1,0:T(8,128)S(1)} %get-tuple-element.48), channel_id=1, source_target_pairs={{0,1},{1,0},{2,3},{3,2},{4,5},{5,4},{6,7},{7,6},{8,9},{9,8},{10,11... | collective-permute-start | bytes 528392 | tf_op jit(solution)/shard_map/ppermute | solution.py:481
  27.3 13.7 %collective-permute-start.12 = (f32[172,256]{1,0:T(8,128)S(1)}, f32[172,256]{1,0:T(8,128)S(1)}, u32[]{:S(2)}, u32[]{:S(2)}) collective-permute-start(f32[172,256]{1,0:T(8,128)S(1)} %get-tuple-element.49), channel_id=1, source_target_pairs={{1,2},{2,1},{3,4},{4,3},{5,6},{6,5},{9,10},{10,9},{11,12},{12,11},... | collective-permute-start | bytes 528392 | tf_op jit(solution)/shard_map/ppermute | solution.py:482
  31.5 5.4 %collective-permute-start.6 = (f32[256,512]{1,0:T(8,128)S(1)}, f32[256,512]{1,0:T(8,128)S(1)}, u32[]{:S(2)}, u32[]{:S(2)}) collective-permute-start(f32[256,512]{1,0:T(8,128)S(1)} %meet.8.refs_2_), channel_id=1, source_target_pairs={{0,8},{8,0},{16,24},{24,16},{1,9},{9,1},{17,25},{25,17},{2,10},{10... | collective-permute-start | bytes 1572872 | tf_op jit(solution)/shard_map/ppermute | solution.py:390
  35.0 12.9 %collective-permute-start.8 = (f32[128,512]{1,0:T(8,128)S(1)}, f32[128,512]{1,0:T(8,128)S(1)}, u32[]{:S(2)}, u32[]{:S(2)}) collective-permute-start(f32[128,512]{1,0:T(8,128)S(1)} %meet.9.refs_0_), channel_id=1, source_target_pairs={{8,16},{16,8},{24,1},{1,24},{9,17},{17,9},{25,2},{2,25},{10,18},{1... | collective-permute-start | bytes 786440 | tf_op jit(solution)/shard_map/ppermute | solution.py:387
  37.1 8.1 %collective-permute-start.9 = (f32[256,512]{1,0:T(8,128)S(1)}, f32[256,512]{1,0:T(8,128)S(1)}, u32[]{:S(2)}, u32[]{:S(2)}) collective-permute-start(f32[256,512]{1,0:T(8,128)S(1)} %meet.11.refs_2_), channel_id=1, source_target_pairs={{0,8},{8,0},{16,24},{24,16},{1,9},{9,1},{17,25},{25,17},{2,10},{10... | collective-permute-start | bytes 1572872 | tf_op jit(solution)/shard_map/ppermute | solution.py:390
  37.2 13.2 %collective-permute-start.7 = (f32[128,512]{1,0:T(8,128)S(1)}, f32[128,512]{1,0:T(8,128)S(1)}, u32[]{:S(2)}, u32[]{:S(2)}) collective-permute-start(f32[128,512]{1,0:T(8,128)S(1)} %meet.10.refs_1_), channel_id=1, source_target_pairs={{8,16},{16,8},{24,1},{1,24},{9,17},{17,9},{25,2},{2,25},{10,18},{1... | collective-permute-start | bytes 786440 | tf_op jit(solution)/shard_map/ppermute | solution.py:387
